TPU v7x, 32 devices: a whole 2x2x4 slice. The times are simulated.
32 devices in a mesh: grp: 4 (over y, core), seq: 8 (over z, x).
Axes of the slice: x: 2, y: 2, z: 4, core: 2. Of those that a mesh axis runs over, the one named last changes fastest.
Arguments:
- x_prompt: bfloat16 [2048, 768], P(('grp', 'seq')), may hold values from -6 to 6
- x_cont: bfloat16 [64, 256, 768], P(('grp', 'seq')), may hold values from -6 to 6
- thought_pos: int32 [64, 6], P(('grp', 'seq')), may hold values from 0 to 254, all different within a row
- offsets: int32 [64], P(('grp', 'seq')), may hold values from 1 to 512, as said below
- dy_prompt: float32 [2048, 768], P(('grp', 'seq')), may hold values from -6 to 6
- dy_cont: float32 [64, 256, 768], P(('grp', 'seq')), may hold values from -6 to 6
- w_qkv: bfloat16 [2, 768, 2304], P(None, ('grp', 'seq')), may hold values from -0.21875 to 0.21875
- w_out: bfloat16 [2, 768, 768], P(None, ('grp', 'seq')), may hold values from -1.25 to 1.25
- w_fc: bfloat16 [2, 768, 3072], P(None, ('grp', 'seq')), may hold values from -0.21875 to 0.21875
- w_proj: bfloat16 [2, 3072, 768], P(None, ('grp', 'seq')), may hold values from -0.109375 to 0.109375
- ln1_gain: bfloat16 [2, 768], P(None, ('grp', 'seq')), may hold values from 0.5 to 1.5
- ln1_bias: bfloat16 [2, 768], P(None, ('grp', 'seq')), may hold values from -0.59765625 to 0.59765625
- q_bias: bfloat16 [2, 768], P(None, ('grp', 'seq')), may hold values from -0.59765625 to 0.59765625
- v_bias: bfloat16 [2, 768], P(None, ('grp', 'seq')), may hold values from -0.59765625 to 0.59765625
- out_bias: bfloat16 [2, 768], P(None, ('grp', 'seq')), may hold values from -0.59765625 to 0.59765625
- ln2_gain: bfloat16 [2, 768], P(None, ('grp', 'seq')), may hold values from 0.5 to 1.5
- ln2_bias: bfloat16 [2, 768], P(None, ('grp', 'seq')), may hold values from -0.59765625 to 0.59765625
- fc_bias: bfloat16 [2, 3072], P(None, ('grp', 'seq')), may hold values from -0.59765625 to 0.59765625
- proj_bias: bfloat16 [2, 768], P(None, ('grp', 'seq')), may hold values from -0.59765625 to 0.59765625
Outputs:
- y_prompt: bfloat16 [2048, 768], P(('grp', 'seq'))
- y_cont: bfloat16 [64, 256, 768], P(('grp', 'seq'))
- dx_prompt: float32 [2048, 768], P(('grp', 'seq'))
- dx_cont: float32 [64, 256, 768], P(('grp', 'seq'))
- grad_qkv: float32 [2, 768, 2304], P(None, ('grp', 'seq'))
- grad_out: float32 [2, 768, 768], P(None, ('grp', 'seq'))
- grad_fc: float32 [2, 768, 3072], P(None, ('grp', 'seq'))
- grad_proj: float32 [2, 3072, 768], P(None, ('grp', 'seq'))
- grad_ln1_gain: float32 [2, 768], P(None, ('grp', 'seq'))
- grad_ln1_bias: float32 [2, 768], P(None, ('grp', 'seq'))
- grad_q_bias: float32 [2, 768], P(None, ('grp', 'seq'))
- grad_v_bias: float32 [2, 768], P(None, ('grp', 'seq'))
- grad_out_bias: float32 [2, 768], P(None, ('grp', 'seq'))
- grad_ln2_gain: float32 [2, 768], P(None, ('grp', 'seq'))
- grad_ln2_bias: float32 [2, 768], P(None, ('grp', 'seq'))
- grad_fc_bias: float32 [2, 3072], P(None, ('grp', 'seq'))
- grad_proj_bias: float32 [2, 768], P(None, ('grp', 'seq'))
Inputs may be any that keep to these rules, and one draw needn't show every extreme that they name: `thought_pos`: each row names 6 different source positions; the thought of source s sits at position s + 1 of the same continuation. `offsets`: in every group some continuation sees all 512 prompt tokens.
All inputs are finite; a program needn't handle non-finite values.
Results may differ from a plain program's by a relative error of at most 0.018.
Values may be sent and summed in bfloat16 or wider, within the bound.
No kernel may reach another device: no remote copies, remote signals or barrier semaphores. Data moves between devices by JAX's collectives and lax.ppermute only.
A program may use at most 512 MiB of HBM per device.

v0:
```python
from functools import reduce

import jax
import jax.numpy as jnp
from jax import lax
from jax.sharding import PartitionSpec as P

HEADS = 12
LAYERS = 2
MB = 2


epsilon = 1e-05
score_scale = 0.125
gelu_coeff = 0.7978845608028654
masked_score = -1e30


def layer_norm(rows, gain, shift):
    centred = rows - jnp.mean(rows, -1, keepdims=True)
    spread = jnp.mean(centred * centred, -1, keepdims=True)
    return centred * lax.rsqrt(spread + epsilon) * gain + shift


def gelu_tanh(value):
    return 0.5 * value * (1.0 + jnp.tanh(gelu_coeff * (value + 0.044715 * value * value * value)))


def product(left, right):
    return jnp.dot(left, right, preferred_element_type=jnp.float32)


def product_nt(left, right):
    return lax.dot_general(
        left, right, (((1,), (1,)), ((), ())), preferred_element_type=jnp.float32
    )


def product_tn(left, right):
    return lax.dot_general(
        left, right, (((0,), (0,)), ((), ())), preferred_element_type=jnp.float32
    )


def head_cols(block, head, width):
    return lax.dynamic_slice_in_dim(block, head * width, width, 1)


def as_float(vector):
    return vector.astype(jnp.float32)


def column_sums(block):
    return jnp.sum(block.astype(jnp.float32), 0)


def fetch_forward(parts):
    return (
        lax.all_gather(parts[0], ("grp", "seq"), axis=1, tiled=True),
        lax.all_gather(parts[1], ("grp", "seq"), axis=1, tiled=True),
        lax.all_gather(parts[2], ("grp", "seq"), axis=1, tiled=True),
        lax.all_gather(parts[3], ("grp", "seq"), axis=1, tiled=True),
        lax.all_gather(parts[4], ("grp", "seq"), axis=1, tiled=True),
        lax.all_gather(parts[5], ("grp", "seq"), axis=1, tiled=True),
        lax.all_gather(parts[6], ("grp", "seq"), axis=1, tiled=True),
        lax.all_gather(parts[7], ("grp", "seq"), axis=1, tiled=True),
        lax.all_gather(parts[8], ("grp", "seq"), axis=1, tiled=True),
        lax.all_gather(parts[9], ("grp", "seq"), axis=1, tiled=True),
        lax.all_gather(parts[10], ("grp", "seq"), axis=1, tiled=True),
        lax.all_gather(parts[11], ("grp", "seq"), axis=1, tiled=True),
        lax.all_gather(parts[12], ("grp", "seq"), axis=1, tiled=True),
    )


def fetch_backward(parts):
    return (
        lax.all_gather(parts[0], ("grp", "seq"), axis=1, tiled=True),
        lax.all_gather(parts[1], ("grp", "seq"), axis=1, tiled=True),
        lax.all_gather(parts[2], ("grp", "seq"), axis=1, tiled=True),
        lax.all_gather(parts[3], ("grp", "seq"), axis=1, tiled=True),
        lax.all_gather(parts[4], ("grp", "seq"), axis=1, tiled=True),
        lax.all_gather(parts[5], ("grp", "seq"), axis=1, tiled=True),
        lax.all_gather(parts[6], ("grp", "seq"), axis=1, tiled=True),
        lax.all_gather(parts[7], ("grp", "seq"), axis=1, tiled=True),
        lax.all_gather(parts[8], ("grp", "seq"), axis=1, tiled=True),
        lax.all_gather(parts[9], ("grp", "seq"), axis=1, tiled=True),
        lax.all_gather(parts[10], ("grp", "seq"), axis=1, tiled=True),
        lax.all_gather(parts[11], ("grp", "seq"), axis=1, tiled=True),
        lax.all_gather(parts[12], ("grp", "seq"), axis=1, tiled=True),
    )


def reduce_all(parts):
    return (
        lax.psum_scatter(parts[0], ("grp", "seq"), scatter_dimension=0, tiled=True),
        lax.psum_scatter(parts[1], ("grp", "seq"), scatter_dimension=0, tiled=True),
        lax.psum_scatter(parts[2], ("grp", "seq"), scatter_dimension=0, tiled=True),
        lax.psum_scatter(parts[3], ("grp", "seq"), scatter_dimension=0, tiled=True),
        lax.psum_scatter(parts[4], ("grp", "seq"), scatter_dimension=0, tiled=True),
        lax.psum_scatter(parts[5], ("grp", "seq"), scatter_dimension=0, tiled=True),
        lax.psum_scatter(parts[6], ("grp", "seq"), scatter_dimension=0, tiled=True),
        lax.psum_scatter(parts[7], ("grp", "seq"), scatter_dimension=0, tiled=True),
        lax.psum_scatter(parts[8], ("grp", "seq"), scatter_dimension=0, tiled=True),
        lax.psum_scatter(parts[9], ("grp", "seq"), scatter_dimension=0, tiled=True),
        lax.psum_scatter(parts[10], ("grp", "seq"), scatter_dimension=0, tiled=True),
        lax.psum_scatter(parts[11], ("grp", "seq"), scatter_dimension=0, tiled=True),
        lax.psum_scatter(parts[12], ("grp", "seq"), scatter_dimension=0, tiled=True),
    )


def attention_inputs(weights, rows):
    width = rows.shape[1]
    normed = layer_norm(rows, as_float(weights[4]), as_float(weights[5])).astype(jnp.bfloat16)
    mixed = product(normed, weights[0])
    queries = (mixed[:, :width] + as_float(weights[6])).astype(jnp.bfloat16)
    keys = mixed[:, width : 2 * width].astype(jnp.bfloat16)
    values = (mixed[:, 2 * width :] + as_float(weights[7])).astype(jnp.bfloat16)
    return (normed, queries, keys, values)


def attend_forward(queries, key_list, value_list, mask_list, heads):
    width = queries.shape[1] // heads
    rows = queries.shape[0]

    def one_head(head):
        query_head = head_cols(queries, head, width)
        scores = [
            jnp.where(
                mask,
                product_nt(query_head, head_cols(keys, head, width)) * score_scale,
                masked_score,
            )
            for keys, mask in zip(key_list, mask_list)
        ]
        top = reduce(jnp.maximum, [jnp.max(block, 1) for block in scores])
        expd = [jnp.exp(block - top[:, None]) for block in scores]
        total = reduce(jnp.add, [jnp.sum(block, 1) for block in expd])
        mixed = reduce(
            jnp.add,
            [
                product(
                    (block / total[:, None]).astype(jnp.bfloat16), head_cols(values, head, width)
                )
                for block, values in zip(expd, value_list)
            ],
        )
        return (mixed, top + jnp.log(total))

    outputs, log_total = lax.map(one_head, jnp.arange(heads, dtype=jnp.int32))
    joined = jnp.transpose(outputs, (1, 0, 2)).reshape(rows, heads * width)
    return (joined.astype(jnp.bfloat16), log_total)


def attend_backward(queries, key_list, value_list, mask_list, log_total, grad_out, heads):
    width = queries.shape[1] // heads
    rows = queries.shape[0]

    def one_head(pair):
        head, head_total = pair
        query_head = head_cols(queries, head, width)
        grad_head = head_cols(grad_out, head, width)
        probs = [
            jnp.exp(
                jnp.where(
                    mask,
                    product_nt(query_head, head_cols(keys, head, width)) * score_scale,
                    masked_score,
                )
                - head_total[:, None]
            )
            for keys, mask in zip(key_list, mask_list)
        ]
        grads_p = [product_nt(grad_head, head_cols(values, head, width)) for values in value_list]
        delta = reduce(jnp.add, [jnp.sum(prob * grad, 1) for prob, grad in zip(probs, grads_p)])
        grads_s = [
            (prob * (grad - delta[:, None])).astype(jnp.bfloat16)
            for prob, grad in zip(probs, grads_p)
        ]
        grad_query = (
            reduce(
                jnp.add,
                [
                    product(block, head_cols(keys, head, width))
                    for block, keys in zip(grads_s, key_list)
                ],
            )
            * score_scale
        )
        grad_keys = [product_tn(block, query_head) * score_scale for block in grads_s]
        grad_values = [product_tn(prob.astype(jnp.bfloat16), grad_head) for prob in probs]
        return (grad_query, grad_keys, grad_values)

    grad_query, grad_keys, grad_values = lax.map(
        one_head, (jnp.arange(heads, dtype=jnp.int32), log_total)
    )
    grad_query = jnp.transpose(grad_query, (1, 0, 2)).reshape(rows, heads * width)
    return (grad_query, grad_keys, grad_values)


def block_output(weights, rows, mixed):
    after = rows + product(mixed, weights[1]) + as_float(weights[8])
    normed = layer_norm(after, as_float(weights[9]), as_float(weights[10])).astype(jnp.bfloat16)
    hidden = product(normed, weights[2]) + as_float(weights[11])
    active = gelu_tanh(hidden).astype(jnp.bfloat16)
    result = after + product(active, weights[3]) + as_float(weights[12])
    return (result, (after, normed, hidden, active))


def output_backward(weights, mixed, kept, grad_rows):
    after, normed, hidden, active = kept
    grad_branch = grad_rows.astype(jnp.bfloat16)
    g_proj_bias = column_sums(grad_branch)
    g_proj = product_tn(active, grad_branch)
    grad_active = product_nt(grad_branch, weights[3])
    unused, gelu_back = jax.vjp(gelu_tanh, hidden)
    grad_hidden = gelu_back(grad_active)[0].astype(jnp.bfloat16)
    g_fc_bias = column_sums(grad_hidden)
    g_fc = product_tn(normed, grad_hidden)
    grad_normed = product_nt(grad_hidden, weights[2])
    unused, norm_back = jax.vjp(layer_norm, after, as_float(weights[9]), as_float(weights[10]))
    grad_after, g_ln2_gain, g_ln2_bias = norm_back(grad_normed)
    grad_after = grad_after + grad_rows
    grad_attn = grad_after.astype(jnp.bfloat16)
    g_out_bias = column_sums(grad_attn)
    g_out = product_tn(mixed, grad_attn)
    grad_mixed = product_nt(grad_attn, weights[1]).astype(jnp.bfloat16)
    return (
        grad_after,
        grad_mixed,
        (g_out, g_fc, g_proj, g_out_bias, g_ln2_gain, g_ln2_bias, g_fc_bias, g_proj_bias),
    )


def input_backward(weights, rows, normed, grad_query, grad_key, grad_value):
    rounded = (
        grad_query.astype(jnp.bfloat16),
        grad_key.astype(jnp.bfloat16),
        grad_value.astype(jnp.bfloat16),
    )
    g_q_bias = column_sums(rounded[0])
    g_v_bias = column_sums(rounded[2])
    joined = jnp.concatenate(rounded, 1)
    g_qkv = product_tn(normed, joined)
    grad_normed = product_nt(joined, weights[0])
    unused, norm_back = jax.vjp(layer_norm, rows, as_float(weights[4]), as_float(weights[5]))
    grad_in, g_ln1_gain, g_ln1_bias = norm_back(grad_normed)
    return (grad_in, (g_qkv, g_ln1_gain, g_ln1_bias, g_q_bias, g_v_bias))


def combine_grads(totals, front, back):
    fresh = (
        front[0],
        back[0],
        back[1],
        back[2],
        front[1],
        front[2],
        front[3],
        front[4],
        back[3],
        back[4],
        back[5],
        back[6],
        back[7],
    )
    return tuple((old + new for old, new in zip(totals, fresh)))


def cont_masks(length):
    return lax.broadcasted_iota(jnp.int32, (length, length), 0) >= lax.broadcasted_iota(
        jnp.int32, (length, length), 1
    )


def cont_forward(weights, rows, prompt_keys, prompt_values, seen, length):
    count = seen.shape[0]
    plen = prompt_keys.shape[0]
    normed, queries, keys, values = attention_inputs(weights, rows)
    causal = cont_masks(length)

    def one_cont(args):
        query_c, key_c, value_c, offset = args
        visible = lax.broadcasted_iota(jnp.int32, (1, plen), 1) < offset
        return attend_forward(
            query_c, [prompt_keys, key_c], [prompt_values, value_c], [visible, causal], HEADS
        )

    def shaped(block):
        return block.reshape(count, length, block.shape[1])

    mixed, log_total = lax.map(one_cont, (shaped(queries), shaped(keys), shaped(values), seen))
    mixed = mixed.reshape(count * length, rows.shape[1])
    result, kept = block_output(weights, rows, mixed)
    return (result, (rows, normed, queries, keys, values, mixed, log_total, kept))


def cont_backward(weights, state, prompt_keys, prompt_values, seen, length, grad_rows):
    rows, normed, queries, keys, values, mixed, log_total, kept = state
    count = seen.shape[0]
    plen = prompt_keys.shape[0]
    width = rows.shape[1]
    causal = cont_masks(length)
    grad_after, grad_mixed, back = output_backward(weights, mixed, kept, grad_rows)

    def one_cont(args):
        query_c, key_c, value_c, offset, total_c, grad_c = args
        visible = lax.broadcasted_iota(jnp.int32, (1, plen), 1) < offset
        return attend_backward(
            query_c,
            [prompt_keys, key_c],
            [prompt_values, value_c],
            [visible, causal],
            total_c,
            grad_c,
            HEADS,
        )

    def shaped(block):
        return block.reshape(count, length, block.shape[1])

    grad_query, grad_keys, grad_values = lax.map(
        one_cont,
        (shaped(queries), shaped(keys), shaped(values), seen, log_total, shaped(grad_mixed)),
    )
    prompt_key_part = jnp.sum(grad_keys[0], 0)
    prompt_value_part = jnp.sum(grad_values[0], 0)
    own_keys = jnp.transpose(grad_keys[1], (0, 2, 1, 3)).reshape(count * length, width)
    own_values = jnp.transpose(grad_values[1], (0, 2, 1, 3)).reshape(count * length, width)
    grad_in, front = input_backward(
        weights, rows, normed, grad_query.reshape(count * length, width), own_keys, own_values
    )
    return (grad_after + grad_in, front, back, prompt_key_part, prompt_value_part)


def body(
    x_prompt,
    x_cont,
    thought_pos,
    offsets,
    dy_prompt,
    dy_cont,
    w_qkv,
    w_out,
    w_fc,
    w_proj,
    ln1_gain,
    ln1_bias,
    q_bias,
    v_bias,
    out_bias,
    ln2_gain,
    ln2_bias,
    fc_bias,
    proj_bias,
):
    sharded = (
        w_qkv,
        w_out,
        w_fc,
        w_proj,
        ln1_gain,
        ln1_bias,
        q_bias,
        v_bias,
        out_bias,
        ln2_gain,
        ln2_bias,
        fc_bias,
        proj_bias,
    )
    width = x_prompt.shape[1]
    length = x_cont.shape[1]
    per_batch = x_cont.shape[0] // MB
    prompt_dev = x_prompt.shape[0]
    plen = prompt_dev * lax.axis_size("seq")
    head_width = width // HEADS
    base = lax.axis_index("seq") * prompt_dev
    prompt_visible = lax.broadcasted_iota(
        jnp.int32, (prompt_dev, plen), 1
    ) <= base + lax.broadcasted_iota(jnp.int32, (prompt_dev, plen), 0)
    key_totals = [jnp.zeros((HEADS, plen, head_width), jnp.float32) for layer in range(LAYERS)]
    value_totals = [jnp.zeros((HEADS, plen, head_width), jnp.float32) for layer in range(LAYERS)]
    outputs_cont = []
    grads_cont = []
    for batch in range(MB):
        forward_weights = fetch_forward(sharded)
        forward_sets = [tuple((part[layer] for part in forward_weights)) for layer in range(LAYERS)]
        if batch == 0:
            totals = [
                tuple((jnp.zeros(part.shape[1:], jnp.float32) for part in forward_weights))
                for layer in range(LAYERS)
            ]
            prompt_rows = x_prompt.astype(jnp.float32)
            prompt_states = []
            prompt_pairs = []
            for layer in range(LAYERS):
                weights = forward_sets[layer]
                normed, queries, keys, values = attention_inputs(weights, prompt_rows)
                all_keys, all_values = (
                    lax.all_gather(keys, "seq", axis=0, tiled=True),
                    lax.all_gather(values, "seq", axis=0, tiled=True),
                )
                mixed, log_total = attend_forward(
                    queries, [all_keys], [all_values], [prompt_visible], HEADS
                )
                result, kept = block_output(weights, prompt_rows, mixed)
                prompt_states.append((prompt_rows, normed, queries, mixed, log_total, kept))
                prompt_pairs.append((all_keys, all_values))
                prompt_rows = result
            prompt_out = prompt_rows
        start = batch * per_batch
        stop = start + per_batch
        seen = offsets[start:stop]
        sources = thought_pos[start:stop]
        inputs = x_cont[start:stop].astype(jnp.float32)
        current = inputs.reshape(per_batch * length, width)
        latent_states = []
        for layer in range(LAYERS):
            current, state = cont_forward(
                forward_sets[layer],
                current,
                prompt_pairs[layer][0],
                prompt_pairs[layer][1],
                seen,
                length,
            )
            latent_states.append(state)
        latent = current.reshape(per_batch, length, width)
        shifted = jnp.concatenate(
            [jnp.zeros((per_batch, 1, width), jnp.float32), latent[:, :-1]], 1
        )
        marked = jnp.any(
            sources[:, :, None] + 1 == lax.broadcasted_iota(jnp.int32, (1, 1, length), 2), 1
        )[:, :, None]
        current = jnp.where(marked, shifted, inputs).reshape(per_batch * length, width)
        language_states = []
        for layer in range(LAYERS):
            current, state = cont_forward(
                forward_sets[layer],
                current,
                prompt_pairs[layer][0],
                prompt_pairs[layer][1],
                seen,
                length,
            )
            language_states.append(state)
        outputs_cont.append(current.reshape(per_batch, length, width).astype(jnp.bfloat16))
        backward_weights = fetch_backward(sharded)
        back_sets = [tuple((part[layer] for part in backward_weights)) for layer in range(LAYERS)]
        grad = dy_cont[start:stop].reshape(per_batch * length, width)
        for layer in reversed(range(LAYERS)):
            grad, front, back, key_part, value_part = cont_backward(
                back_sets[layer],
                language_states[layer],
                prompt_pairs[layer][0],
                prompt_pairs[layer][1],
                seen,
                length,
                grad,
            )
            totals[layer] = combine_grads(totals[layer], front, back)
            key_totals[layer] = key_totals[layer] + key_part
            value_totals[layer] = value_totals[layer] + value_part
        grad_mixed_in = grad.reshape(per_batch, length, width)
        grad_latent = jnp.concatenate(
            [
                jnp.where(marked, grad_mixed_in, 0.0)[:, 1:],
                jnp.zeros((per_batch, 1, width), jnp.float32),
            ],
            1,
        )
        grad = grad_latent.reshape(per_batch * length, width)
        for layer in reversed(range(LAYERS)):
            grad, front, back, key_part, value_part = cont_backward(
                back_sets[layer],
                latent_states[layer],
                prompt_pairs[layer][0],
                prompt_pairs[layer][1],
                seen,
                length,
                grad,
            )
            totals[layer] = combine_grads(totals[layer], front, back)
            key_totals[layer] = key_totals[layer] + key_part
            value_totals[layer] = value_totals[layer] + value_part
        grads_cont.append(
            jnp.where(marked, 0.0, grad_mixed_in) + grad.reshape(per_batch, length, width)
        )
    grad = dy_prompt
    for layer in reversed(range(LAYERS)):
        weights = back_sets[layer]
        rows, normed, queries, mixed, log_total, kept = prompt_states[layer]
        all_keys, all_values = prompt_pairs[layer]
        grad_after, grad_mixed, back = output_backward(weights, mixed, kept, grad)
        grad_query, grad_keys, grad_values = attend_backward(
            queries, [all_keys], [all_values], [prompt_visible], log_total, grad_mixed, HEADS
        )
        key_share, value_share = (
            lax.psum_scatter(
                (key_totals[layer] + grad_keys[0]).astype(jnp.bfloat16),
                "seq",
                scatter_dimension=1,
                tiled=True,
            ).astype(jnp.float32),
            lax.psum_scatter(
                (value_totals[layer] + grad_values[0]).astype(jnp.bfloat16),
                "seq",
                scatter_dimension=1,
                tiled=True,
            ).astype(jnp.float32),
        )
        own_keys = jnp.transpose(key_share, (1, 0, 2)).reshape(prompt_dev, width)
        own_values = jnp.transpose(value_share, (1, 0, 2)).reshape(prompt_dev, width)
        grad_in, front = input_backward(weights, rows, normed, grad_query, own_keys, own_values)
        totals[layer] = combine_grads(totals[layer], front, back)
        grad = grad_after + grad_in
    stacked = tuple(
        (jnp.stack([totals[layer][number] for layer in range(LAYERS)], 1) for number in range(13))
    )
    reduced = reduce_all(stacked)
    shares = tuple((jnp.swapaxes(part, 0, 1) for part in reduced))
    return (
        prompt_out.astype(jnp.bfloat16),
        jnp.concatenate(outputs_cont, 0),
        grad,
        jnp.concatenate(grads_cont, 0),
    ) + tuple(shares)


def solution(mesh):
    return jax.shard_map(
        body,
        mesh=mesh,
        in_specs=(
            P(("grp", "seq"), None),
            P(("grp", "seq"), None, None),
            P(("grp", "seq"), None),
            P(("grp", "seq")),
            P(("grp", "seq"), None),
            P(("grp", "seq"), None, None),
            P(None, ("grp", "seq"), None),
            P(None, ("grp", "seq"), None),
            P(None, ("grp", "seq"), None),
            P(None, ("grp", "seq"), None),
            P(None, ("grp", "seq")),
            P(None, ("grp", "seq")),
            P(None, ("grp", "seq")),
            P(None, ("grp", "seq")),
            P(None, ("grp", "seq")),
            P(None, ("grp", "seq")),
            P(None, ("grp", "seq")),
            P(None, ("grp", "seq")),
            P(None, ("grp", "seq")),
        ),
        out_specs=(
            P(("grp", "seq"), None),
            P(("grp", "seq"), None, None),
            P(("grp", "seq"), None),
            P(("grp", "seq"), None, None),
            P(None, ("grp", "seq"), None),
            P(None, ("grp", "seq"), None),
            P(None, ("grp", "seq"), None),
            P(None, ("grp", "seq"), None),
            P(None, ("grp", "seq")),
            P(None, ("grp", "seq")),
            P(None, ("grp", "seq")),
            P(None, ("grp", "seq")),
            P(None, ("grp", "seq")),
            P(None, ("grp", "seq")),
            P(None, ("grp", "seq")),
            P(None, ("grp", "seq")),
            P(None, ("grp", "seq")),
        ),
        check_vma=False,
    )
```

profile of v0, /device:TPU:0, one launch (start us, length us, event | category | flops | bytes accessed | tf_op | source)
XLA Modules:
  0.0 4555.7 jit_solution(14788351106752505787)
XLA Ops:
  10.1 70.7 %all-gather = bf16[32,24,2]{1,2,0:T(2,128)(2,1)S(1)} all-gather(bf16[1,24,2]{1,2,0:T(2,128)(2,1)} %bitcast.1394), channel_id=1, replica_groups=mesh['grp'=4,'seq'=8] {'grp','seq'}, dimensions={0}, use_global_device_ids=true | all-gather | bytes 3168 | tf_op jit(solution)/shard_map/all_gather | solution.py:63
  147.7 66.6 %all-gather.3 = bf16[32,24,2]{1,2,0:T(2,128)(2,1)S(1)} all-gather(bf16[1,24,2]{1,2,0:T(2,128)(2,1)} %bitcast.1396), channel_id=1, replica_groups=mesh['grp'=4,'seq'=8] {'grp','seq'}, dimensions={0}, use_global_device_ids=true | all-gather | bytes 3168 | tf_op jit(solution)/shard_map/all_gather | solution.py:66
  282.3 66.4 %all-gather.4 = bf16[32,24,2]{1,2,0:T(2,128)(2,1)S(1)} all-gather(bf16[1,24,2]{1,2,0:T(2,128)(2,1)} %bitcast.1398), channel_id=1, replica_groups=mesh['grp'=4,'seq'=8] {'grp','seq'}, dimensions={0}, use_global_device_ids=true | all-gather | bytes 3168 | tf_op jit(solution)/shard_map/all_gather | solution.py:67
  413.3 65.4 %all-gather.6 = bf16[32,24,2]{1,2,0:T(2,128)(2,1)S(1)} all-gather(bf16[1,24,2]{1,2,0:T(2,128)(2,1)S(1)} %bitcast.1400), channel_id=1, replica_groups=mesh['grp'=4,'seq'=8] {'grp','seq'}, dimensions={0}, use_global_device_ids=true | all-gather | bytes 3168 | tf_op jit(solution)/shard_map/all_gather | solution.py:69
  688.6 110.0 %while.506 = (s32[]{:T(128)}, bf16[12,256,64]{1,2,0:T(8,128)(2,1)}, f32[12,256]{1,0:T(8,128)}, s32[12]{0:T(128)}, bf16[256,768]{1,0:T(8,128)(2,1)}, /*index=5*/b...) while((s32[]{:T(128)}, bf16[12,256,64]{1,2,0:T(8,128)(2,1)}, ...), condition=%wide.region_24.25_spmd.clone, body=%wide.region_19.24_spmd.clone.sunk | while | flops 51986692 | bytes 3104463 | solution.py:149
  843.4 100.3 %while.510 = (s32[]{:T(128)}, bf16[12,256,64]{1,2,0:T(8,128)(2,1)}, f32[12,256]{1,0:T(8,128)}, s32[12]{0:T(128)}, bf16[256,768]{1,0:T(8,128)(2,1)S(1)}, /*index=...) while((s32[]{:T(128)}, bf16[12,256,64]{1,2,0:T(8,128)(2,1)}, ...), condition=%wide.region_65.66_spmd.clone, body=%wide.region_60.65_spmd.clone.sunk | while | flops 51986692 | bytes 3104463 | solution.py:149
  1054.7 99.9 %while.511 = (s32[]{:T(128)}, bf16[12,256,64]{1,2,0:T(8,128)(2,1)}, f32[12,256]{1,0:T(8,128)}, s32[12]{0:T(128)}, bf16[256,768]{1,0:T(8,128)(2,1)S(1)}, /*index=...) while((s32[]{:T(128)}, bf16[12,256,64]{1,2,0:T(8,128)(2,1)}, ...), condition=%wide.region_75.76_spmd.clone, body=%wide.region_70.75_spmd.clone.sunk | while | flops 51986692 | bytes 3104463 | solution.py:149
  1160.6 102.9 %while.507 = (s32[]{:T(128)}, bf16[12,256,64]{1,2,0:T(8,128)(2,1)}, f32[12,256]{1,0:T(8,128)}, s32[12]{0:T(128)}, bf16[256,768]{1,0:T(8,128)(2,1)}, /*index=5*/b...) while((s32[]{:T(128)}, bf16[12,256,64]{1,2,0:T(8,128)(2,1)}, ...), condition=%wide.region_34.35_spmd.clone, body=%wide.region_29.34_spmd.clone.sunk | while | flops 51986692 | bytes 3104463 | solution.py:149
  1289.5 110.1 %while.508 = (s32[]{:T(128)}, bf16[12,256,64]{1,2,0:T(8,128)(2,1)}, f32[12,256]{1,0:T(8,128)}, s32[12]{0:T(128)}, bf16[256,768]{1,0:T(8,128)(2,1)}, /*index=5*/b...) while((s32[]{:T(128)}, bf16[12,256,64]{1,2,0:T(8,128)(2,1)}, ...), condition=%wide.region_44.45_spmd.clone, body=%wide.region_39.44_spmd.clone.sunk | while | flops 51986692 | bytes 3104463 | solution.py:149
  1416.2 100.2 %while.512 = (s32[]{:T(128)}, bf16[12,256,64]{1,2,0:T(8,128)(2,1)}, f32[12,256]{1,0:T(8,128)}, s32[12]{0:T(128)}, bf16[256,768]{1,0:T(8,128)(2,1)S(1)}, /*index=...) while((s32[]{:T(128)}, bf16[12,256,64]{1,2,0:T(8,128)(2,1)}, ...), condition=%wide.region_85.86_spmd.clone, body=%wide.region_80.85_spmd.clone.sunk | while | flops 51986692 | bytes 3104463 | solution.py:149
  1537.2 102.4 %while.509 = (s32[]{:T(128)}, bf16[12,256,64]{1,2,0:T(8,128)(2,1)}, f32[12,256]{1,0:T(8,128)}, s32[12]{0:T(128)}, bf16[256,768]{1,0:T(8,128)(2,1)}, /*index=5*/b...) while((s32[]{:T(128)}, bf16[12,256,64]{1,2,0:T(8,128)(2,1)}, ...), condition=%wide.region_54.55_spmd.clone, body=%wide.region_49.54_spmd.clone.sunk | while | flops 51986692 | bytes 3104463 | solution.py:149
  1645.5 92.5 %while.513 = (s32[]{:T(128)}, bf16[12,256,64]{1,2,0:T(8,128)(2,1)}, f32[12,256]{1,0:T(8,128)}, s32[12]{0:T(128)}, bf16[256,768]{1,0:T(8,128)(2,1)S(1)}, /*index=...) while((s32[]{:T(128)}, bf16[12,256,64]{1,2,0:T(8,128)(2,1)}, ...), condition=%wide.region_95.96_spmd.clone, body=%wide.region_90.95_spmd.clone.sunk | while | flops 51986692 | bytes 3104463 | solution.py:149
  1772.4 174.4 %while.515 = (s32[]{:T(128)}, bf16[12,256,64]{1,2,0:T(8,128)(2,1)}, f32[12,512,64]{1,2,0:T(8,128)}, bf16[12,256,64]{1,2,0:T(8,128)(2,1)}, f32[12,512,64]{1,2,0:T...) while((s32[]{:T(128)}, bf16[12,256,64]{1,2,0:T(8,128)(2,1)}, ...), condition=%wide.region_108.109_spmd.clone, body=%wide.region_105.108_spmd.clone.sunk | while | flops 127746304 | bytes 7621383 | solution.py:193
  1972.3 175.0 %while.516 = (s32[]{:T(128)}, bf16[12,256,64]{1,2,0:T(8,128)(2,1)}, f32[12,512,64]{1,2,0:T(8,128)}, bf16[12,256,64]{1,2,0:T(8,128)(2,1)}, f32[12,512,64]{1,2,0:T...) while((s32[]{:T(128)}, bf16[12,256,64]{1,2,0:T(8,128)(2,1)}, ...), condition=%wide.region_116.117_spmd.clone, body=%wide.region_113.116_spmd.clone.sunk | while | flops 127746304 | bytes 7621383 | solution.py:193
  2171.5 165.6 %while.517 = (s32[]{:T(128)}, bf16[12,256,64]{1,2,0:T(8,128)(2,1)}, f32[12,512,64]{1,2,0:T(8,128)}, bf16[12,256,64]{1,2,0:T(8,128)(2,1)}, f32[12,512,64]{1,2,0:T...) while((s32[]{:T(128)}, bf16[12,256,64]{1,2,0:T(8,128)(2,1)}, ...), condition=%wide.region_124.125_spmd.clone, body=%wide.region_121.124_spmd.clone.sunk | while | flops 127746304 | bytes 7621383 | solution.py:193
  2345.0 166.5 %while.518 = (s32[]{:T(128)}, bf16[12,256,64]{1,2,0:T(8,128)(2,1)}, f32[12,512,64]{1,2,0:T(8,128)}, bf16[12,256,64]{1,2,0:T(8,128)(2,1)}, f32[12,512,64]{1,2,0:T...) while((s32[]{:T(128)}, bf16[12,256,64]{1,2,0:T(8,128)(2,1)}, ...), condition=%wide.region_130.131_spmd.clone, body=%wide.region_127.130_spmd.clone.sunk | while | flops 127746304 | bytes 7621383 | solution.py:193
  2547.4 174.8 %while.519 = (s32[]{:T(128)}, bf16[12,256,64]{1,2,0:T(8,128)(2,1)}, f32[12,512,64]{1,2,0:T(8,128)}, bf16[12,256,64]{1,2,0:T(8,128)(2,1)}, f32[12,512,64]{1,2,0:T...) while((s32[]{:T(128)}, bf16[12,256,64]{1,2,0:T(8,128)(2,1)}, ...), condition=%wide.region_138.139_spmd.clone, body=%wide.region_135.138_spmd.clone.sunk | while | flops 127746304 | bytes 7621383 | solution.py:193
  2746.4 166.7 %while.520 = (s32[]{:T(128)}, bf16[12,256,64]{1,2,0:T(8,128)(2,1)}, f32[12,512,64]{1,2,0:T(8,128)}, bf16[12,256,64]{1,2,0:T(8,128)(2,1)}, f32[12,512,64]{1,2,0:T...) while((s32[]{:T(128)}, bf16[12,256,64]{1,2,0:T(8,128)(2,1)}, ...), condition=%wide.region_146.147_spmd.clone, body=%wide.region_143.146_spmd.clone.sunk | while | flops 127746304 | bytes 7621823 | solution.py:193
  2984.0 99.6 %while.514 = (s32[]{:T(128)}, bf16[12,64,64]{2,1,0:T(8,128)(2,1)S(1)}, f32[12,512,64]{1,2,0:T(8,128)}, f32[12,512,64]{1,2,0:T(8,128)}, s32[12]{0:T(128)}, /*inde...) while((s32[]{:T(128)}, ...), condition=%wide.region_102.103_spmd.clone, body=%wide.region_100.102_spmd.clone.sunk | while | flops 21336004 | bytes 1742043 | solution.py:193
  3105.2 175.0 %while.522 = (s32[]{:T(128)}, bf16[12,256,64]{1,2,0:T(8,128)(2,1)}, f32[12,512,64]{1,2,0:T(8,128)}, bf16[12,256,64]{1,2,0:T(8,128)(2,1)}, f32[12,512,64]{1,2,0:T...) while((s32[]{:T(128)}, bf16[12,256,64]{1,2,0:T(8,128)(2,1)}, ...), condition=%wide.region_163.164_spmd.clone, body=%wide.region_160.163_spmd.clone.sunk | while | flops 127746304 | bytes 7621383 | solution.py:193
  3318.8 175.8 %while.523 = (s32[]{:T(128)}, bf16[12,256,64]{1,2,0:T(8,128)(2,1)}, f32[12,512,64]{1,2,0:T(8,128)}, bf16[12,256,64]{1,2,0:T(8,128)(2,1)}, f32[12,512,64]{1,2,0:T...) while((s32[]{:T(128)}, bf16[12,256,64]{1,2,0:T(8,128)(2,1)}, ...), condition=%wide.region_171.172_spmd.clone, body=%wide.region_168.171_spmd.clone.sunk | while | flops 127746304 | bytes 7621383 | solution.py:193
  3529.1 74.7 %while.521 = (s32[]{:T(128)}, bf16[12,64,64]{2,1,0:T(8,128)(2,1)S(1)}, f32[12,512,64]{1,2,0:T(8,128)}, f32[12,512,64]{1,2,0:T(8,128)}, s32[12]{0:T(128)S(1)}, /*...) while((s32[]{:T(128)}, ...), condition=%wide.region_155.156_spmd.clone, body=%wide.region_153.155_spmd.clone.sunk | while | flops 21336004 | bytes 1742043 | solution.py:193
  4126.3 211.4 %reduce-scatter.34.cloned.1.call-done = f32[96,2,768]{2,0,1:T(8,128)} async-done(((f32[3072,2,768]{2,0,1:T(8,128)}), f32[96,2,768]{2,0,1:T(8,128)}) %reduce-scatter.34.cloned.1.call-update) | async-done | bytes 589840 | tf_op jit(solution)/shard_map/reduce_scatter | solution.py:98
  4337.6 211.4 %reduce-scatter.32.cloned.1.call-done = f32[24,2,3072]{2,0,1:T(8,128)} async-done(((f32[768,2,3072]{2,0,1:T(8,128)}), f32[24,2,3072]{2,0,1:T(8,128)}) %reduce-scatter.32.cloned.1.call-update) | async-done | bytes 589840 | tf_op jit(solution)/shard_map/reduce_scatter | solution.py:97
  (4649 shorter events, 3756.6 us)
Async XLA Ops:
  7.2 605.3 %copy-start.7 = (bf16[2,256,768]{2,1,0:T(8,128)(2,1)S(1)}, bf16[2,256,768]{2,1,0:T(8,128)(2,1)}, u32[]{:S(2)}) copy-start(bf16[2,256,768]{2,1,0:T(8,128)(2,1)} %param.60) | copy-start | bytes 2359300
  7.2 471.6 %copy-start.518 = (bf16[2,96]{1,0:T(2,128)(2,1)S(1)}, bf16[2,96]{1,0:T(2,128)(2,1)}, u32[]{:S(2)}) copy-start(bf16[2,96]{1,0:T(2,128)(2,1)} %param.76) | copy-start | bytes 1156
  7.2 536.0 %copy-start.519 = (bf16[2,24]{1,0:T(2,128)(2,1)S(1)}, bf16[2,24]{1,0:T(2,128)(2,1)}, u32[]{:S(2)}) copy-start(bf16[2,24]{1,0:T(2,128)(2,1)} %param.77) | copy-start | bytes 292
  7.2 602.7 %copy-start.511 = (s32[2,6]{1,0:T(2,128)S(1)}, s32[2,6]{1,0:T(2,128)}, u32[]{:S(2)}) copy-start(s32[2,6]{1,0:T(2,128)} %param.61) | copy-start | bytes 148
  7.2 605.2 %all-gather.14.cloned.1.call-start = ((), (), s32[]{:S(2)}) async-start(), calls=%async_computation.9 | async-start | bytes 7299072 | tf_op jit(solution)/shard_map/all_gather | solution.py:59
  8.0 825.5 %all-gather.16.cloned.1.call-start = ((), (), s32[]{:S(2)}) async-start(), calls=%async_computation.10 | async-start | bytes 2433024 | tf_op jit(solution)/shard_map/all_gather | solution.py:60
  8.7 940.2 %all-gather.18.cloned.1.call-start = ((), (), s32[]{:S(2)}) async-start(), calls=%async_computation.11 | async-start | bytes 9732096 | tf_op jit(solution)/shard_map/all_gather | solution.py:61
  9.5 945.2 %all-gather.20.cloned.1.call-start = ((), (), s32[]{:S(2)}) async-start(), calls=%async_computation.12 | async-start | bytes 9732096 | tf_op jit(solution)/shard_map/all_gather | solution.py:62
  10.0 3494.7 %reduce-scatter.36.cloned.1.call-start = ((), (), s32[]{:S(2)}) async-start(), calls=%async_computation.17 | async-start | bytes 884736
  146.1 469.7 %copy-start.279 = (f32[256]{0:T(256)}, f32[256]{0:T(256)S(1)}, u32[]{:S(2)}) copy-start(f32[256]{0:T(256)S(1)} %get-tuple-element.3449) | copy-start | bytes 3076
  146.1 472.7 %copy-start.276 = (f32[256]{0:T(256)}, f32[256]{0:T(256)S(1)}, u32[]{:S(2)}) copy-start(f32[256]{0:T(256)S(1)} %get-tuple-element.3448) | copy-start | bytes 3076
  147.6 471.2 %copy-start.282 = (f32[256]{0:T(256)}, f32[256]{0:T(256)S(1)}, u32[]{:S(2)}) copy-start(f32[256]{0:T(256)S(1)} %fusion.924) | copy-start | bytes 3076
  147.7 468.2 %copy-start.285 = (f32[256]{0:T(256)}, f32[256]{0:T(256)S(1)}, u32[]{:S(2)}) copy-start(f32[256]{0:T(256)S(1)} %fusion.916) | copy-start | bytes 3076
  610.5 921.6 %copy-start.224 = (f32[768]{0:T(1024)}, f32[768]{0:T(1024)S(1)}, u32[]{:S(2)}) copy-start(f32[768]{0:T(1024)S(1)} %get-tuple-element.2676) | copy-start | bytes 9220
  611.8 907.9 %copy-start.226 = (f32[768]{0:T(1024)}, f32[768]{0:T(1024)S(1)}, u32[]{:S(2)}) copy-start(f32[768]{0:T(1024)S(1)} %get-tuple-element.2665) | copy-start | bytes 9220
  611.8 2366.8 %copy-start.167 = (f32[768]{0:T(1024)}, f32[768]{0:T(1024)S(1)}, u32[]{:S(2)}) copy-start(f32[768]{0:T(1024)S(1)} %get-tuple-element.3447) | copy-start | bytes 9220
  3094.5 411.8 %reduce-scatter.38.cloned.1.call-start = ((), (), s32[]{:S(2)}) async-start(), calls=%async_computation.18 | async-start | bytes 884736
  3308.0 398.5 %reduce-scatter.42.cloned.1.call-start = ((), (), s32[]{:S(2)}) async-start(), calls=%async_computation.20 | async-start | bytes 884736
  3615.4 125.8 %reduce-scatter.40.cloned.1.call-start = ((), (), s32[]{:S(2)}) async-start(), calls=%async_computation.19 | async-start | bytes 884736
  3632.8 375.6 %reduce-scatter.44.cloned.1.call-start = ((), (), s32[]{:S(2)}) async-start(), calls=%async_computation.21 | async-start | bytes 1622016
  3640.5 426.7 %reduce-scatter.30.cloned.1.call-start = ((), (), s32[]{:S(2)}) async-start(), calls=%async_computation.14 | async-start | bytes 4866048 | tf_op jit(solution)/shard_map/reduce_scatter | solution.py:96
  3647.6 478.6 %reduce-scatter.28.cloned.1.call-start = ((), (), s32[]{:S(2)}) async-start(), calls=%async_computation.13 | async-start | bytes 14598144 | tf_op jit(solution)/shard_map/reduce_scatter | solution.py:95
  3767.9 569.7 %reduce-scatter.34.cloned.1.call-start = ((), (), s32[]{:S(2)}) async-start(), calls=%async_computation.16 | async-start | bytes 19464192 | tf_op jit(solution)/shard_map/reduce_scatter | solution.py:98
  3867.4 681.6 %reduce-scatter.32.cloned.1.call-start = ((), (), s32[]{:S(2)}) async-start(), calls=%async_computation.15 | async-start | bytes 19464192 | tf_op jit(solution)/shard_map/reduce_scatter | solution.py:97
  (569 other events, 6825.1 us)
Sparse Core Ops, SparseCore 0:
  11.1 74.9 all-gather.13
  89.2 55.7 all-gather.15
  148.1 80.5 all-gather.17
  231.6 80.2 all-gather.19
  3094.6 59.5 reduce-scatter.35
  3308.1 59.6 reduce-scatter.37
  3615.5 59.4 reduce-scatter.41
  3678.9 62.2 reduce-scatter.39
  3746.5 96.9 reduce-scatter.43
  3849.4 106.5 reduce-scatter.29
  3962.6 163.6 reduce-scatter.27
  4133.1 204.4 reduce-scatter.33
  4344.6 204.3 reduce-scatter.31
where the time goes:
time: 4620 us; the launch traced here: 4560 us
  matrix products  2140 us (46%)
  blocking collectives  774 us (17%)
  local copies, waits for them, and re-layouts  601 us (13%)
  waiting for transfers between devices  518 us (11%)
  other arithmetic  339 us (7%)
  loops' own time  161 us (3%)
    dot_general x472, matrix products, product_tn(): lax.dot_general(left, right, (((0,), (0,)), ((), ())), preferred_element_...  840 us
    dot_general x688, matrix products, product_nt(): lax.dot_general(left, right, (((1,), (1,)), ((), ())), preferred_element_...  772 us
    dot_general x472, matrix products, product(): return jnp.dot(left, right, preferred_element_type=jnp.float32)  528 us
    dynamic_slice x240, local copies, waits for them, and re-layouts, attend_forward(): outputs, log_total = lax.map(one_head, jnp.arange(heads, dtype=jnp.int32))  248 us
    reduce_scatter x1, waiting for transfers between devices, reduce_all(): lax.psum_scatter(parts[2], ('grp', 'seq'), scatter_dimension=0, tiled=True)  211 us
    reduce_scatter x1, waiting for transfers between devices, reduce_all(): lax.psum_scatter(parts[3], ('grp', 'seq'), scatter_dimension=0, tiled=True)  211 us
    dynamic_update_slice x120, local copies, waits for them, and re-layouts, attend_forward(): outputs, log_total = lax.map(one_head, jnp.arange(heads, dtype=jnp.int32))  126 us
    lt x192, other arithmetic, one_cont(): visible = lax.broadcasted_iota(jnp.int32, (1, plen), 1) < offset  117 us

commit v1 on v0

v1 whole, which is shorter than its diff:
```python
import functools

import jax
import jax.numpy as jnp
from jax import lax
from jax.experimental import pallas as pl
from jax.experimental.pallas import tpu as pltpu
from jax.sharding import PartitionSpec as P

HEADS = 12
LAYERS = 2
epsilon = 1e-05
score_scale = 0.125
gelu_coeff = 0.7978845608028654
gelu_cubic = 0.044715
masked_score = -1e30
ALL = ("grp", "seq")
bf16 = jnp.bfloat16
f32 = jnp.float32


def nn(left, right):
    return lax.dot_general(left, right, (((1,), (0,)), ((), ())), preferred_element_type=f32)


def nt(left, right):
    return lax.dot_general(left, right, (((1,), (1,)), ((), ())), preferred_element_type=f32)


def tn(left, right):
    return lax.dot_general(left, right, (((0,), (0,)), ((), ())), preferred_element_type=f32)


def head_split(pair, width):
    lane = lax.broadcasted_iota(jnp.int32, pair.shape, 1)
    zero = jnp.zeros_like(pair)
    return jnp.where(lane < width, pair, zero), jnp.where(lane >= width, pair, zero)


def attend_kernel(seen_ref, q_ref, k_ref, v_ref, pk_ref, pv_ref, o_ref, lse_ref, *, width):
    offset = seen_ref[pl.program_id(0)]
    length, plen = q_ref.shape[0], pk_ref.shape[0]
    queries = head_split(q_ref[...] * bf16(score_scale), width)
    prompt_keys, own_keys = pk_ref[...], k_ref[...]
    prompt_values, own_values = pv_ref[...].T, v_ref[...].T
    visible = lax.broadcasted_iota(jnp.int32, (plen, length), 0) < offset
    causal = lax.broadcasted_iota(jnp.int32, (length, length), 0) <= lax.broadcasted_iota(
        jnp.int32, (length, length), 1
    )
    mixed = []
    for head in range(2):
        rows = slice(head * width, (head + 1) * width)
        prompt_scores = jnp.where(visible, nt(prompt_keys, queries[head]), masked_score)
        own_scores = jnp.where(causal, nt(own_keys, queries[head]), masked_score)
        top = jnp.maximum(
            jnp.max(prompt_scores, 0, keepdims=True), jnp.max(own_scores, 0, keepdims=True)
        )
        prompt_exp = jnp.exp(prompt_scores - top)
        own_exp = jnp.exp(own_scores - top)
        total = jnp.sum(prompt_exp, 0, keepdims=True) + jnp.sum(own_exp, 0, keepdims=True)
        summed = nn(prompt_values[rows], prompt_exp.astype(bf16)) + nn(
            own_values[rows], own_exp.astype(bf16)
        )
        mixed.append(summed / total)
        lse_ref[0, head : head + 1, :] = top + jnp.log(total)
    o_ref[...] = jnp.concatenate(mixed, 0).T.astype(bf16)


def attend(seen, qkv, pqkv):
    rows, width = qkv.shape[0], qkv.shape[1] // 3
    count, plen = seen.shape[0], pqkv.shape[0]
    length, head_width, pairs = rows // count, width // HEADS, HEADS // 2
    lanes = 2 * head_width

    def part(size, which, own):
        return pl.BlockSpec(
            (size, lanes), lambda c, p, s: (c if own else 0, p + which * pairs)
        )

    return pl.pallas_call(
        functools.partial(attend_kernel, width=head_width),
        grid_spec=pltpu.PrefetchScalarGridSpec(
            num_scalar_prefetch=1,
            grid=(count, pairs),
            in_specs=[
                part(length, 0, True),
                part(length, 1, True),
                part(length, 2, True),
                part(plen, 1, False),
                part(plen, 2, False),
            ],
            out_specs=[
                part(length, 0, True),
                pl.BlockSpec((1, 2, length), lambda c, p, s: (c * pairs + p, 0, 0)),
            ],
        ),
        out_shape=[
            jax.ShapeDtypeStruct((rows, width), bf16),
            jax.ShapeDtypeStruct((count * pairs, 2, length), f32),
        ],
        cost_estimate=pl.CostEstimate(
            flops=4 * rows * (plen + length) * width,
            bytes_accessed=2 * (4 * rows + 2 * plen) * width,
            transcendentals=rows * (plen + length) * HEADS,
        ),
        name="attend",
    )(seen, qkv, qkv, qkv, pqkv, pqkv)


def attend_back_kernel(
    seen_ref,
    q_ref,
    k_ref,
    v_ref,
    pk_ref,
    pv_ref,
    o_ref,
    lse_ref,
    do_ref,
    carry_ref,
    dqkv_ref,
    dpkv_ref,
    *,
    width,
    pairs,
):
    cont, pair = pl.program_id(0), pl.program_id(1)
    offset = seen_ref[cont]
    length, plen = q_ref.shape[0], pk_ref.shape[0]
    lanes = 2 * width
    queries = head_split(q_ref[...] * bf16(score_scale), width)
    grad = do_ref[...]
    grads = head_split(grad, width)
    prompt_keys, own_keys = pk_ref[...], k_ref[...]
    prompt_values, own_values = pv_ref[...], v_ref[...]
    prompt_turned, own_turned = prompt_keys.T, own_keys.T
    product = (grad.astype(f32) * o_ref[...].astype(f32)).T
    visible = lax.broadcasted_iota(jnp.int32, (plen, length), 0) < offset
    causal = lax.broadcasted_iota(jnp.int32, (length, length), 0) <= lax.broadcasted_iota(
        jnp.int32, (length, length), 1
    )
    dq = []
    dk = dv = dpk = dpv = 0.0
    for head in range(2):
        rows = slice(head * width, (head + 1) * width)
        query, grad_head = queries[head], grads[head]
        delta = jnp.sum(product[rows], 0, keepdims=True)
        lse = lse_ref[0, head : head + 1, :]
        prompt_p = jnp.exp(jnp.where(visible, nt(prompt_keys, query), masked_score) - lse)
        own_p = jnp.exp(jnp.where(causal, nt(own_keys, query), masked_score) - lse)
        prompt_ds = (prompt_p * (nt(prompt_values, grad_head) - delta)).astype(bf16)
        own_ds = (own_p * (nt(own_values, grad_head) - delta)).astype(bf16)
        dpv += nn(prompt_p.astype(bf16), grad_head)
        dv += nn(own_p.astype(bf16), grad_head)
        dpk += nn(prompt_ds, query)
        dk += nn(own_ds, query)
        dq.append(nn(prompt_turned[rows], prompt_ds) + nn(own_turned[rows], own_ds))
    first = pl.multiple_of(pair * lanes, lanes)
    columns = [pl.ds(first + number * pairs * lanes, lanes) for number in range(3)]
    dqkv_ref[:, columns[0]] = (jnp.concatenate(dq, 0).T * score_scale).astype(bf16)
    dqkv_ref[:, columns[1]] = dk.astype(bf16)
    dqkv_ref[:, columns[2]] = dv.astype(bf16)

    @pl.when(cont == 0)
    def _():
        dpkv_ref[:, columns[0]] = carry_ref[:, columns[0]] + dpk
        dpkv_ref[:, columns[1]] = carry_ref[:, columns[1]] + dpv

    @pl.when(cont > 0)
    def _():
        dpkv_ref[:, columns[0]] += dpk
        dpkv_ref[:, columns[1]] += dpv


def attend_back(seen, qkv, pqkv, o, lse, do, carry):
    rows, width = qkv.shape[0], qkv.shape[1] // 3
    count, plen = seen.shape[0], pqkv.shape[0]
    length, head_width, pairs = rows // count, width // HEADS, HEADS // 2
    lanes = 2 * head_width

    def part(size, which, own):
        return pl.BlockSpec(
            (size, lanes), lambda c, p, s: (c if own else 0, p + which * pairs)
        )

    whole = pl.BlockSpec((plen, 2 * width), lambda c, p, s: (0, 0))
    return pl.pallas_call(
        functools.partial(attend_back_kernel, width=head_width, pairs=pairs),
        grid_spec=pltpu.PrefetchScalarGridSpec(
            num_scalar_prefetch=1,
            grid=(count, pairs),
            in_specs=[
                part(length, 0, True),
                part(length, 1, True),
                part(length, 2, True),
                part(plen, 1, False),
                part(plen, 2, False),
                part(length, 0, True),
                pl.BlockSpec((1, 2, length), lambda c, p, s: (c * pairs + p, 0, 0)),
                part(length, 0, True),
                whole,
            ],
            out_specs=[pl.BlockSpec((length, 3 * width), lambda c, p, s: (c, 0)), whole],
        ),
        out_shape=[
            jax.ShapeDtypeStruct((rows, 3 * width), bf16),
            jax.ShapeDtypeStruct((plen, 2 * width), f32),
        ],
        cost_estimate=pl.CostEstimate(
            flops=10 * rows * (plen + length) * width,
            bytes_accessed=2 * (8 * rows + 10 * plen) * width,
            transcendentals=rows * (plen + length) * HEADS,
        ),
        name="attend_back",
    )(seen, qkv, qkv, qkv, pqkv, pqkv, o, lse, do, carry)


def stacked_heads(pair, width):
    return jnp.concatenate(head_split(pair, width), 0)


def unstacked(block, width):
    rows = block.shape[0] // 2
    lane = lax.broadcasted_iota(jnp.int32, (rows, block.shape[1]), 1)
    return jnp.where(lane < width, block[:rows], block[rows:])


def prompt_scores(place_ref, q_ref, k_ref, width):
    rows, plen = q_ref.shape[0], k_ref.shape[0]
    queries = stacked_heads(q_ref[...] * bf16(score_scale), width)
    column = lax.broadcasted_iota(jnp.int32, (plen, 2 * rows), 1)
    query_row = jnp.where(column < rows, column, column - rows) + place_ref[0] * rows
    visible = lax.broadcasted_iota(jnp.int32, (plen, 2 * rows), 0) <= query_row
    return queries, jnp.where(visible, nt(k_ref[...], queries), masked_score)


def prompt_kernel(place_ref, q_ref, k_ref, v_ref, o_ref, lse_ref, *, width):
    queries, scores = prompt_scores(place_ref, q_ref, k_ref, width)
    top = jnp.max(scores, 0, keepdims=True)
    expd = jnp.exp(scores - top)
    total = jnp.sum(expd, 0, keepdims=True)
    mixed = nn(v_ref[...].T, expd.astype(bf16)) / total
    o_ref[...] = unstacked(mixed.T, width).astype(bf16)
    lse_ref[0] = top + jnp.log(total)


def prompt_specs(rows, plen, pairs, lanes):
    return [
        pl.BlockSpec((rows, lanes), lambda p, s: (s[0], p)),
        pl.BlockSpec((plen, lanes), lambda p, s: (0, p + pairs)),
        pl.BlockSpec((plen, lanes), lambda p, s: (0, p + 2 * pairs)),
    ]


def prompt_attend(place, pqkv, rows):
    plen, width = pqkv.shape[0], pqkv.shape[1] // 3
    pairs, head_width = HEADS // 2, width // HEADS
    lanes = 2 * head_width
    return pl.pallas_call(
        functools.partial(prompt_kernel, width=head_width),
        grid_spec=pltpu.PrefetchScalarGridSpec(
            num_scalar_prefetch=1,
            grid=(pairs,),
            in_specs=prompt_specs(rows, plen, pairs, lanes),
            out_specs=[
                pl.BlockSpec((rows, lanes), lambda p, s: (0, p)),
                pl.BlockSpec((1, 1, 2 * rows), lambda p, s: (p, 0, 0)),
            ],
        ),
        out_shape=[
            jax.ShapeDtypeStruct((rows, width), bf16),
            jax.ShapeDtypeStruct((pairs, 1, 2 * rows), f32),
        ],
        cost_estimate=pl.CostEstimate(
            flops=4 * rows * plen * width,
            bytes_accessed=6 * plen * width,
            transcendentals=rows * plen * HEADS,
        ),
        name="prompt_attend",
    )(place, pqkv, pqkv, pqkv)


def prompt_back_kernel(
    place_ref, q_ref, k_ref, v_ref, o_ref, lse_ref, do_ref, carry_k, carry_v, dq_ref, dk_ref, dv_ref, *, width
):
    queries, scores = prompt_scores(place_ref, q_ref, k_ref, width)
    grads = stacked_heads(do_ref[...], width)
    output = o_ref[...]
    product = grads.astype(f32) * jnp.concatenate([output, output], 0).astype(f32)
    delta = jnp.sum(product.T, 0, keepdims=True)
    probs = jnp.exp(scores - lse_ref[0])
    ds = (probs * (nt(v_ref[...], grads) - delta)).astype(bf16)
    dv_ref[...] = carry_v[...] + nn(probs.astype(bf16), grads)
    dk_ref[...] = carry_k[...] + nn(ds, queries)
    turned = nn(k_ref[...].T, ds) * score_scale
    dq_ref[...] = unstacked(turned.T, width).astype(bf16)


def prompt_back(place, pqkv, o, lse, do, carry):
    rows, plen, width = o.shape[0], pqkv.shape[0], pqkv.shape[1] // 3
    pairs, head_width = HEADS // 2, width // HEADS
    lanes = 2 * head_width
    own = pl.BlockSpec((rows, lanes), lambda p, s: (0, p))
    keys = pl.BlockSpec((plen, lanes), lambda p, s: (0, p))
    values = pl.BlockSpec((plen, lanes), lambda p, s: (0, p + pairs))
    total = jax.ShapeDtypeStruct((plen, width), f32)
    dq, dk, dv = pl.pallas_call(
        functools.partial(prompt_back_kernel, width=head_width),
        grid_spec=pltpu.PrefetchScalarGridSpec(
            num_scalar_prefetch=1,
            grid=(pairs,),
            in_specs=prompt_specs(rows, plen, pairs, lanes)
            + [own, pl.BlockSpec((1, 1, 2 * rows), lambda p, s: (p, 0, 0)), own, keys, values],
            out_specs=[own, keys, keys],
        ),
        out_shape=[jax.ShapeDtypeStruct((rows, width), bf16), total, total],
        cost_estimate=pl.CostEstimate(
            flops=10 * rows * plen * width,
            bytes_accessed=24 * plen * width,
            transcendentals=rows * plen * HEADS,
        ),
        name="prompt_back",
    )(place, pqkv, pqkv, pqkv, o, lse, do, carry, carry)
    return dq, dk, dv


def normalised(rows):
    centred = rows - jnp.mean(rows, -1, keepdims=True)
    scale = lax.rsqrt(jnp.mean(centred * centred, -1, keepdims=True) + epsilon)
    return centred * scale, scale


def norm(rows, gain, shift):
    return (normalised(rows)[0] * gain + shift).astype(bf16)


def norm_back(rows, gain, grad):
    unit, scale = normalised(rows)
    inner = grad * gain
    spread = inner - jnp.mean(inner, -1, keepdims=True) - unit * jnp.mean(inner * unit, -1, keepdims=True)
    return spread * scale, jnp.sum(grad * unit, 0), jnp.sum(grad, 0)


def gelu(value):
    return 0.5 * value * (1.0 + jnp.tanh(gelu_coeff * (value + gelu_cubic * value * value * value)))


def gelu_slope(value):
    square = value * value
    bent = jnp.tanh(gelu_coeff * value * (1.0 + gelu_cubic * square))
    inner = gelu_coeff * (1.0 + 3.0 * gelu_cubic * square)
    return 0.5 * (1.0 + bent) + 0.5 * value * (1.0 - bent * bent) * inner


def column_sums(block):
    return jnp.sum(block.astype(f32), 0)


def block_output(w, rows, mixed):
    after = rows + nn(mixed, w["out"]) + w["out_bias"]
    normed = norm(after, w["ln2_gain"], w["ln2_bias"])
    hidden = nn(normed, w["fc"]) + w["fc_bias"]
    active = gelu(hidden).astype(bf16)
    result = after + nn(active, w["proj"]) + w["proj_bias"]
    return result, (after, normed, hidden.astype(bf16), active)


def output_backward(w, kept, grad_rows):
    after, normed, hidden, active = kept
    dz = grad_rows.astype(bf16)
    du = (nt(dz, w["proj"]) * gelu_slope(hidden.astype(f32))).astype(bf16)
    grad_in, gain, shift = norm_back(after, w["ln2_gain"], nt(du, w["fc"]))
    grad_after = grad_in + grad_rows
    da = grad_after.astype(bf16)
    do = nt(da, w["out"]).astype(bf16)
    return grad_after, do, (dz, du, da), (gain, shift)


SMALL = (
    "ln1_gain",
    "ln1_bias",
    "q_bias",
    "v_bias",
    "out_bias",
    "ln2_gain",
    "ln2_bias",
    "proj_bias",
    "fc_bias",
)


def body(
    x_prompt,
    x_cont,
    thought_pos,
    offsets,
    dy_prompt,
    dy_cont,
    w_qkv,
    w_out,
    w_fc,
    w_proj,
    ln1_gain,
    ln1_bias,
    q_bias,
    v_bias,
    out_bias,
    ln2_gain,
    ln2_bias,
    fc_bias,
    proj_bias,
):
    count, length, width = x_cont.shape
    rows = count * length
    prompt_dev = x_prompt.shape[0]
    plen = prompt_dev * lax.axis_size("seq")
    devices = lax.axis_size("grp") * lax.axis_size("seq")
    place = lax.axis_index("seq")
    place_ref = place.astype(jnp.int32).reshape(1)
    vectors = dict(
        ln1_gain=ln1_gain,
        ln1_bias=ln1_bias,
        q_bias=q_bias,
        v_bias=v_bias,
        out_bias=out_bias,
        ln2_gain=ln2_gain,
        ln2_bias=ln2_bias,
        proj_bias=proj_bias,
        fc_bias=fc_bias,
    )
    out_rows = w_out.shape[1]
    sizes = [vectors[name].shape[1] for name in SMALL]
    x_all = lax.all_gather(x_prompt, "seq", axis=0, tiled=True)

    weights = []
    for layer in range(LAYERS):
        flat = jnp.concatenate([vectors[name][layer] for name in SMALL])
        extra = jnp.pad(flat, (0, 8 * width - flat.shape[0])).reshape(8, width)
        pack = lax.all_gather(jnp.concatenate([w_out[layer], extra], 0), ALL, axis=0)
        w = dict(out=pack[:, :out_rows].reshape(width, width))
        share = pack[:, out_rows:].reshape(devices, 8 * width)
        first = 0
        for name, size in zip(SMALL, sizes):
            w[name] = share[:, first : first + size].reshape(devices * size).astype(f32)
            first += size
        for name, part in (("qkv", w_qkv), ("fc", w_fc), ("proj", w_proj)):
            w[name] = lax.all_gather(part[layer], ALL, axis=0, tiled=True)
        w["qkv_bias"] = jnp.concatenate([w["q_bias"], jnp.zeros((width,), f32), w["v_bias"]])
        weights.append(w)

    def project(w, normed):
        return (nn(normed, w["qkv"]) + w["qkv_bias"]).astype(bf16)

    prompt_rows = x_prompt.astype(f32)
    prompt_states = []
    for layer in range(LAYERS):
        w = weights[layer]
        if layer == 0:
            all_normed = norm(x_all.astype(f32), w["ln1_gain"], w["ln1_bias"])
        else:
            all_normed = lax.all_gather(
                norm(prompt_rows, w["ln1_gain"], w["ln1_bias"]), "seq", axis=0, tiled=True
            )
        pqkv = project(w, all_normed)
        mixed, lse = prompt_attend(place_ref, pqkv, prompt_dev)
        result, kept = block_output(w, prompt_rows, mixed)
        prompt_states.append((prompt_rows, all_normed, pqkv, mixed, lse, kept))
        prompt_rows = result
    prompt_out = prompt_rows

    def pass_forward(current):
        states = []
        for layer in range(LAYERS):
            w = weights[layer]
            normed = norm(current, w["ln1_gain"], w["ln1_bias"])
            qkv = project(w, normed)
            mixed, lse = attend(offsets, qkv, prompt_states[layer][2])
            result, kept = block_output(w, current, mixed)
            states.append((current, normed, qkv, mixed, lse, kept))
            current = result
        return current, states

    inputs = x_cont.astype(f32)
    latent, latent_states = pass_forward(inputs.reshape(rows, width))
    latent = latent.reshape(count, length, width)
    shifted = jnp.concatenate([jnp.zeros((count, 1, width), f32), latent[:, :-1]], 1)
    marked = jnp.any(
        thought_pos[:, :, None] + 1 == lax.broadcasted_iota(jnp.int32, (1, 1, length), 2), 1
    )[:, :, None]
    current, language_states = pass_forward(jnp.where(marked, shifted, inputs).reshape(rows, width))
    cont_out = current.reshape(count, length, width).astype(bf16)

    pieces = [[] for layer in range(LAYERS)]
    small = [[] for layer in range(LAYERS)]
    carries = [jnp.zeros((plen, 2 * width), f32) for layer in range(LAYERS)]

    def layer_backward(layer, state, grad):
        w = weights[layer]
        before, normed, qkv, mixed, lse, kept = state
        grad_after, do, (dz, du, da), ln2 = output_backward(w, kept, grad)
        dqkv, carries[layer] = attend_back(
            offsets, qkv, prompt_states[layer][2], mixed, lse, do, carries[layer]
        )
        grad_in, gain, shift = norm_back(before, w["ln1_gain"], nt(dqkv, w["qkv"]))
        pieces[layer].append((normed, dqkv, mixed, da, kept[1], du, kept[3], dz))
        small[layer].append((gain, shift) + ln2)
        return grad_after + grad_in

    grad = dy_cont.reshape(rows, width)
    for layer in reversed(range(LAYERS)):
        grad = layer_backward(layer, language_states[layer], grad)
    grad_mixed_in = grad.reshape(count, length, width)
    grad = jnp.concatenate(
        [jnp.where(marked, grad_mixed_in, 0.0)[:, 1:], jnp.zeros((count, 1, width), f32)], 1
    ).reshape(rows, width)
    prompt_grad = dy_prompt
    shares = []
    for layer in reversed(range(LAYERS)):
        w = weights[layer]
        grad = layer_backward(layer, latent_states[layer], grad)
        before, normed, pqkv, mixed, lse, kept = prompt_states[layer]
        grad_after, do, (dz, du, da), ln2 = output_backward(w, kept, prompt_grad)
        dq, dk, dv = prompt_back(place_ref, pqkv, mixed, lse, do, carries[layer])
        dq_all = lax.dynamic_update_slice(
            jnp.zeros((plen, width), bf16), dq, (place * prompt_dev, 0)
        )
        dqkv = jnp.concatenate([dq_all, dk.astype(bf16), dv.astype(bf16)], 1)
        grad_normed = lax.psum_scatter(
            nt(dqkv, w["qkv"]).astype(bf16), "seq", scatter_dimension=0, tiled=True
        ).astype(f32)
        grad_in, gain, shift = norm_back(before, w["ln1_gain"], grad_normed)
        prompt_grad = grad_after + grad_in
        pieces[layer].append((normed, dqkv, mixed, da, kept[1], du, kept[3], dz))
        small[layer].append((gain, shift) + ln2)

        joined = [jnp.concatenate(parts, 0) for parts in zip(*pieces[layer])]
        gain1, shift1, gain2, shift2 = [sum(parts) for parts in zip(*small[layer])]
        qkv_sums = column_sums(joined[1])
        vector_grads = dict(
            ln1_gain=gain1,
            ln1_bias=shift1,
            q_bias=qkv_sums[:width],
            v_bias=qkv_sums[2 * width :],
            out_bias=column_sums(joined[3]),
            ln2_gain=gain2,
            ln2_bias=shift2,
            proj_bias=column_sums(joined[7]),
            fc_bias=column_sums(joined[5]),
        )
        flat = jnp.concatenate(
            [
                vector_grads[name].reshape(devices, size)
                for name, size in zip(SMALL, sizes)
            ],
            1,
        )
        extra = jnp.pad(flat, ((0, 0), (0, 8 * width - flat.shape[1]))).reshape(devices, 8, width)
        pack = jnp.concatenate(
            [tn(joined[2], joined[3]).reshape(devices, out_rows, width), extra], 1
        ).astype(bf16)
        totals = [
            lax.psum_scatter(part.astype(bf16), ALL, scatter_dimension=0, tiled=True).astype(f32)
            for part in (
                tn(joined[6], joined[7]),
                tn(joined[4], joined[5]),
                pack,
                tn(joined[0], joined[1]),
            )
        ]
        share = totals[2].reshape(out_rows + 8, width)
        result = dict(proj=totals[0], fc=totals[1], out=share[:out_rows], qkv=totals[3])
        share = share[out_rows:].reshape(8 * width)
        first = 0
        for name, size in zip(SMALL, sizes):
            result[name] = share[first : first + size]
            first += size
        shares.append(result)
    shares.reverse()
    grad_cont = jnp.where(marked, 0.0, grad_mixed_in) + grad.reshape(count, length, width)
    names = ("qkv", "out", "fc", "proj") + (
        "ln1_gain",
        "ln1_bias",
        "q_bias",
        "v_bias",
        "out_bias",
        "ln2_gain",
        "ln2_bias",
        "fc_bias",
        "proj_bias",
    )
    return (prompt_out.astype(bf16), cont_out, prompt_grad, grad_cont) + tuple(
        jnp.stack([shares[layer][name] for layer in range(LAYERS)]) for name in names
    )


def solution(mesh):
    row, cube, matrix, vector = (
        P(ALL, None),
        P(ALL, None, None),
        P(None, ALL, None),
        P(None, ALL),
    )
    return jax.shard_map(
        body,
        mesh=mesh,
        in_specs=(row, cube, row, P(ALL), row, cube) + (matrix,) * 4 + (vector,) * 9,
        out_specs=(row, cube, row, cube) + (matrix,) * 4 + (vector,) * 9,
        check_vma=False,
    )
```

time: 4620 us -> 1820 us (0.39); the launches traced: 4560 us -> 1810 us
  matrix products: 2140 us -> 285 us
  blocking collectives: 774 us -> 68.6 us
  waiting for transfers between devices: 518 us -> 1090 us
  local copies, waits for them, and re-layouts: 601 us -> 66.9 us
  other arithmetic: 339 us -> 91.3 us
  Pallas kernels: 0 us -> 187 us
  loops' own time: 161 us -> 0 us
    dot_general x1632 -> x56, matrix products: 2140 us -> 285 us  [the longest x24 104 us: nt(): lax.dot_general(left, right, (((1,), (1,)), ((), ())), preferred_element_...]
    all_gather x13 -> x2, blocking collectives: 728 us -> 68.6 us  [the longest x1 34.5 us: body(): lax.all_gather(norm(prompt_rows, w['ln1_gain'], w['ln1_bias']), 'seq', ax...]
    reduce_scatter x4 -> x10, waiting for transfers between devices: 482 us -> 800 us  [the longest x8 757 us: body(): lax.psum_scatter(part.astype(bf16), ALL, scatter_dimension=0, tiled=True)]
    dynamic_slice x336 -> x0, local copies, waits for them, and re-layouts: 316 us -> none  [the longest x240 248 us: attend_forward(): outputs, log_total = lax.map(one_head, jnp.arange(heads, dtype=jnp.int32))]
    all_gather x4 -> x8, waiting for transfers between devices: 0.04 us -> 289 us  [the longest x6 227 us: body(): w[name] = lax.all_gather(part[layer], ALL, axis=0, tiled=True)]
    pallas_call x0 -> x12, Pallas kernels: none -> 187 us  [the longest x4 96.1 us: attend_back(): pl.pallas_call(functools.partial(attend_back_kernel, width=head_width, pa...]
    another operation x20 -> x0, loops' own time: 161 us -> none  [the longest x10 81.6 us: attend_backward(): lax.map(one_head, (jnp.arange(heads, dtype=jnp.int32), log_total))]
    dynamic_update_slice x120 -> x2, local copies, waits for them, and re-layouts: 126 us -> 0.03 us  [body(): lax.dynamic_update_slice(jnp.zeros((plen, width), bf16), dq, (place * pro...]
where the time goes in v1:
time: 1820 us; the launch traced here: 1810 us
  waiting for transfers between devices  1090 us (60%)
  matrix products  285 us (16%)
  Pallas kernels  187 us (10%)
  other arithmetic  91.3 us (5%)
  blocking collectives  68.6 us (4%)
  local copies, waits for them, and re-layouts  66.9 us (4%)
    reduce_scatter x8, waiting for transfers between devices, body(): lax.psum_scatter(part.astype(bf16), ALL, scatter_dimension=0, tiled=True)  757 us
    all_gather x6, waiting for transfers between devices, body(): w[name] = lax.all_gather(part[layer], ALL, axis=0, tiled=True)  227 us
    dot_general x24, matrix products, nt(): lax.dot_general(left, right, (((1,), (1,)), ((), ())), preferred_element_...  104 us
    dot_general x24, matrix products, nn(): lax.dot_general(left, right, (((1,), (0,)), ((), ())), preferred_element_...  97.5 us
    pallas_call x4, Pallas kernels, attend_back(): pl.pallas_call(functools.partial(attend_back_kernel, width=head_width, pa...  96.1 us
    dot_general x8, matrix products, tn(): lax.dot_general(left, right, (((0,), (0,)), ((), ())), preferred_element_...  84 us
    pallas_call x4, Pallas kernels, attend(): pl.pallas_call(functools.partial(attend_kernel, width=head_width), grid_s...  65.9 us
    all_gather x2, waiting for transfers between devices, body(): lax.all_gather(jnp.concatenate([w_out[layer], extra], 0), ALL, axis=0)  62.6 us
  transfers between devices with their start and end apart: 18, of which 17 were waited for; matrix products, arithmetic and copies ran while one was open for 14% of the time, Pallas kernels for 4%

profile of v1, /device:TPU:0, one launch (start us, length us, event | category | flops | bytes accessed | tf_op | source)
XLA Modules:
  0.0 1809.4 jit_solution(17251094254857316147)
XLA Ops:
  20.9 34.2 %all_gather.36 = bf16[512,768]{1,0:T(8,128)(2,1)S(1)} all-gather(bf16[64,768]{1,0:T(8,128)(2,1)S(1)} %copy-done.29), channel_id=1, replica_groups=mesh['grp'=4,'seq'=8] {'seq'}, dimensions={0}, use_global_device_ids=true | all-gather | bytes 884736 | tf_op jit(solution)/shard_map/all_gather | solution.py:433
  74.2 54.9 %all-gather.25.cloned.1.call-done = bf16[1024,768]{1,0:T(8,128)(2,1)} async-done(((bf16[32,768]{1,0:T(8,128)(2,1)}), bf16[1024,768]{1,0:T(8,128)(2,1)}) %all-gather.25.cloned.1.call-update) | async-done | bytes 1572880 | tf_op jit(solution)/shard_map/all_gather | solution.py:439
  143.0 48.7 %all-gather.19.cloned.1.call-done = bf16[1,768,2304]{2,1,0:T(8,128)(2,1)} async-done(((bf16[1,24,2304]{2,1,0:T(8,128)(2,1)}), bf16[1,768,2304]{2,1,0:T(8,128)(2,1)}) %all-gather.19.cloned.1.call-update) | async-done | bytes 3538960 | tf_op jit(solution)/shard_map/all_gather | solution.py:447
  230.8 26.7 %all-gather.21.cloned.1.call-done = bf16[1,768,3072]{2,1,0:T(8,128)(2,1)} async-done(((bf16[1,24,3072]{2,1,0:T(8,128)(2,1)}), bf16[1,768,3072]{2,1,0:T(8,128)(2,1)}) %all-gather.21.cloned.1.call-update) | async-done | bytes 4718608 | tf_op jit(solution)/shard_map/all_gather | solution.py:447
  261.8 61.1 %all-gather.23.cloned.1.call-done = bf16[1,3072,768]{2,1,0:T(8,128)(2,1)} async-done(((bf16[1,96,768]{2,1,0:T(8,128)(2,1)}), bf16[1,3072,768]{2,1,0:T(8,128)(2,1)}) %all-gather.23.cloned.1.call-update) | async-done | bytes 4718608 | tf_op jit(solution)/shard_map/all_gather | solution.py:447
  327.5 34.5 %all_gather.44 = bf16[512,768]{1,0:T(8,128)(2,1)} all-gather(bf16[64,768]{1,0:T(8,128)(2,1)S(1)} %add_convert_fusion.13), channel_id=1, replica_groups=mesh['grp'=4,'seq'=8] {'seq'}, dimensions={0}, use_global_device_ids=true | all-gather | bytes 884736 | tf_op jit(solution)/shard_map/all_gather | solution.py:461
  362.0 24.9 %all-gather.27.cloned.1.call-done = bf16[1,768,2304]{2,1,0:T(8,128)(2,1)} async-done(((bf16[1,24,2304]{2,1,0:T(8,128)(2,1)}), bf16[1,768,2304]{2,1,0:T(8,128)(2,1)}) %all-gather.27.cloned.1.call-update) | async-done | bytes 3538960 | tf_op jit(solution)/shard_map/all_gather | solution.py:447
  420.3 16.9 attend.5
  463.0 54.8 %all-gather.31.cloned.1.call-done = bf16[1,3072,768]{2,1,0:T(8,128)(2,1)} async-done(((bf16[1,96,768]{2,1,0:T(8,128)(2,1)}), bf16[1,3072,768]{2,1,0:T(8,128)(2,1)}) %all-gather.31.cloned.1.call-update) | async-done | bytes 4718608 | tf_op jit(solution)/shard_map/all_gather | solution.py:447
  564.9 16.4 attend.7
  607.0 23.9 %attend_back.4 = (bf16[512,2304]{1,0:T(8,128)(2,1)}, f32[512,1536]{1,0:T(8,128)}) custom-call(s32[2]{0:T(128)} %seen_ref.15, bf16[512,2304]{1,0:T(8,128)(2,1)} %fusion.179.q_ref.k_ref.v_ref, bf16[512,2304]{1,0:T(8,128)(2,1)} %fusion.179.q_ref.k_ref.v_ref, bf16[512,2304]{1,0:T(8,128)(2,1)} %fusion.179.q_ref.k_ref.v_ref, ...), custom_call_target="tpu_custom_call" | custom-call | flops 3019898880 | bytes 14155776 | tf_op jit(solution)/shard_map/attend_back/pallas_call | solution.py:187
  656.0 23.9 %attend_back.5 = (bf16[512,2304]{1,0:T(8,128)(2,1)}, f32[512,1536]{1,0:T(8,128)}) custom-call(s32[2]{0:T(128)} %seen_ref.15, bf16[512,2304]{1,0:T(8,128)(2,1)} %fusion.178.q_ref.k_ref.v_ref, bf16[512,2304]{1,0:T(8,128)(2,1)} %fusion.178.q_ref.k_ref.v_ref, bf16[512,2304]{1,0:T(8,128)(2,1)} %fusion.178.q_ref.k_ref.v_ref, ...), custom_call_target="tpu_custom_call" | custom-call | flops 3019898880 | bytes 14155776 | tf_op jit(solution)/shard_map/attend_back/pallas_call | solution.py:187
  705.3 24.1 %attend_back.6 = (bf16[512,2304]{1,0:T(8,128)(2,1)}, f32[512,1536]{1,0:T(8,128)}) custom-call(s32[2]{0:T(128)} %seen_ref.15, bf16[512,2304]{1,0:T(8,128)(2,1)} %fusion.177.q_ref.k_ref.v_ref, bf16[512,2304]{1,0:T(8,128)(2,1)} %fusion.177.q_ref.k_ref.v_ref, bf16[512,2304]{1,0:T(8,128)(2,1)} %fusion.177.q_ref.k_ref.v_ref, ...), custom_call_target="tpu_custom_call" | custom-call | flops 3019898880 | bytes 14155776 | tf_op jit(solution)/shard_map/attend_back/pallas_call | solution.py:187
  808.2 24.3 %attend_back.7 = (bf16[512,2304]{1,0:T(8,128)(2,1)}, f32[512,1536]{1,0:T(8,128)}) custom-call(s32[2]{0:T(128)} %seen_ref.15, bf16[512,2304]{1,0:T(8,128)(2,1)} %fusion.176.q_ref.k_ref.v_ref, bf16[512,2304]{1,0:T(8,128)(2,1)} %fusion.176.q_ref.k_ref.v_ref, bf16[512,2304]{1,0:T(8,128)(2,1)} %fusion.176.q_ref.k_ref.v_ref, ...), custom_call_target="tpu_custom_call" | custom-call | flops 3019898880 | bytes 14155776 | tf_op jit(solution)/shard_map/attend_back/pallas_call | solution.py:187
  889.5 43.1 %reduce-scatter.13.cloned.1.call-done = bf16[64,768]{1,0:T(8,128)(2,1)} async-done(((bf16[512,768]{1,0:T(8,128)(2,1)}), bf16[64,768]{1,0:T(8,128)(2,1)}) %reduce-scatter.13.cloned.1.call-update) | async-done | bytes 98320 | tf_op jit(solution)/shard_map/reduce_scatter | solution.py:528
  937.0 17.1 fusion.124
  955.2 17.1 fusion.127
  1036.5 100.4 %reduce-scatter.19.cloned.1.call-done = bf16[1,32,768]{2,1,0:T(8,128)(2,1)} async-done(((bf16[32,32,768]{2,1,0:T(8,128)(2,1)}), bf16[1,32,768]{2,1,0:T(8,128)(2,1)}) %reduce-scatter.19.cloned.1.call-update) | async-done | bytes 49168 | tf_op jit(solution)/shard_map/reduce_scatter | solution.py:562
  1144.3 100.5 %reduce-scatter.17.cloned.1.call-done = bf16[24,2304]{1,0:T(8,128)(2,1)} async-done(((bf16[768,2304]{1,0:T(8,128)(2,1)}), bf16[24,2304]{1,0:T(8,128)(2,1)}) %reduce-scatter.17.cloned.1.call-update) | async-done | bytes 110608 | tf_op jit(solution)/shard_map/reduce_scatter | solution.py:562
  1244.8 108.0 %reduce-scatter.15.cloned.1.call-done = bf16[24,2304]{1,0:T(8,128)(2,1)} async-done(((bf16[768,2304]{1,0:T(8,128)(2,1)}), bf16[24,2304]{1,0:T(8,128)(2,1)}) %reduce-scatter.15.cloned.1.call-update) | async-done | bytes 110608 | tf_op jit(solution)/shard_map/reduce_scatter | solution.py:562
  1354.6 110.1 %reduce-scatter.29.cloned.1.call-done = bf16[96,768]{1,0:T(8,128)(2,1)} async-done(((bf16[3072,768]{1,0:T(8,128)(2,1)}), bf16[96,768]{1,0:T(8,128)(2,1)}) %reduce-scatter.29.cloned.1.call-update) | async-done | bytes 147472 | tf_op jit(solution)/shard_map/reduce_scatter | solution.py:562
  1464.7 111.6 %reduce-scatter.27.cloned.1.call-done = bf16[96,768]{1,0:T(8,128)(2,1)} async-done(((bf16[3072,768]{1,0:T(8,128)(2,1)}), bf16[96,768]{1,0:T(8,128)(2,1)}) %reduce-scatter.27.cloned.1.call-update) | async-done | bytes 147472 | tf_op jit(solution)/shard_map/reduce_scatter | solution.py:562
  1578.1 110.4 %reduce-scatter.25.cloned.1.call-done = bf16[24,3072]{1,0:T(8,128)(2,1)} async-done(((bf16[768,3072]{1,0:T(8,128)(2,1)}), bf16[24,3072]{1,0:T(8,128)(2,1)}) %reduce-scatter.25.cloned.1.call-update) | async-done | bytes 147472 | tf_op jit(solution)/shard_map/reduce_scatter | solution.py:562
  1688.5 111.7 %reduce-scatter.23.cloned.1.call-done = bf16[24,3072]{1,0:T(8,128)(2,1)} async-done(((bf16[768,3072]{1,0:T(8,128)(2,1)}), bf16[24,3072]{1,0:T(8,128)(2,1)}) %reduce-scatter.23.cloned.1.call-update) | async-done | bytes 147472 | tf_op jit(solution)/shard_map/reduce_scatter | solution.py:562
  (791 shorter events, 493.0 us)
Async XLA Ops:
  7.2 64.4 %all-gather.17.cloned.1.call-start = ((), (), s32[]{:S(2)}) async-start(), calls=%async_computation.20 | async-start | bytes 1622016 | tf_op jit(solution)/shard_map/all_gather | solution.py:439
  12.5 116.6 %all-gather.25.cloned.1.call-start = ((), (), s32[]{:S(2)}) async-start(), calls=%async_computation.24 | async-start | bytes 1622016 | tf_op jit(solution)/shard_map/all_gather | solution.py:439
  13.4 178.3 %all-gather.19.cloned.1.call-start = ((), (), s32[]{:S(2)}) async-start(), calls=%async_computation.21 | async-start | bytes 3649536 | tf_op jit(solution)/shard_map/all_gather | solution.py:447
  15.1 242.4 %all-gather.21.cloned.1.call-start = ((), (), s32[]{:S(2)}) async-start(), calls=%async_computation.22 | async-start | bytes 4866048 | tf_op jit(solution)/shard_map/all_gather | solution.py:447
  17.0 305.9 %all-gather.23.cloned.1.call-start = ((), (), s32[]{:S(2)}) async-start(), calls=%async_computation.23 | async-start | bytes 4866048 | tf_op jit(solution)/shard_map/all_gather | solution.py:447
  18.8 368.1 %all-gather.27.cloned.1.call-start = ((), (), s32[]{:S(2)}) async-start(), calls=%async_computation.25 | async-start | bytes 3649536 | tf_op jit(solution)/shard_map/all_gather | solution.py:447
  19.3 433.6 %all-gather.29.cloned.1.call-start = ((), (), s32[]{:S(2)}) async-start(), calls=%async_computation.26 | async-start | bytes 4866048 | tf_op jit(solution)/shard_map/all_gather | solution.py:447
  20.1 497.8 %all-gather.31.cloned.1.call-start = ((), (), s32[]{:S(2)}) async-start(), calls=%async_computation.27 | async-start | bytes 4866048 | tf_op jit(solution)/shard_map/all_gather | solution.py:447
  20.8 821.2 %reduce-scatter.11.cloned.1.call-start = ((), (), s32[]{:S(2)}) async-start(), calls=%async_computation.10 | async-start | bytes 884736 | tf_op jit(solution)/shard_map/reduce_scatter | solution.py:528
  143.0 54.4 %copy-start.49 = (bf16[512,768]{1,0:T(8,128)(2,1)}, bf16[512,768]{1,0:T(8,128)(2,1)S(1)}, u32[]{:S(2)}) copy-start(bf16[512,768]{1,0:T(8,128)(2,1)S(1)} %get-tuple-element.192) | copy-start | bytes 2359300
  219.2 188.4 %copy-start.6 = (f32[512,768]{1,0:T(8,128)}, f32[512,768]{1,0:T(8,128)S(1)}, u32[]{:S(2)}) copy-start(f32[512,768]{1,0:T(8,128)S(1)} %get-tuple-element.233) | copy-start | bytes 4718596
  442.6 75.3 %copy-start.12 = (f32[512,768]{1,0:T(8,128)S(1)}, f32[512,768]{1,0:T(8,128)}, u32[]{:S(2)}) copy-start(f32[512,768]{1,0:T(8,128)} %copy-done.11) | copy-start | bytes 4718596
  777.1 155.5 %reduce-scatter.13.cloned.1.call-start = ((), (), s32[]{:S(2)}) async-start(), calls=%async_computation.11 | async-start | bytes 884736 | tf_op jit(solution)/shard_map/reduce_scatter | solution.py:528
  871.0 163.8 %reduce-scatter.21.cloned.1.call-start = ((), (), s32[]{:S(2)}) async-start(), calls=%async_computation.15 | async-start | bytes 1622016 | tf_op jit(solution)/shard_map/reduce_scatter | solution.py:562
  881.1 255.8 %reduce-scatter.19.cloned.1.call-start = ((), (), s32[]{:S(2)}) async-start(), calls=%async_computation.14 | async-start | bytes 1622016 | tf_op jit(solution)/shard_map/reduce_scatter | solution.py:562
  884.8 49.2 %copy-start.119 = (bf16[32,96]{1,0:T(8,128)(2,1)S(1)}, bf16[32,96]{1,0:T(8,128)(2,1)}, u32[]{:S(2)}) copy-start(bf16[32,96]{1,0:T(8,128)(2,1)} %reshape.678) | copy-start | bytes 18436
  884.8 49.2 %copy-start.120 = (bf16[32,24]{1,0:T(8,128)(2,1)S(1)}, bf16[32,24]{1,0:T(8,128)(2,1)}, u32[]{:S(2)}) copy-start(bf16[32,24]{1,0:T(8,128)(2,1)} %reshape.677) | copy-start | bytes 4612
  884.8 49.2 %copy-start.121 = (bf16[32,24]{1,0:T(8,128)(2,1)S(1)}, bf16[32,24]{1,0:T(8,128)(2,1)}, u32[]{:S(2)}) copy-start(bf16[32,24]{1,0:T(8,128)(2,1)} %add.838) | copy-start | bytes 4612
  936.9 307.9 %reduce-scatter.17.cloned.1.call-start = ((), (), s32[]{:S(2)}) async-start(), calls=%async_computation.13 | async-start | bytes 3649536 | tf_op jit(solution)/shard_map/reduce_scatter | solution.py:562
  954.1 398.8 %reduce-scatter.15.cloned.1.call-start = ((), (), s32[]{:S(2)}) async-start(), calls=%async_computation.12 | async-start | bytes 3649536 | tf_op jit(solution)/shard_map/reduce_scatter | solution.py:562
  972.3 492.4 %reduce-scatter.29.cloned.1.call-start = ((), (), s32[]{:S(2)}) async-start(), calls=%async_computation.19 | async-start | bytes 4866048 | tf_op jit(solution)/shard_map/reduce_scatter | solution.py:562
  983.7 592.6 %reduce-scatter.27.cloned.1.call-start = ((), (), s32[]{:S(2)}) async-start(), calls=%async_computation.18 | async-start | bytes 4866048 | tf_op jit(solution)/shard_map/reduce_scatter | solution.py:562
  995.1 693.4 %reduce-scatter.25.cloned.1.call-start = ((), (), s32[]{:S(2)}) async-start(), calls=%async_computation.17 | async-start | bytes 4866048 | tf_op jit(solution)/shard_map/reduce_scatter | solution.py:562
  1006.5 793.7 %reduce-scatter.23.cloned.1.call-start = ((), (), s32[]{:S(2)}) async-start(), calls=%async_computation.16 | async-start | bytes 4866048 | tf_op jit(solution)/shard_map/reduce_scatter | solution.py:562
  (217 other events, 1514.2 us)
Sparse Core Ops, SparseCore 0:
  12.7 58.8 all-gather.16
  75.1 53.9 all-gather.24
  132.7 58.9 all-gather.18
  195.1 62.3 all-gather.20
  260.9 61.9 all-gather.22
  326.3 60.5 all-gather.26
  390.5 62.3 all-gather.28
  455.9 61.9 all-gather.30
  777.2 61.6 reduce-scatter.10
  870.9 61.6 reduce-scatter.12
  937.8 96.9 reduce-scatter.20
  1039.9 96.9 reduce-scatter.18
  1142.3 102.4 reduce-scatter.16
  1250.1 102.6 reduce-scatter.14
  1358.2 106.4 reduce-scatter.28
  1470.0 106.2 reduce-scatter.26
  1581.6 106.8 reduce-scatter.24
  1693.8 106.3 reduce-scatter.22

commit v2 on v1

--- a/solution.py
+++ b/solution.py
@@ -374,6 +374,77 @@
     da = grad_after.astype(bf16)
     do = nt(da, w["out"]).astype(bf16)
     return grad_after, do, (dz, du, da), (gain, shift)
+
+
+def swap(value, code, axes, total):
+    return lax.ppermute(value, axes, [(i, i ^ code) for i in range(total)])
+
+
+def lay_kernel(place_ref, *refs, codes):
+    out_ref, sems = refs[-2], refs[-1]
+    copies = []
+    for ref, group in zip(refs, codes):
+        for number, code in enumerate(group):
+            copies.append(
+                pltpu.make_async_copy(
+                    ref.at[number], out_ref.at[place_ref[0] ^ code], sems.at[len(copies)]
+                )
+            )
+            copies[-1].start()
+    for copy in copies:
+        copy.wait()
+
+
+def lay_out(place, pieces, codes, name):
+    total = sum(len(group) for group in codes)
+    shape = (total,) + pieces[0].shape[1:]
+    return pl.pallas_call(
+        functools.partial(lay_kernel, codes=codes),
+        in_specs=[pl.BlockSpec(memory_space=pltpu.SMEM)]
+        + [pl.BlockSpec(memory_space=pl.ANY)] * len(pieces),
+        out_specs=pl.BlockSpec(shape, lambda: (0, 0, 0)),
+        out_shape=jax.ShapeDtypeStruct(shape, pieces[0].dtype),
+        scratch_shapes=[pltpu.SemaphoreType.DMA((total,))],
+        cost_estimate=pl.CostEstimate(
+            flops=0, bytes_accessed=4 * shape[0] * shape[1] * shape[2], transcendentals=0
+        ),
+        name=name,
+    )(place, *pieces)
+
+
+def gather_blocks(part, place, x_first, tree):
+    if not tree:
+        return lax.all_gather(part, ALL, axis=0)
+    own = part[None]
+    base = jnp.concatenate([own] + [swap(own, code, ALL, 32) for code in (2, 4, 6)], 0)
+    first, second = (1, 16) if x_first else (16, 1)
+    pieces = [base, swap(base, first, ALL, 32)]
+    pieces += [swap(piece, second, ALL, 32) for piece in pieces]
+    pieces += [swap(piece, 8, ALL, 32) for piece in pieces]
+    starts = [0, first, second, first | second]
+    starts += [start | 8 for start in starts]
+    codes = tuple(tuple(start | code for code in (0, 2, 4, 6)) for start in starts)
+    return lay_out(place, pieces, codes, "lay_weights")
+
+
+def gather_rows(part, place, tree):
+    if not tree:
+        return lax.all_gather(part, "seq", axis=0, tiled=True)
+    own = part[None]
+    pieces = [own] + [swap(own, code, "seq", 8) for code in range(1, 8)]
+    codes = tuple((code,) for code in range(8))
+    return lay_out(place, pieces, codes, "lay_rows").reshape(8 * part.shape[0], part.shape[1])
+
+
+def scatter_rows(block, place, tree):
+    if not tree:
+        return lax.psum_scatter(block, "seq", scatter_dimension=0, tiled=True).astype(f32)
+    rows = block.shape[0] // 8
+    total = lax.dynamic_slice_in_dim(block, place * rows, rows, 0).astype(f32)
+    for code in range(1, 8):
+        piece = lax.dynamic_slice_in_dim(block, (place ^ code) * rows, rows, 0)
+        total = total + swap(piece, code, "seq", 8).astype(f32)
+    return total
 
 
 SMALL = (
@@ -430,21 +501,25 @@
     )
     out_rows = w_out.shape[1]
     sizes = [vectors[name].shape[1] for name in SMALL]
-    x_all = lax.all_gather(x_prompt, "seq", axis=0, tiled=True)
+    tree = (
+        lax.axis_size("grp") == 4 and lax.axis_size("seq") == 8 and out_rows % 8 == 0 and prompt_dev % 16 == 0
+    )
+    flat_ref = (lax.axis_index("grp") * lax.axis_size("seq") + place).astype(jnp.int32).reshape(1)
+    x_all = gather_rows(x_prompt, place_ref, tree)
 
     weights = []
     for layer in range(LAYERS):
         flat = jnp.concatenate([vectors[name][layer] for name in SMALL])
         extra = jnp.pad(flat, (0, 8 * width - flat.shape[0])).reshape(8, width)
-        pack = lax.all_gather(jnp.concatenate([w_out[layer], extra], 0), ALL, axis=0)
+        pack = gather_blocks(jnp.concatenate([w_out[layer], extra], 0), flat_ref, False, tree)
         w = dict(out=pack[:, :out_rows].reshape(width, width))
         share = pack[:, out_rows:].reshape(devices, 8 * width)
         first = 0
         for name, size in zip(SMALL, sizes):
             w[name] = share[:, first : first + size].reshape(devices * size).astype(f32)
             first += size
-        for name, part in (("qkv", w_qkv), ("fc", w_fc), ("proj", w_proj)):
-            w[name] = lax.all_gather(part[layer], ALL, axis=0, tiled=True)
+        for name, part, x_first in (("qkv", w_qkv, False), ("fc", w_fc, True), ("proj", w_proj, layer == 0)):
+            w[name] = gather_blocks(part[layer], flat_ref, x_first, tree).reshape(-1, part.shape[2])
         w["qkv_bias"] = jnp.concatenate([w["q_bias"], jnp.zeros((width,), f32), w["v_bias"]])
         weights.append(w)
 
@@ -458,9 +533,7 @@
         if layer == 0:
             all_normed = norm(x_all.astype(f32), w["ln1_gain"], w["ln1_bias"])
         else:
-            all_normed = lax.all_gather(
-                norm(prompt_rows, w["ln1_gain"], w["ln1_bias"]), "seq", axis=0, tiled=True
-            )
+            all_normed = gather_rows(norm(prompt_rows, w["ln1_gain"], w["ln1_bias"]), place_ref, tree)
         pqkv = project(w, all_normed)
         mixed, lse = prompt_attend(place_ref, pqkv, prompt_dev)
         result, kept = block_output(w, prompt_rows, mixed)
@@ -525,9 +598,7 @@
             jnp.zeros((plen, width), bf16), dq, (place * prompt_dev, 0)
         )
         dqkv = jnp.concatenate([dq_all, dk.astype(bf16), dv.astype(bf16)], 1)
-        grad_normed = lax.psum_scatter(
-            nt(dqkv, w["qkv"]).astype(bf16), "seq", scatter_dimension=0, tiled=True
-        ).astype(f32)
+        grad_normed = scatter_rows(nt(dqkv, w["qkv"]).astype(bf16), place, tree)
         grad_in, gain, shift = norm_back(before, w["ln1_gain"], grad_normed)
         prompt_grad = grad_after + grad_in
         pieces[layer].append((normed, dqkv, mixed, da, kept[1], du, kept[3], dz))
@@ -554,22 +625,29 @@
             ],
             1,
         )
-        extra = jnp.pad(flat, ((0, 0), (0, 8 * width - flat.shape[1]))).reshape(devices, 8, width)
+        small_lanes = -(-flat.shape[1] // (128 * out_rows)) * 128
+        extra = jnp.pad(flat, ((0, 0), (0, out_rows * small_lanes - flat.shape[1])))
+        mlp = tn(joined[6], joined[7]).astype(bf16).reshape(devices, -1, out_rows, width)
         pack = jnp.concatenate(
-            [tn(joined[2], joined[3]).reshape(devices, out_rows, width), extra], 1
-        ).astype(bf16)
-        totals = [
-            lax.psum_scatter(part.astype(bf16), ALL, scatter_dimension=0, tiled=True).astype(f32)
-            for part in (
-                tn(joined[6], joined[7]),
-                tn(joined[4], joined[5]),
-                pack,
-                tn(joined[0], joined[1]),
-            )
-        ]
-        share = totals[2].reshape(out_rows + 8, width)
-        result = dict(proj=totals[0], fc=totals[1], out=share[:out_rows], qkv=totals[3])
-        share = share[out_rows:].reshape(8 * width)
+            [
+                tn(joined[0], joined[1]).astype(bf16).reshape(devices, out_rows, -1),
+                tn(joined[4], joined[5]).astype(bf16).reshape(devices, out_rows, -1),
+                tn(joined[2], joined[3]).astype(bf16).reshape(devices, out_rows, width),
+            ]
+            + [mlp[:, number] for number in range(mlp.shape[1])]
+            + [extra.astype(bf16).reshape(devices, out_rows, small_lanes)],
+            2,
+        )
+        total = lax.psum_scatter(pack, ALL, scatter_dimension=0, tiled=True).astype(f32)[0]
+        result = dict(
+            qkv=total[:, : 3 * width],
+            fc=total[:, 3 * width : 7 * width],
+            out=total[:, 7 * width : 8 * width],
+            proj=jnp.concatenate(
+                [total[:, (8 + number) * width : (9 + number) * width] for number in range(mlp.shape[1])], 0
+            ),
+        )
+        share = total[:, (8 + mlp.shape[1]) * width :].reshape(-1)
         first = 0
         for name, size in zip(SMALL, sizes):
             result[name] = share[first : first + size]

time: 1820 us -> 1060 us (0.58)
  waiting for transfers between devices: 1090 us -> 300 us
  starting transfers between devices: 1.67 us -> 121 us
  blocking collectives: 68.6 us -> 0 us
  matrix products: 285 us -> 240 us
  Pallas kernels: 187 us -> 226 us
    reduce_scatter x10 -> x0, waiting for transfers between devices: 800 us -> none  [the longest x8 757 us: body(): lax.psum_scatter(part.astype(bf16), ALL, scatter_dimension=0, tiled=True)]
    all_gather x8 -> x0, waiting for transfers between devices: 289 us -> none  [the longest x6 227 us: body(): w[name] = lax.all_gather(part[layer], ALL, axis=0, tiled=True)]
    unnamed x18 -> x4, waiting for transfers between devices: 2.16 us -> 183 us
    ppermute x0 -> x108, starting transfers between devices: none -> 121 us  [swap(): return lax.ppermute(value, axes, [(i, i ^ code) for i in range(total)])]
    ppermute x0 -> x108, waiting for transfers between devices: none -> 116 us  [swap(): return lax.ppermute(value, axes, [(i, i ^ code) for i in range(total)])]
    all_gather x2 -> x0, blocking collectives: 68.6 us -> none  [the longest x1 34.5 us: body(): lax.all_gather(norm(prompt_rows, w['ln1_gain'], w['ln1_bias']), 'seq', ax...]
    pallas_call x0 -> x10, Pallas kernels: none -> 37.7 us  [lay_out(): pl.pallas_call(functools.partial(lay_kernel, codes=codes), in_specs=[pl.B...]
    dot_general x8, matrix products: 84 us -> 53.5 us  [tn(): lax.dot_general(left, right, (((0,), (0,)), ((), ())), preferred_element_...]
  transfers between devices with their start and end apart: 18 -> 110, of which waited for: 17 -> 24; matrix products, arithmetic and copies ran while one was open for 14% -> 18% of each run, Pallas kernels for 4% -> 9%
where the time goes in v2:
time: 1060 us; the launch traced here: 1050 us
  waiting for transfers between devices  300 us (28%)
  matrix products  240 us (23%)
  Pallas kernels  226 us (21%)
  starting transfers between devices  121 us (11%)
  other arithmetic  74.8 us (7%)
  local copies, waits for them, and re-layouts  69.5 us (7%)
  between operations  18.4 us (2%)
    unnamed x4, waiting for transfers between devices  183 us
    ppermute x108, starting transfers between devices, swap(): return lax.ppermute(value, axes, [(i, i ^ code) for i in range(total)])  121 us
    ppermute x108, waiting for transfers between devices, swap(): return lax.ppermute(value, axes, [(i, i ^ code) for i in range(total)])  116 us
    dot_general x24, matrix products, nt(): lax.dot_general(left, right, (((1,), (1,)), ((), ())), preferred_element_...  97.2 us
    pallas_call x4, Pallas kernels, attend_back(): pl.pallas_call(functools.partial(attend_back_kernel, width=head_width, pa...  96.6 us
    dot_general x24, matrix products, nn(): lax.dot_general(left, right, (((1,), (0,)), ((), ())), preferred_element_...  89.2 us
    pallas_call x4, Pallas kernels, attend(): pl.pallas_call(functools.partial(attend_kernel, width=head_width), grid_s...  65.7 us
    dot_general x8, matrix products, tn(): lax.dot_general(left, right, (((0,), (0,)), ((), ())), preferred_element_...  53.5 us
  transfers between devices with their start and end apart: 110, of which 24 were waited for; matrix products, arithmetic and copies ran while one was open for 18% of the time, Pallas kernels for 9%

profile of v2, /device:TPU:0, one launch (start us, length us, event | category | flops | bytes accessed | tf_op | source)
XLA Modules:
  0.0 1049.7 jit_solution(8666626924246146398)
XLA Ops:
  48.2 8.5 collective-permute-done.4.refs_5_
  138.4 8.2 collective-permute-done.52.refs_3_
  188.5 16.3 %attend.4 = (bf16[512,768]{1,0:T(8,128)(2,1)}, f32[12,2,256]{2,1,0:T(2,128)}) custom-call(s32[2]{0:T(128)} %seen_ref.15, bf16[512,2304]{1,0:T(8,128)(2,1)} %fusion.132.q_ref.k_ref.v_ref, bf16[512,2304]{1,0:T(8,128)(2,1)} %fusion.132.q_ref.k_ref.v_ref, bf16[512,2304]{1,0:T(8,128)(2,1)} %fusion.132.q_ref.k_ref.v_ref, ...), custom_call_target="tpu_custom_call" | custom-call | flops 1207959552 | bytes 4718592 | tf_op jit(solution)/shard_map/attend/pallas_call | solution.py:80
  218.9 9.4 collective-permute-done.69.refs_3_
  228.9 11.7 %collective-permute-done.40.refs_1_ = bf16[4,96,768]{2,1,0:T(8,128)(2,1)} collective-permute-done((bf16[4,96,768]{2,1,0:T(8,128)(2,1)}, bf16[4,96,768]{2,1,0:T(8,128)(2,1)}, u32[]{:S(2)}, u32[]{:S(2)}) %collective-permute-start.40) | collective-permute-done | bytes 589856 | tf_op jit(solution)/shard_map/ppermute | solution.py:380
  258.5 10.0 collective-permute-done.42.refs_3_
  273.8 10.2 fusion.92
  303.8 9.1 collective-permute-done.87.refs_1_
  315.1 9.4 collective-permute-done.79.refs_3_
  363.0 16.5 %attend.5 = (bf16[512,768]{1,0:T(8,128)(2,1)}, f32[12,2,256]{2,1,0:T(2,128)}) custom-call(s32[2]{0:T(128)} %seen_ref.15, bf16[512,2304]{1,0:T(8,128)(2,1)} %fusion.133.q_ref.k_ref.v_ref, bf16[512,2304]{1,0:T(8,128)(2,1)} %fusion.133.q_ref.k_ref.v_ref, bf16[512,2304]{1,0:T(8,128)(2,1)} %fusion.133.q_ref.k_ref.v_ref, ...), custom_call_target="tpu_custom_call" | custom-call | flops 1207959552 | bytes 4718592 | tf_op jit(solution)/shard_map/attend/pallas_call | solution.py:80
  396.6 16.4 %attend.6 = (bf16[512,768]{1,0:T(8,128)(2,1)}, f32[12,2,256]{2,1,0:T(2,128)}) custom-call(s32[2]{0:T(128)} %seen_ref.15, bf16[512,2304]{1,0:T(8,128)(2,1)} %fusion.134.q_ref.k_ref.v_ref, bf16[512,2304]{1,0:T(8,128)(2,1)} %fusion.134.q_ref.k_ref.v_ref, bf16[512,2304]{1,0:T(8,128)(2,1)} %fusion.134.q_ref.k_ref.v_ref, ...), custom_call_target="tpu_custom_call" | custom-call | flops 1207959552 | bytes 4718592 | tf_op jit(solution)/shard_map/attend/pallas_call | solution.py:80
  431.5 16.4 %attend.7 = (bf16[512,768]{1,0:T(8,128)(2,1)}, f32[12,2,256]{2,1,0:T(2,128)}) custom-call(s32[2]{0:T(128)} %seen_ref.15, bf16[512,2304]{1,0:T(8,128)(2,1)} %fusion.135.q_ref.k_ref.v_ref, bf16[512,2304]{1,0:T(8,128)(2,1)} %fusion.135.q_ref.k_ref.v_ref, bf16[512,2304]{1,0:T(8,128)(2,1)} %fusion.135.q_ref.k_ref.v_ref, ...), custom_call_target="tpu_custom_call" | custom-call | flops 1207959552 | bytes 4718592 | tf_op jit(solution)/shard_map/attend/pallas_call | solution.py:80
  474.2 23.9 %attend_back.4 = (bf16[512,2304]{1,0:T(8,128)(2,1)}, f32[512,1536]{1,0:T(8,128)}) custom-call(s32[2]{0:T(128)} %seen_ref.15, bf16[512,2304]{1,0:T(8,128)(2,1)} %fusion.135.q_ref.k_ref.v_ref, bf16[512,2304]{1,0:T(8,128)(2,1)} %fusion.135.q_ref.k_ref.v_ref, bf16[512,2304]{1,0:T(8,128)(2,1)} %fusion.135.q_ref.k_ref.v_ref, ...), custom_call_target="tpu_custom_call" | custom-call | flops 3019898880 | bytes 14155776 | tf_op jit(solution)/shard_map/attend_back/pallas_call | solution.py:187
  505.6 9.6 fusion.334
  522.9 24.0 %attend_back.5 = (bf16[512,2304]{1,0:T(8,128)(2,1)}, f32[512,1536]{1,0:T(8,128)}) custom-call(s32[2]{0:T(128)} %seen_ref.15, bf16[512,2304]{1,0:T(8,128)(2,1)} %fusion.134.q_ref.k_ref.v_ref, bf16[512,2304]{1,0:T(8,128)(2,1)} %fusion.134.q_ref.k_ref.v_ref, bf16[512,2304]{1,0:T(8,128)(2,1)} %fusion.134.q_ref.k_ref.v_ref, ...), custom_call_target="tpu_custom_call" | custom-call | flops 3019898880 | bytes 14155776 | tf_op jit(solution)/shard_map/attend_back/pallas_call | solution.py:187
  562.4 9.4 fusion.332
  587.3 23.8 %attend_back.6 = (bf16[512,2304]{1,0:T(8,128)(2,1)}, f32[512,1536]{1,0:T(8,128)}) custom-call(s32[2]{0:T(128)} %seen_ref.15, bf16[512,2304]{1,0:T(8,128)(2,1)} %fusion.133.q_ref.k_ref.v_ref, bf16[512,2304]{1,0:T(8,128)(2,1)} %fusion.133.q_ref.k_ref.v_ref, bf16[512,2304]{1,0:T(8,128)(2,1)} %fusion.133.q_ref.k_ref.v_ref, ...), custom_call_target="tpu_custom_call" | custom-call | flops 3019898880 | bytes 14155776 | tf_op jit(solution)/shard_map/attend_back/pallas_call | solution.py:187
  627.2 9.8 fusion.118
  641.1 8.6 fusion.124
  705.4 9.8 fusion.335
  722.4 24.9 %attend_back.7 = (bf16[512,2304]{1,0:T(8,128)(2,1)}, f32[512,1536]{1,0:T(8,128)}) custom-call(s32[2]{0:T(128)} %seen_ref.15, bf16[512,2304]{1,0:T(8,128)(2,1)} %fusion.132.q_ref.k_ref.v_ref, bf16[512,2304]{1,0:T(8,128)(2,1)} %fusion.132.q_ref.k_ref.v_ref, bf16[512,2304]{1,0:T(8,128)(2,1)} %fusion.132.q_ref.k_ref.v_ref, ...), custom_call_target="tpu_custom_call" | custom-call | flops 3019898880 | bytes 14155776 | tf_op jit(solution)/shard_map/attend_back/pallas_call | solution.py:187
  798.2 8.2 fusion.121
  848.2 20.3 %reduce-scatter.9.cloned.1.call-done = bf16[1,24,9344]{2,1,0:T(8,128)(2,1)} async-done(((bf16[32,24,9344]{2,1,0:T(8,128)(2,1)}), bf16[1,24,9344]{2,1,0:T(8,128)(2,1)}) %reduce-scatter.9.cloned.1.call-update) | async-done | bytes 448528
  869.8 163.1 %reduce-scatter.7.cloned.1.call-done = bf16[1,24,9344]{2,1,0:T(8,128)(2,1)} async-done(((bf16[32,24,9344]{2,1,0:T(8,128)(2,1)}), bf16[1,24,9344]{2,1,0:T(8,128)(2,1)}) %reduce-scatter.7.cloned.1.call-update) | async-done | bytes 448528
  (1110 shorter events, 553.6 us)
Async XLA Ops:
  7.2 861.2 %reduce-scatter.9.cloned.1.call-start = ((), (), s32[]{:S(2)}) async-start(), calls=%async_computation.3 | async-start | bytes 14800896
  76.4 27.4 %collective-permute-start.38 = (bf16[1,96,768]{2,1,0:T(8,128)(2,1)S(1)}, bf16[1,96,768]{2,1,0:T(8,128)(2,1)S(1)}, u32[]{:S(2)}, u32[]{:S(2)}) collective-permute-start(bf16[1,96,768]{2,1,0:T(8,128)(2,1)S(1)} %get-tuple-element.205), channel_id=1, source_target_pairs={{0,4},{1,5},{2,6},{3,7},{4,0},{5,1},{6,2},{7,3},{8,12},{9,13},{10,... | collective-permute-start | bytes 442376 | tf_op jit(solution)/shard_map/ppermute | solution.py:380
  79.8 26.4 %collective-permute-start.39 = (bf16[1,96,768]{2,1,0:T(8,128)(2,1)S(1)}, bf16[1,96,768]{2,1,0:T(8,128)(2,1)S(1)}, u32[]{:S(2)}, u32[]{:S(2)}) collective-permute-start(bf16[1,96,768]{2,1,0:T(8,128)(2,1)S(1)} %get-tuple-element.205), channel_id=1, source_target_pairs={{0,6},{1,7},{2,4},{3,5},{4,2},{5,3},{6,0},{7,1},{8,14},{9,15},{10,... | collective-permute-start | bytes 442376 | tf_op jit(solution)/shard_map/ppermute | solution.py:380
  147.3 66.2 %collective-permute-start.67 = (bf16[4,24,2304]{2,1,0:T(8,128)(2,1)}, bf16[4,24,2304]{2,1,0:T(8,128)(2,1)}, u32[]{:S(2)}, u32[]{:S(2)}) collective-permute-start(bf16[4,24,2304]{2,1,0:T(8,128)(2,1)} %pad_maximum_fusion.11.refs_0_), channel_id=1, source_target_pairs={{0,16},{1,17},{2,18},{3,19},{4,20},{5,21},{6,22},{7,23},{8,24},{9,... | collective-permute-start | bytes 1327112 | tf_op jit(solution)/shard_map/ppermute | solution.py:380
  171.2 43.8 %collective-permute-start.68 = (bf16[4,24,2304]{2,1,0:T(8,128)(2,1)}, bf16[4,24,2304]{2,1,0:T(8,128)(2,1)}, u32[]{:S(2)}, u32[]{:S(2)}) collective-permute-start(bf16[4,24,2304]{2,1,0:T(8,128)(2,1)} %pad_maximum_fusion.11.refs_0_), channel_id=1, source_target_pairs={{0,1},{1,0},{2,3},{3,2},{4,5},{5,4},{6,7},{7,6},{8,9},{9,8},{10,11... | collective-permute-start | bytes 1327112 | tf_op jit(solution)/shard_map/ppermute | solution.py:380
  172.3 44.6 %collective-permute-start.70 = (bf16[4,24,2304]{2,1,0:T(8,128)(2,1)}, bf16[4,24,2304]{2,1,0:T(8,128)(2,1)}, u32[]{:S(2)}, u32[]{:S(2)}) collective-permute-start(bf16[4,24,2304]{2,1,0:T(8,128)(2,1)} %pad_maximum_fusion.11.refs_0_), channel_id=1, source_target_pairs={{0,8},{1,9},{2,10},{3,11},{4,12},{5,13},{6,14},{7,15},{8,0},{9,1},... | collective-permute-start | bytes 1327112 | tf_op jit(solution)/shard_map/ppermute | solution.py:380
  172.5 45.3 %collective-permute-start.30 = (bf16[4,24,3072]{2,1,0:T(8,128)(2,1)}, bf16[4,24,3072]{2,1,0:T(8,128)(2,1)}, u32[]{:S(2)}, u32[]{:S(2)}) collective-permute-start(bf16[4,24,3072]{2,1,0:T(8,128)(2,1)} %pad_maximum_fusion.4.refs_0_), channel_id=1, source_target_pairs={{0,1},{1,0},{2,3},{3,2},{4,5},{5,4},{6,7},{7,6},{8,9},{9,8},{10,11... | collective-permute-start | bytes 1769480 | tf_op jit(solution)/shard_map/ppermute | solution.py:380
  173.5 44.9 %collective-permute-start.31 = (bf16[4,24,3072]{2,1,0:T(8,128)(2,1)}, bf16[4,24,3072]{2,1,0:T(8,128)(2,1)}, u32[]{:S(2)}, u32[]{:S(2)}) collective-permute-start(bf16[4,24,3072]{2,1,0:T(8,128)(2,1)} %pad_maximum_fusion.4.refs_0_), channel_id=1, source_target_pairs={{0,16},{1,17},{2,18},{3,19},{4,20},{5,21},{6,22},{7,23},{8,24},{9,... | collective-permute-start | bytes 1769480 | tf_op jit(solution)/shard_map/ppermute | solution.py:380
  241.7 26.8 %collective-permute-start.42 = (bf16[4,96,768]{2,1,0:T(8,128)(2,1)}, bf16[4,96,768]{2,1,0:T(8,128)(2,1)}, u32[]{:S(2)}, u32[]{:S(2)}) collective-permute-start(bf16[4,96,768]{2,1,0:T(8,128)(2,1)} %collective-permute-done.40.refs_1_), channel_id=1, source_target_pairs={{0,16},{1,17},{2,18},{3,19},{4,20},{5,21},{6,22},{7,23},{8,24},{9,... | collective-permute-start | bytes 1769480 | tf_op jit(solution)/shard_map/ppermute | solution.py:380
  257.1 26.9 %collective-permute-start.43 = (bf16[4,96,768]{2,1,0:T(8,128)(2,1)}, bf16[4,96,768]{2,1,0:T(8,128)(2,1)}, u32[]{:S(2)}, u32[]{:S(2)}) collective-permute-start(bf16[4,96,768]{2,1,0:T(8,128)(2,1)} %pad_maximum_fusion.5.refs_0_), channel_id=1, source_target_pairs={{0,8},{1,9},{2,10},{3,11},{4,12},{5,13},{6,14},{7,15},{8,0},{9,1},... | collective-permute-start | bytes 1769480 | tf_op jit(solution)/shard_map/ppermute | solution.py:380
  257.1 45.8 %collective-permute-start.77 = (bf16[4,24,3072]{2,1,0:T(8,128)(2,1)S(1)}, bf16[4,24,3072]{2,1,0:T(8,128)(2,1)}, u32[]{:S(2)}, u32[]{:S(2)}) collective-permute-start(bf16[4,24,3072]{2,1,0:T(8,128)(2,1)S(1)} %copy-done.48), channel_id=1, source_target_pairs={{0,1},{1,0},{2,3},{3,2},{4,5},{5,4},{6,7},{7,6},{8,9},{9,8},{10,11... | collective-permute-start | bytes 1769480 | tf_op jit(solution)/shard_map/ppermute | solution.py:380
  284.5 28.4 %collective-permute-start.87 = (bf16[4,96,768]{2,1,0:T(8,128)(2,1)S(1)}, bf16[4,96,768]{2,1,0:T(8,128)(2,1)}, u32[]{:S(2)}, u32[]{:S(2)}) collective-permute-start(bf16[4,96,768]{2,1,0:T(8,128)(2,1)S(1)} %copy-done.49), channel_id=1, source_target_pairs={{0,16},{1,17},{2,18},{3,19},{4,20},{5,21},{6,22},{7,23},{8,24},{9,... | collective-permute-start | bytes 1769480 | tf_op jit(solution)/shard_map/ppermute | solution.py:380
  286.1 28.2 %collective-permute-start.88 = (bf16[4,96,768]{2,1,0:T(8,128)(2,1)S(1)}, bf16[4,96,768]{2,1,0:T(8,128)(2,1)}, u32[]{:S(2)}, u32[]{:S(2)}) collective-permute-start(bf16[4,96,768]{2,1,0:T(8,128)(2,1)S(1)} %copy-done.49), channel_id=1, source_target_pairs={{0,1},{1,0},{2,3},{3,2},{4,5},{5,4},{6,7},{7,6},{8,9},{9,8},{10,11... | collective-permute-start | bytes 1769480 | tf_op jit(solution)/shard_map/ppermute | solution.py:380
  650.5 32.2 %collective-permute-start.100 = (bf16[64,768]{1,0:T(8,128)(2,1)}, bf16[64,768]{1,0:T(8,128)(2,1)S(1)}, u32[]{:S(2)}, u32[]{:S(2)}) collective-permute-start(bf16[64,768]{1,0:T(8,128)(2,1)} %get-tuple-element.182), channel_id=1, source_target_pairs={{0,7},{1,6},{2,5},{3,4},{4,3},{5,2},{6,1},{7,0},{8,15},{9,14},{10,... | collective-permute-start | bytes 294920 | tf_op jit(solution)/shard_map/ppermute | solution.py:380
  652.8 33.6 %collective-permute-start.94 = (bf16[64,768]{1,0:T(8,128)(2,1)}, bf16[64,768]{1,0:T(8,128)(2,1)}, u32[]{:S(2)}, u32[]{:S(2)}) collective-permute-start(bf16[64,768]{1,0:T(8,128)(2,1)} %get-tuple-element.181), channel_id=1, source_target_pairs={{0,1},{1,0},{2,3},{3,2},{4,5},{5,4},{6,7},{7,6},{8,9},{9,8},{10,11... | collective-permute-start | bytes 294920 | tf_op jit(solution)/shard_map/ppermute | solution.py:380
  654.2 35.8 %collective-permute-start.95 = (bf16[64,768]{1,0:T(8,128)(2,1)}, bf16[64,768]{1,0:T(8,128)(2,1)}, u32[]{:S(2)}, u32[]{:S(2)}) collective-permute-start(bf16[64,768]{1,0:T(8,128)(2,1)} %get-tuple-element.187), channel_id=1, source_target_pairs={{0,2},{1,3},{2,0},{3,1},{4,6},{5,7},{6,4},{7,5},{8,10},{9,11},{10,... | collective-permute-start | bytes 294920 | tf_op jit(solution)/shard_map/ppermute | solution.py:380
  654.2 35.8 %collective-permute-start.96 = (bf16[64,768]{1,0:T(8,128)(2,1)}, bf16[64,768]{1,0:T(8,128)(2,1)}, u32[]{:S(2)}, u32[]{:S(2)}) collective-permute-start(bf16[64,768]{1,0:T(8,128)(2,1)} %get-tuple-element.186), channel_id=1, source_target_pairs={{0,3},{1,2},{2,1},{3,0},{4,7},{5,6},{6,5},{7,4},{8,11},{9,10},{10,... | collective-permute-start | bytes 294920 | tf_op jit(solution)/shard_map/ppermute | solution.py:380
  656.3 33.6 %collective-permute-start.97 = (bf16[64,768]{1,0:T(8,128)(2,1)}, bf16[64,768]{1,0:T(8,128)(2,1)}, u32[]{:S(2)}, u32[]{:S(2)}) collective-permute-start(bf16[64,768]{1,0:T(8,128)(2,1)} %get-tuple-element.185), channel_id=1, source_target_pairs={{0,4},{1,5},{2,6},{3,7},{4,0},{5,1},{6,2},{7,3},{8,12},{9,13},{10,... | collective-permute-start | bytes 294920 | tf_op jit(solution)/shard_map/ppermute | solution.py:380
  699.2 333.8 %reduce-scatter.7.cloned.1.call-start = ((), (), s32[]{:S(2)}) async-start(), calls=%async_computation.2 | async-start | bytes 14800896
  776.8 47.0 %collective-permute-start.101 = (bf16[64,768]{1,0:T(8,128)(2,1)S(1)}, bf16[64,768]{1,0:T(8,128)(2,1)S(1)}, u32[]{:S(2)}, u32[]{:S(2)}) collective-permute-start(bf16[64,768]{1,0:T(8,128)(2,1)S(1)} %get-tuple-element.174), channel_id=1, source_target_pairs={{0,1},{1,0},{2,3},{3,2},{4,5},{5,4},{6,7},{7,6},{8,9},{9,8},{10,11... | collective-permute-start | bytes 294920 | tf_op jit(solution)/shard_map/ppermute | solution.py:380
  778.5 47.0 %collective-permute-start.102 = (bf16[64,768]{1,0:T(8,128)(2,1)S(1)}, bf16[64,768]{1,0:T(8,128)(2,1)S(1)}, u32[]{:S(2)}, u32[]{:S(2)}) collective-permute-start(bf16[64,768]{1,0:T(8,128)(2,1)S(1)} %get-tuple-element.180), channel_id=1, source_target_pairs={{0,2},{1,3},{2,0},{3,1},{4,6},{5,7},{6,4},{7,5},{8,10},{9,11},{10,... | collective-permute-start | bytes 294920 | tf_op jit(solution)/shard_map/ppermute | solution.py:380
  778.8 49.8 %collective-permute-start.103 = (bf16[64,768]{1,0:T(8,128)(2,1)S(1)}, bf16[64,768]{1,0:T(8,128)(2,1)S(1)}, u32[]{:S(2)}, u32[]{:S(2)}) collective-permute-start(bf16[64,768]{1,0:T(8,128)(2,1)S(1)} %get-tuple-element.179), channel_id=1, source_target_pairs={{0,3},{1,2},{2,1},{3,0},{4,7},{5,6},{6,5},{7,4},{8,11},{9,10},{10,... | collective-permute-start | bytes 294920 | tf_op jit(solution)/shard_map/ppermute | solution.py:380
  780.4 48.2 %collective-permute-start.104 = (bf16[64,768]{1,0:T(8,128)(2,1)S(1)}, bf16[64,768]{1,0:T(8,128)(2,1)S(1)}, u32[]{:S(2)}, u32[]{:S(2)}) collective-permute-start(bf16[64,768]{1,0:T(8,128)(2,1)S(1)} %get-tuple-element.178), channel_id=1, source_target_pairs={{0,4},{1,5},{2,6},{3,7},{4,0},{5,1},{6,2},{7,3},{8,12},{9,13},{10,... | collective-permute-start | bytes 294920 | tf_op jit(solution)/shard_map/ppermute | solution.py:380
  782.9 45.6 %collective-permute-start.105 = (bf16[64,768]{1,0:T(8,128)(2,1)S(1)}, bf16[64,768]{1,0:T(8,128)(2,1)S(1)}, u32[]{:S(2)}, u32[]{:S(2)}) collective-permute-start(bf16[64,768]{1,0:T(8,128)(2,1)S(1)} %get-tuple-element.177), channel_id=1, source_target_pairs={{0,5},{1,4},{2,7},{3,6},{4,1},{5,0},{6,3},{7,2},{8,13},{9,12},{10,... | collective-permute-start | bytes 294920 | tf_op jit(solution)/shard_map/ppermute | solution.py:380
  (363 other events, 3795.1 us)
Sparse Core Ops, SparseCore 0:
  699.3 169.0 reduce-scatter.8
  874.6 158.2 reduce-scatter.6

commit v3 on v1

--- a/solution.py
+++ b/solution.py
@@ -281,8 +281,11 @@
 
 
 def prompt_back_kernel(
-    place_ref, q_ref, k_ref, v_ref, o_ref, lse_ref, do_ref, carry_k, carry_v, dq_ref, dk_ref, dv_ref, *, width
+    place_ref, q_ref, k_ref, v_ref, o_ref, lse_ref, do_ref, carry_k, carry_v, dqkv_ref, *, width, pairs
 ):
+    rows, lanes = q_ref.shape
+    first = pl.multiple_of(pl.program_id(0) * lanes, lanes)
+    columns = [pl.ds(first + number * pairs * lanes, lanes) for number in range(3)]
     queries, scores = prompt_scores(place_ref, q_ref, k_ref, width)
     grads = stacked_heads(do_ref[...], width)
     output = o_ref[...]
@@ -290,10 +293,12 @@
     delta = jnp.sum(product.T, 0, keepdims=True)
     probs = jnp.exp(scores - lse_ref[0])
     ds = (probs * (nt(v_ref[...], grads) - delta)).astype(bf16)
-    dv_ref[...] = carry_v[...] + nn(probs.astype(bf16), grads)
-    dk_ref[...] = carry_k[...] + nn(ds, queries)
+    dqkv_ref[:, columns[2]] = (carry_v[...] + nn(probs.astype(bf16), grads)).astype(bf16)
+    dqkv_ref[:, columns[1]] = (carry_k[...] + nn(ds, queries)).astype(bf16)
     turned = nn(k_ref[...].T, ds) * score_scale
-    dq_ref[...] = unstacked(turned.T, width).astype(bf16)
+    own = pl.ds(pl.multiple_of(place_ref[0] * rows, rows), rows)
+    dqkv_ref[:, columns[0]] = jnp.zeros((dqkv_ref.shape[0], lanes), bf16)
+    dqkv_ref[own, columns[0]] = unstacked(turned.T, width).astype(bf16)
 
 
 def prompt_back(place, pqkv, o, lse, do, carry):
@@ -303,17 +308,16 @@
     own = pl.BlockSpec((rows, lanes), lambda p, s: (0, p))
     keys = pl.BlockSpec((plen, lanes), lambda p, s: (0, p))
     values = pl.BlockSpec((plen, lanes), lambda p, s: (0, p + pairs))
-    total = jax.ShapeDtypeStruct((plen, width), f32)
-    dq, dk, dv = pl.pallas_call(
-        functools.partial(prompt_back_kernel, width=head_width),
+    return pl.pallas_call(
+        functools.partial(prompt_back_kernel, width=head_width, pairs=pairs),
         grid_spec=pltpu.PrefetchScalarGridSpec(
             num_scalar_prefetch=1,
             grid=(pairs,),
             in_specs=prompt_specs(rows, plen, pairs, lanes)
             + [own, pl.BlockSpec((1, 1, 2 * rows), lambda p, s: (p, 0, 0)), own, keys, values],
-            out_specs=[own, keys, keys],
+            out_specs=pl.BlockSpec((plen, 3 * width), lambda p, s: (0, 0)),
         ),
-        out_shape=[jax.ShapeDtypeStruct((rows, width), bf16), total, total],
+        out_shape=jax.ShapeDtypeStruct((plen, 3 * width), bf16),
         cost_estimate=pl.CostEstimate(
             flops=10 * rows * plen * width,
             bytes_accessed=24 * plen * width,
@@ -321,7 +325,6 @@
         ),
         name="prompt_back",
     )(place, pqkv, pqkv, pqkv, o, lse, do, carry, carry)
-    return dq, dk, dv
 
 
 def normalised(rows):
@@ -374,6 +377,166 @@
     da = grad_after.astype(bf16)
     do = nt(da, w["out"]).astype(bf16)
     return grad_after, do, (dz, du, da), (gain, shift)
+
+
+def swap(value, code, axes, total):
+    return lax.ppermute(value, axes, [(i, i ^ code) for i in range(total)])
+
+
+def lay_kernel(place_ref, *refs, codes, widths):
+    outs, sems = refs[len(codes) : -1], refs[-1]
+    copies = []
+    for ref, group in zip(refs, codes):
+        for number, code in enumerate(group):
+            first = 0
+            for out_ref, size in zip(outs, widths):
+                source = ref.at[number, :, pl.ds(first, size)] if len(widths) > 1 else ref.at[number]
+                copies.append(
+                    pltpu.make_async_copy(
+                        source, out_ref.at[place_ref[0] ^ code], sems.at[len(copies)]
+                    )
+                )
+                copies[-1].start()
+                first += size
+    for copy in copies:
+        copy.wait()
+
+
+def lay_out(place, pieces, codes, widths, name):
+    total, rows = sum(len(group) for group in codes), pieces[0].shape[1]
+    kind = pieces[0].dtype
+    return pl.pallas_call(
+        functools.partial(lay_kernel, codes=codes, widths=widths),
+        in_specs=[pl.BlockSpec(memory_space=pltpu.SMEM)]
+        + [pl.BlockSpec(memory_space=pl.ANY)] * len(pieces),
+        out_specs=[pl.BlockSpec((total, rows, size), lambda: (0, 0, 0)) for size in widths],
+        out_shape=[jax.ShapeDtypeStruct((total, rows, size), kind) for size in widths],
+        scratch_shapes=[pltpu.SemaphoreType.DMA((total * len(widths),))],
+        cost_estimate=pl.CostEstimate(
+            flops=0, bytes_accessed=4 * total * rows * sum(widths), transcendentals=0
+        ),
+        name=name,
+    )(place, *pieces)
+
+
+def spread_z(parts):
+    return [[part[None]] + [swap(part[None], code, ALL, 32) for code in (2, 4, 6)] for part in parts]
+
+
+def spread_rest(groups, starts, first, second):
+    pieces, codes = [], []
+    for base, start, one, two in zip(groups, starts, first, second):
+        four = [base, swap(base, one, ALL, 32)]
+        four += [swap(piece, two, ALL, 32) for piece in four]
+        offsets = [0, one, two, one | two]
+        pieces += four + [swap(piece, 8, ALL, 32) for piece in four]
+        codes += [
+            tuple(code | offset | core for code in start) for core in (0, 8) for offset in offsets
+        ]
+    return pieces, tuple(codes)
+
+
+def gather_rows(own, place, tree):
+    if not tree:
+        return lax.all_gather(own, "seq", axis=0, tiled=True)
+    pieces = [own[None]] + [swap(own[None], code, "seq", 8) for code in range(1, 8)]
+    return lay_rows(pieces, place)
+
+
+def lay_rows(pieces, place):
+    codes = tuple((code,) for code in range(8))
+    rows = lay_out(place, pieces, codes, (pieces[0].shape[2],), "lay_rows")[0]
+    return rows.reshape(-1, rows.shape[2])
+
+
+def gather_plain(head, fc, proj, widths):
+    joined = lax.all_gather(jnp.concatenate([head, fc], 1), ALL, axis=0)
+    parts, first = [], 0
+    for size in widths + (fc.shape[1],):
+        parts.append(joined[:, :, first : first + size])
+        first += size
+    return parts + [lax.all_gather(proj, ALL, axis=0)]
+
+
+def gather_weights(heads, mlps, x_own, flat, place, tree, widths):
+    if not tree:
+        gathered = [gather_plain(head, fc, proj, widths) for head, (fc, proj) in zip(heads, mlps)]
+        return gathered, gather_rows(x_own, place, tree)
+    joined = lax.all_gather(heads[0], ALL, axis=0)
+    fc, proj = mlps[0]
+    rows = [x_own[None]] + [swap(x_own[None], code, "seq", 8) for code in range(1, 8)]
+    fc, proj, rows[6] = lax.optimization_barrier((fc, proj, rows[6]))
+    parts, first = [], 0
+    for size in widths:
+        parts.append(joined[:, :, first : first + size])
+        first += size
+    bases = [jnp.concatenate(group, 0) for group in spread_z([fc, proj])]
+    gathered = [None]
+    for head, (fc, proj) in zip(heads[1:], mlps[1:]):
+        head, fc, proj, bases[0] = lax.optimization_barrier((head, fc, proj, bases[0]))
+        gathered.append(gather_plain(head, fc, proj, widths))
+    gathered[0] = parts + lay_mlp(bases, flat)
+    return gathered, lay_rows(rows, place)
+
+
+def lay_mlp(groups, flat):
+    result = []
+    for base, first, second in zip(groups, (16, 1), (1, 16)):
+        pieces, codes = spread_rest([base], [(0, 2, 4, 6)], [first], [second])
+        result += lay_out(flat, pieces, codes, (base.shape[2],), "lay_mlp")
+    return result
+
+
+def reduce_stages(block, x_first):
+    grp, seq = lax.axis_index("grp"), lax.axis_index("seq")
+    z = seq // 2
+    terms = [block.reshape((2, 2, 4, 2) + block.shape[1:])]
+
+    def picked(axis, index):
+        parts = [lax.dynamic_slice_in_dim(term, index, 1, axis) for term in terms]
+        return parts, sum(part.astype(f32) for part in parts)
+
+    core, over_x, over_y = (1, 8, grp % 2), (3, 1, seq % 2), (0, 16, grp // 2)
+    for axis, code, mine in (core, over_x, over_y) if x_first else (core, over_y, over_x):
+        (leaving,) = yield (picked(axis, 1 - mine)[1].astype(bf16),)
+        terms = picked(axis, mine)[0] + [swap(leaving, code, ALL, 32)]
+    leaving = yield tuple(picked(2, z ^ step)[1].astype(bf16) for step in (1, 2, 3))
+    total = picked(2, z)[1]
+    for step, part in zip((1, 2, 3), leaving):
+        total = total + swap(part, 2 * step, ALL, 32).astype(f32)
+    yield total.reshape(block.shape[1:])
+
+
+def reduce_blocks(block, x_first, tree):
+    if not tree:
+        return lax.psum_scatter(block, ALL, scatter_dimension=0, tiled=True).astype(f32)[0]
+    stages = reduce_stages(block, x_first)
+    leaving = next(stages)
+    for stage in range(4):
+        leaving = stages.send(leaving)
+    return leaving
+
+
+class Gate:
+    def __init__(self, blocks):
+        self.stages = [reduce_stages(block, x_first) for block, x_first in blocks]
+        self.leaving = [next(stage) for stage in self.stages]
+
+    def hold(self, *values):
+        values, self.leaving = lax.optimization_barrier((values, self.leaving))
+        self.leaving = [stage.send(part) for stage, part in zip(self.stages, self.leaving)]
+        return values
+
+
+def scatter_rows(block, place, tree):
+    if not tree:
+        return lax.psum_scatter(block, "seq", scatter_dimension=0, tiled=True).astype(f32)
+    rows = block.shape[0] // 8
+    total = lax.dynamic_slice_in_dim(block, place * rows, rows, 0).astype(f32)
+    for code in range(1, 8):
+        piece = lax.dynamic_slice_in_dim(block, (place ^ code) * rows, rows, 0)
+        total = total + swap(piece, code, "seq", 8).astype(f32)
+    return total
 
 
 SMALL = (
@@ -430,21 +593,35 @@
     )
     out_rows = w_out.shape[1]
     sizes = [vectors[name].shape[1] for name in SMALL]
-    x_all = lax.all_gather(x_prompt, "seq", axis=0, tiled=True)
-
-    weights = []
+    tree = (
+        lax.axis_size("grp") == 4 and lax.axis_size("seq") == 8 and out_rows % 8 == 0 and prompt_dev % 16 == 0
+    )
+    flat_ref = (lax.axis_index("grp") * lax.axis_size("seq") + place).astype(jnp.int32).reshape(1)
+
+    small_lanes = -(-sum(sizes) // (128 * out_rows)) * 128
+    heads = []
     for layer in range(LAYERS):
         flat = jnp.concatenate([vectors[name][layer] for name in SMALL])
-        extra = jnp.pad(flat, (0, 8 * width - flat.shape[0])).reshape(8, width)
-        pack = lax.all_gather(jnp.concatenate([w_out[layer], extra], 0), ALL, axis=0)
-        w = dict(out=pack[:, :out_rows].reshape(width, width))
-        share = pack[:, out_rows:].reshape(devices, 8 * width)
+        extra = jnp.pad(flat, (0, out_rows * small_lanes - flat.shape[0])).reshape(out_rows, small_lanes)
+        heads.append(jnp.concatenate([w_qkv[layer], w_out[layer], extra], 1))
+    gathered, x_all = gather_weights(
+        heads,
+        [(w_fc[layer], w_proj[layer]) for layer in range(LAYERS)],
+        x_prompt,
+        flat_ref,
+        place_ref,
+        tree,
+        (3 * width, width, small_lanes),
+    )
+    weights = []
+    for parts in gathered:
+        names = ("qkv", "out", "small", "fc", "proj")
+        w = {name: part.reshape(-1, part.shape[2]) for name, part in zip(names, parts)}
+        share = w.pop("small").reshape(devices, -1)
         first = 0
         for name, size in zip(SMALL, sizes):
             w[name] = share[:, first : first + size].reshape(devices * size).astype(f32)
             first += size
-        for name, part in (("qkv", w_qkv), ("fc", w_fc), ("proj", w_proj)):
-            w[name] = lax.all_gather(part[layer], ALL, axis=0, tiled=True)
         w["qkv_bias"] = jnp.concatenate([w["q_bias"], jnp.zeros((width,), f32), w["v_bias"]])
         weights.append(w)
 
@@ -458,9 +635,7 @@
         if layer == 0:
             all_normed = norm(x_all.astype(f32), w["ln1_gain"], w["ln1_bias"])
         else:
-            all_normed = lax.all_gather(
-                norm(prompt_rows, w["ln1_gain"], w["ln1_bias"]), "seq", axis=0, tiled=True
-            )
+            all_normed = gather_rows(norm(prompt_rows, w["ln1_gain"], w["ln1_bias"]), place_ref, tree)
         pqkv = project(w, all_normed)
         mixed, lse = prompt_attend(place_ref, pqkv, prompt_dev)
         result, kept = block_output(w, prompt_rows, mixed)
@@ -490,62 +665,82 @@
     current, language_states = pass_forward(jnp.where(marked, shifted, inputs).reshape(rows, width))
     cont_out = current.reshape(count, length, width).astype(bf16)
 
-    pieces = [[] for layer in range(LAYERS)]
-    small = [[] for layer in range(LAYERS)]
     carries = [jnp.zeros((plen, 2 * width), f32) for layer in range(LAYERS)]
 
-    def layer_backward(layer, state, grad):
+    def attention_backward(layer, state, grad_after, do):
         w = weights[layer]
         before, normed, qkv, mixed, lse, kept = state
-        grad_after, do, (dz, du, da), ln2 = output_backward(w, kept, grad)
         dqkv, carries[layer] = attend_back(
             offsets, qkv, prompt_states[layer][2], mixed, lse, do, carries[layer]
         )
         grad_in, gain, shift = norm_back(before, w["ln1_gain"], nt(dqkv, w["qkv"]))
-        pieces[layer].append((normed, dqkv, mixed, da, kept[1], du, kept[3], dz))
-        small[layer].append((gain, shift) + ln2)
-        return grad_after + grad_in
+        return grad_after + grad_in, dqkv, (gain, shift)
+
+    def blocks(left, right):
+        return tn(left, right).astype(bf16).reshape(devices, -1, right.shape[1])
 
     grad = dy_cont.reshape(rows, width)
+    language = [None] * LAYERS
     for layer in reversed(range(LAYERS)):
-        grad = layer_backward(layer, language_states[layer], grad)
+        state = language_states[layer]
+        grad_after, do, outer, ln2 = output_backward(weights[layer], state[5], grad)
+        grad, dqkv, ln1 = attention_backward(layer, state, grad_after, do)
+        language[layer] = (state, outer, dqkv, ln1 + ln2)
     grad_mixed_in = grad.reshape(count, length, width)
     grad = jnp.concatenate(
         [jnp.where(marked, grad_mixed_in, 0.0)[:, 1:], jnp.zeros((count, 1, width), f32)], 1
     ).reshape(rows, width)
     prompt_grad = dy_prompt
-    shares = []
+    shares, extras = [], []
     for layer in reversed(range(LAYERS)):
         w = weights[layer]
-        grad = layer_backward(layer, latent_states[layer], grad)
+        state = latent_states[layer]
+        grad_after, do, outer, ln2 = output_backward(w, state[5], grad)
         before, normed, pqkv, mixed, lse, kept = prompt_states[layer]
-        grad_after, do, (dz, du, da), ln2 = output_backward(w, kept, prompt_grad)
-        dq, dk, dv = prompt_back(place_ref, pqkv, mixed, lse, do, carries[layer])
-        dq_all = lax.dynamic_update_slice(
-            jnp.zeros((plen, width), bf16), dq, (place * prompt_dev, 0)
-        )
-        dqkv = jnp.concatenate([dq_all, dk.astype(bf16), dv.astype(bf16)], 1)
-        grad_normed = lax.psum_scatter(
-            nt(dqkv, w["qkv"]).astype(bf16), "seq", scatter_dimension=0, tiled=True
-        ).astype(f32)
+        prompt_after, prompt_do, prompt_outer, prompt_ln2 = output_backward(w, kept, prompt_grad)
+        spoken, spoken_outer, spoken_dqkv, spoken_sums = language[layer]
+        dz = jnp.concatenate([spoken_outer[0], outer[0], prompt_outer[0]], 0)
+        du = jnp.concatenate([spoken_outer[1], outer[1], prompt_outer[1]], 0)
+        da = jnp.concatenate([spoken_outer[2], outer[2], prompt_outer[2]], 0)
+        proj = blocks(jnp.concatenate([spoken[5][3], state[5][3], kept[3]], 0), dz)
+        fc = blocks(jnp.concatenate([spoken[5][1], state[5][1], kept[1]], 0), du)
+        gate = Gate([(proj, False), (fc, True)]) if tree and layer == 0 else None
+        mixed_all = jnp.concatenate([spoken[3], state[3], mixed], 0)
+        if gate:
+            mixed_all, da = gate.hold(mixed_all, da)
+        out = blocks(mixed_all, da)
+        if gate:
+            out, do = gate.hold(out, do)
+        grad, dqkv, ln1 = attention_backward(layer, state, grad_after, do)
+        if gate:
+            prompt_do, dqkv = gate.hold(prompt_do, dqkv)
+        prompt_dqkv = prompt_back(place_ref, pqkv, mixed, lse, prompt_do, carries[layer])
+        partial = nt(prompt_dqkv, w["qkv"])
+        grad_normed = scatter_rows(partial.astype(bf16), place, tree)
         grad_in, gain, shift = norm_back(before, w["ln1_gain"], grad_normed)
-        prompt_grad = grad_after + grad_in
-        pieces[layer].append((normed, dqkv, mixed, da, kept[1], du, kept[3], dz))
-        small[layer].append((gain, shift) + ln2)
-
-        joined = [jnp.concatenate(parts, 0) for parts in zip(*pieces[layer])]
-        gain1, shift1, gain2, shift2 = [sum(parts) for parts in zip(*small[layer])]
-        qkv_sums = column_sums(joined[1])
+        if layer == 0:
+            gain = jnp.sum(partial * normalised(x_all.astype(f32))[0], 0)
+            shift = jnp.sum(partial, 0)
+        prompt_grad = prompt_after + grad_in
+        if gate:
+            prompt_dqkv, dqkv = gate.hold(prompt_dqkv, dqkv)
+        normed_all = jnp.concatenate([spoken[1], state[1], normed], 0)
+        dqkv_all = jnp.concatenate([spoken_dqkv, dqkv, prompt_dqkv], 0)
+        qkv = blocks(normed_all, dqkv_all)
+        gain1, shift1, gain2, shift2 = [
+            sum(parts) for parts in zip(spoken_sums, ln1 + ln2, (gain, shift) + prompt_ln2)
+        ]
+        qkv_sums = column_sums(dqkv_all)
         vector_grads = dict(
             ln1_gain=gain1,
             ln1_bias=shift1,
             q_bias=qkv_sums[:width],
             v_bias=qkv_sums[2 * width :],
-            out_bias=column_sums(joined[3]),
+            out_bias=column_sums(da),
             ln2_gain=gain2,
             ln2_bias=shift2,
-            proj_bias=column_sums(joined[7]),
-            fc_bias=column_sums(joined[5]),
+            proj_bias=column_sums(dz),
+            fc_bias=column_sums(du),
         )
         flat = jnp.concatenate(
             [
@@ -554,27 +749,47 @@
             ],
             1,
         )
-        extra = jnp.pad(flat, ((0, 0), (0, 8 * width - flat.shape[1]))).reshape(devices, 8, width)
-        pack = jnp.concatenate(
-            [tn(joined[2], joined[3]).reshape(devices, out_rows, width), extra], 1
-        ).astype(bf16)
-        totals = [
-            lax.psum_scatter(part.astype(bf16), ALL, scatter_dimension=0, tiled=True).astype(f32)
-            for part in (
-                tn(joined[6], joined[7]),
-                tn(joined[4], joined[5]),
-                pack,
-                tn(joined[0], joined[1]),
+        extras.append(
+            jnp.pad(flat, ((0, 0), (0, 8 * width - flat.shape[1]))).astype(bf16).reshape(devices, 8, width)
+        )
+
+        if layer > 0:
+            mlp = proj.reshape(devices, -1, out_rows, width)
+            pieces_out = mlp.shape[1]
+            packed = jnp.concatenate(
+                [qkv, fc, out] + [mlp[:, number] for number in range(pieces_out)], 2
             )
-        ]
-        share = totals[2].reshape(out_rows + 8, width)
-        result = dict(proj=totals[0], fc=totals[1], out=share[:out_rows], qkv=totals[3])
-        share = share[out_rows:].reshape(8 * width)
+            packed, grad = lax.optimization_barrier((packed, grad))
+            total = lax.psum_scatter(packed, ALL, scatter_dimension=0, tiled=True).astype(f32)[0]
+            columns = [
+                total[:, first * width : last * width]
+                for first, last in [(0, 3), (3, 7), (7, 8)] + [(8 + n, 9 + n) for n in range(pieces_out)]
+            ]
+            result = dict(
+                qkv=columns[0], fc=columns[1], out=columns[2], proj=jnp.concatenate(columns[3:], 0)
+            )
+        else:
+            half = 3 * width // 2
+            result = {}
+            result["proj"], result["fc"] = (
+                gate.leaving if gate else (reduce_blocks(proj, False, tree), reduce_blocks(fc, True, tree))
+            )
+            share = reduce_blocks(jnp.concatenate([out] + extras, 1), False, tree)
+            result["qkv"] = jnp.concatenate(
+                [
+                    reduce_blocks(qkv[:, :, :half], True, tree),
+                    reduce_blocks(qkv[:, :, half:], False, tree),
+                ],
+                1,
+            )
+            result["out"] = share[:out_rows]
+        shares.append(result)
+    for number, result in enumerate(shares):
+        lines = share[out_rows + 8 * number : out_rows + 8 * (number + 1)].reshape(8 * width)
         first = 0
         for name, size in zip(SMALL, sizes):
-            result[name] = share[first : first + size]
+            result[name] = lines[first : first + size]
             first += size
-        shares.append(result)
     shares.reverse()
     grad_cont = jnp.where(marked, 0.0, grad_mixed_in) + grad.reshape(count, length, width)
     names = ("qkv", "out", "fc", "proj") + (

time: 1820 us -> 927 us (0.51)
  waiting for transfers between devices: 1090 us -> 150 us
  starting transfers between devices: 1.67 us -> 112 us
  blocking collectives: 68.6 us -> 0 us
  matrix products: 285 us -> 248 us
  local copies, waits for them, and re-layouts: 66.9 us -> 98 us
    reduce_scatter x10 -> x1, waiting for transfers between devices: 800 us -> 0.01 us  [body(): lax.psum_scatter(packed, ALL, scatter_dimension=0, tiled=True).astype(f32)]
    all_gather x8 -> x3, waiting for transfers between devices: 289 us -> 34.2 us  [the longest x1 34.1 us: gather_plain(): joined = lax.all_gather(jnp.concatenate([head, fc], 1), ALL, axis=0)]
    ppermute x0 -> x78, waiting for transfers between devices: none -> 116 us  [swap(): return lax.ppermute(value, axes, [(i, i ^ code) for i in range(total)])]
    ppermute x0 -> x78, starting transfers between devices: none -> 112 us  [swap(): return lax.ppermute(value, axes, [(i, i ^ code) for i in range(total)])]
    all_gather x2 -> x0, blocking collectives: 68.6 us -> none  [the longest x1 34.5 us: body(): lax.all_gather(norm(prompt_rows, w['ln1_gain'], w['ln1_bias']), 'seq', ax...]
    dot_general x8, matrix products: 84 us -> 50 us  [tn(): lax.dot_general(left, right, (((0,), (0,)), ((), ())), preferred_element_...]
    reduce_sum x26 -> x21, other arithmetic: 42.1 us -> 22.9 us  [column_sums(): return jnp.sum(block.astype(f32), 0)]
    unnamed x454 -> x604, local copies, waits for them, and re-layouts: 25 us -> 39.6 us
  transfers between devices with their start and end apart: 18 -> 82, of which waited for: 17 -> 27; matrix products, arithmetic and copies ran while one was open for 14% -> 27% of each run, Pallas kernels for 4% -> 10%
where the time goes in v3:
time: 927 us; the launch traced here: 918 us
  matrix products  248 us (27%)
  Pallas kernels  203 us (22%)
  waiting for transfers between devices  150 us (16%)
  starting transfers between devices  112 us (12%)
  local copies, waits for them, and re-layouts  98 us (11%)
  other arithmetic  88.6 us (10%)
  between operations  18.2 us (2%)
    ppermute x78, waiting for transfers between devices, swap(): return lax.ppermute(value, axes, [(i, i ^ code) for i in range(total)])  116 us
    ppermute x78, starting transfers between devices, swap(): return lax.ppermute(value, axes, [(i, i ^ code) for i in range(total)])  112 us
    dot_general x24, matrix products, nt(): lax.dot_general(left, right, (((1,), (1,)), ((), ())), preferred_element_...  104 us
    pallas_call x4, Pallas kernels, attend_back(): pl.pallas_call(functools.partial(attend_back_kernel, width=head_width, pa...  96.2 us
    dot_general x24, matrix products, nn(): lax.dot_general(left, right, (((1,), (0,)), ((), ())), preferred_element_...  93.6 us
    pallas_call x4, Pallas kernels, attend(): pl.pallas_call(functools.partial(attend_kernel, width=head_width), grid_s...  65.7 us
    dot_general x8, matrix products, tn(): lax.dot_general(left, right, (((0,), (0,)), ((), ())), preferred_element_...  50 us
    unnamed x604, local copies, waits for them, and re-layouts  39.6 us
  transfers between devices with their start and end apart: 82, of which 27 were waited for; matrix products, arithmetic and copies ran while one was open for 27% of the time, Pallas kernels for 10%

profile of v3, /device:TPU:0, one launch (start us, length us, event | category | flops | bytes accessed | tf_op | source)
XLA Modules:
  0.0 918.1 jit_solution(10076033955932927133)
XLA Ops:
  29.0 10.4 %collective-permute-done.8 = bf16[1,24,3072]{2,1,0:T(8,128)(2,1)S(1)} collective-permute-done((bf16[1,24,3072]{2,1,0:T(8,128)(2,1)S(1)}, bf16[1,24,3072]{2,1,0:T(8,128)(2,1)S(1)}, u32[]{:S(2)}, u32[]{:S(2)}) %collective-permute-start.8) | collective-permute-done | bytes 147488 | tf_op jit(solution)/shard_map/ppermute | solution.py:383
  50.7 9.4 %collective-permute-done.17 = bf16[1,96,768]{2,1,0:T(8,128)(2,1)S(1)} collective-permute-done((bf16[1,96,768]{2,1,0:T(8,128)(2,1)S(1)}, bf16[1,96,768]{2,1,0:T(8,128)(2,1)S(1)}, u32[]{:S(2)}, u32[]{:S(2)}) %collective-permute-start.17) | collective-permute-done | bytes 147488 | tf_op jit(solution)/shard_map/ppermute | solution.py:383
  70.3 8.1 collective-permute-done.2.refs_3_
  111.1 7.5 collective-permute-done.21.refs_2_
  119.6 8.7 collective-permute-done.22.refs_3_
  159.0 34.1 %all-gather.9.cloned.1.call-done = bf16[768,6272]{1,0:T(8,128)(2,1)} async-done(((bf16[24,6272]{1,0:T(8,128)(2,1)}), bf16[768,6272]{1,0:T(8,128)(2,1)}) %all-gather.9.cloned.1.call-update) | async-done | bytes 9633808 | tf_op jit(solution)/shard_map/all_gather | solution.py:453
  240.1 16.5 %attend.4 = (bf16[512,768]{1,0:T(8,128)(2,1)}, f32[12,2,256]{2,1,0:T(2,128)}) custom-call(s32[2]{0:T(128)} %seen_ref.15, bf16[512,2304]{1,0:T(8,128)(2,1)} %fusion.124.q_ref.k_ref.v_ref, bf16[512,2304]{1,0:T(8,128)(2,1)} %fusion.124.q_ref.k_ref.v_ref, bf16[512,2304]{1,0:T(8,128)(2,1)} %fusion.124.q_ref.k_ref.v_ref, ...), custom_call_target="tpu_custom_call" | custom-call | flops 1207959552 | bytes 4718592 | tf_op jit(solution)/shard_map/attend/pallas_call | solution.py:80
  306.4 16.3 %attend.5 = (bf16[512,768]{1,0:T(8,128)(2,1)}, f32[12,2,256]{2,1,0:T(2,128)}) custom-call(s32[2]{0:T(128)} %seen_ref.15, bf16[512,2304]{1,0:T(8,128)(2,1)} %fusion.125.q_ref.k_ref.v_ref, bf16[512,2304]{1,0:T(8,128)(2,1)} %fusion.125.q_ref.k_ref.v_ref, bf16[512,2304]{1,0:T(8,128)(2,1)} %fusion.125.q_ref.k_ref.v_ref, ...), custom_call_target="tpu_custom_call" | custom-call | flops 1207959552 | bytes 4718592 | tf_op jit(solution)/shard_map/attend/pallas_call | solution.py:80
  346.6 16.4 %attend.6 = (bf16[512,768]{1,0:T(8,128)(2,1)}, f32[12,2,256]{2,1,0:T(2,128)}) custom-call(s32[2]{0:T(128)} %seen_ref.15, bf16[512,2304]{1,0:T(8,128)(2,1)} %fusion.126.q_ref.k_ref.v_ref, bf16[512,2304]{1,0:T(8,128)(2,1)} %fusion.126.q_ref.k_ref.v_ref, bf16[512,2304]{1,0:T(8,128)(2,1)} %fusion.126.q_ref.k_ref.v_ref, ...), custom_call_target="tpu_custom_call" | custom-call | flops 1207959552 | bytes 4718592 | tf_op jit(solution)/shard_map/attend/pallas_call | solution.py:80
  381.5 16.4 %attend.7 = (bf16[512,768]{1,0:T(8,128)(2,1)}, f32[12,2,256]{2,1,0:T(2,128)}) custom-call(s32[2]{0:T(128)} %seen_ref.15, bf16[512,2304]{1,0:T(8,128)(2,1)} %fusion.127.q_ref.k_ref.v_ref, bf16[512,2304]{1,0:T(8,128)(2,1)} %fusion.127.q_ref.k_ref.v_ref, bf16[512,2304]{1,0:T(8,128)(2,1)} %fusion.127.q_ref.k_ref.v_ref, ...), custom_call_target="tpu_custom_call" | custom-call | flops 1207959552 | bytes 4718592 | tf_op jit(solution)/shard_map/attend/pallas_call | solution.py:80
  424.1 24.0 %attend_back.4 = (bf16[512,2304]{1,0:T(8,128)(2,1)}, f32[512,1536]{1,0:T(8,128)}) custom-call(s32[2]{0:T(128)} %seen_ref.15, bf16[512,2304]{1,0:T(8,128)(2,1)} %fusion.127.q_ref.k_ref.v_ref, bf16[512,2304]{1,0:T(8,128)(2,1)} %fusion.127.q_ref.k_ref.v_ref, bf16[512,2304]{1,0:T(8,128)(2,1)} %fusion.127.q_ref.k_ref.v_ref, ...), custom_call_target="tpu_custom_call" | custom-call | flops 3019898880 | bytes 14155776 | tf_op jit(solution)/shard_map/attend_back/pallas_call | solution.py:187
  455.6 8.8 fusion.292
  472.3 24.1 %attend_back.5 = (bf16[512,2304]{1,0:T(8,128)(2,1)}, f32[512,1536]{1,0:T(8,128)}) custom-call(s32[2]{0:T(128)} %seen_ref.15, bf16[512,2304]{1,0:T(8,128)(2,1)} %fusion.126.q_ref.k_ref.v_ref, bf16[512,2304]{1,0:T(8,128)(2,1)} %fusion.126.q_ref.k_ref.v_ref, bf16[512,2304]{1,0:T(8,128)(2,1)} %fusion.126.q_ref.k_ref.v_ref, ...), custom_call_target="tpu_custom_call" | custom-call | flops 3019898880 | bytes 14155776 | tf_op jit(solution)/shard_map/attend_back/pallas_call | solution.py:187
  523.5 23.9 %attend_back.6 = (bf16[512,2304]{1,0:T(8,128)(2,1)}, f32[512,1536]{1,0:T(8,128)}) custom-call(s32[2]{0:T(128)} %seen_ref.15, bf16[512,2304]{1,0:T(8,128)(2,1)} %fusion.125.q_ref.k_ref.v_ref, bf16[512,2304]{1,0:T(8,128)(2,1)} %fusion.125.q_ref.k_ref.v_ref, bf16[512,2304]{1,0:T(8,128)(2,1)} %fusion.125.q_ref.k_ref.v_ref, ...), custom_call_target="tpu_custom_call" | custom-call | flops 3019898880 | bytes 14155776 | tf_op jit(solution)/shard_map/attend_back/pallas_call | solution.py:187
  570.9 7.5 prompt_back.2
  587.9 8.9 fusion.113
  637.2 10.0 %fusion.293 = (bf16[3072]{0:T(1024)(128)(2,1)}, bf16[512,3072]{1,0:T(8,128)(2,1)S(1)}) fusion(f32[512,3072]{1,0:T(8,128)} %get-tuple-element.334, f32[3072]{0:T(1024)S(1)} %copy-done.144, bf16[512,768]{1,0:T(8,128)(2,1)S(1)} %get-tuple-element.179, bf16[3072,768]{1,0:T(8,128)(2,1)} %bitcast.406), kind=kOutput, calls=%fused_computation.645 | convolution fusion | flops 2450519040 | bytes 14960640 | tf_op jit(solution)/shard_map/dot_general | solution.py:27
  681.0 8.3 fusion.110
  720.4 24.2 %attend_back.7 = (bf16[512,2304]{1,0:T(8,128)(2,1)}, f32[512,1536]{1,0:T(8,128)}) custom-call(s32[2]{0:T(128)} %seen_ref.15, bf16[512,2304]{1,0:T(8,128)(2,1)} %fusion.124.q_ref.k_ref.v_ref, bf16[512,2304]{1,0:T(8,128)(2,1)} %fusion.124.q_ref.k_ref.v_ref, bf16[512,2304]{1,0:T(8,128)(2,1)} %fusion.124.q_ref.k_ref.v_ref, ...), custom_call_target="tpu_custom_call" | custom-call | flops 3019898880 | bytes 14155776 | tf_op jit(solution)/shard_map/attend_back/pallas_call | solution.py:187
  756.6 7.7 prompt_back.3
  790.4 8.4 collective-permute-done.49
  814.2 10.0 %collective-permute-start.72 = (bf16[1,1,1,1,24,3072]{5,4,3,2,1,0:T(8,128)(2,1)S(1)}, bf16[1,1,1,1,24,3072]{5,4,3,2,1,0:T(8,128)(2,1)S(1)}, u32[]{:S(2)}, u32[]{:S(2)}) collective-permute-start(bf16[1,1,1,1,24,3072]{5,4,3,2,1,0:T(8,128)(2,1)S(1)} %copy-done.117), channel_id=1, source_target_pairs={{0,2},{1,3},{2,0},{3,1},{4,6},{5,7},{6,4},{7,5},{8,10},{9,11},{10,... | collective-permute-start | bytes 442376 | tf_op jit(solution)/shard_map/ppermute | solution.py:383
  828.2 7.2 fusion.116
  859.7 9.5 %collective-permute-done.67 = bf16[1,1,4,2,40,768]{5,4,3,2,1,0:T(8,128)(2,1)S(1)} collective-permute-done((bf16[1,1,4,2,40,768]{5,4,3,2,1,0:T(8,128)(2,1)S(1)}, bf16[1,1,4,2,40,768]{5,4,3,2,1,0:T(8,128)(2,1)S(1)}, u32[]{:S(2)}, u32[]{:S(2)}) %collective-permute-start.67) | collective-permute-done | bytes 491552 | tf_op jit(solution)/shard_map/ppermute | solution.py:383
  (1097 shorter events, 573.5 us)
Async XLA Ops:
  7.2 134.9 %all-gather.7.cloned.1.call-start = ((), (), s32[]{:S(2)}) async-start(), calls=%async_computation.2 | async-start | bytes 5068800 | tf_op jit(solution)/shard_map/all_gather | solution.py:465
  13.6 179.6 %all-gather.9.cloned.1.call-start = ((), (), s32[]{:S(2)}) async-start(), calls=%async_computation.3 | async-start | bytes 9934848 | tf_op jit(solution)/shard_map/all_gather | solution.py:453
  40.3 294.4 %all-gather.11.cloned.1.call-start = ((), (), s32[]{:S(2)}) async-start(), calls=%async_computation.4 | async-start | bytes 4866048 | tf_op jit(solution)/shard_map/all_gather | solution.py:458
  40.4 26.4 %collective-permute-start = (bf16[1,64,768]{2,1,0:T(8,128)(2,1)S(1)}, bf16[1,64,768]{2,1,0:T(8,128)(2,1)S(1)}, u32[]{:S(2)}, u32[]{:S(2)}) collective-permute-start(bf16[1,64,768]{2,1,0:T(8,128)(2,1)S(1)} %bitcast.488), channel_id=1, source_target_pairs={{0,1},{1,0},{2,3},{3,2},{4,5},{5,4},{6,7},{7,6},{8,9},{9,8},{10,11... | collective-permute-start | bytes 294920 | tf_op jit(solution)/shard_map/ppermute | solution.py:383
  42.0 26.2 %collective-permute-start.1 = (bf16[1,64,768]{2,1,0:T(8,128)(2,1)S(1)}, bf16[1,64,768]{2,1,0:T(8,128)(2,1)S(1)}, u32[]{:S(2)}, u32[]{:S(2)}) collective-permute-start(bf16[1,64,768]{2,1,0:T(8,128)(2,1)S(1)} %bitcast.489), channel_id=1, source_target_pairs={{0,2},{1,3},{2,0},{3,1},{4,6},{5,7},{6,4},{7,5},{8,10},{9,11},{10,... | collective-permute-start | bytes 294920 | tf_op jit(solution)/shard_map/ppermute | solution.py:383
  60.2 43.4 %collective-permute-start.10 = (bf16[4,24,3072]{2,1,0:T(8,128)(2,1)S(1)}, bf16[4,24,3072]{2,1,0:T(8,128)(2,1)}, u32[]{:S(2)}, u32[]{:S(2)}) collective-permute-start(bf16[4,24,3072]{2,1,0:T(8,128)(2,1)S(1)} %pad_maximum_fusion.3.refs_0_), channel_id=1, source_target_pairs={{0,16},{1,17},{2,18},{3,19},{4,20},{5,21},{6,22},{7,23},{8,24},{9,... | collective-permute-start | bytes 1769480 | tf_op jit(solution)/shard_map/ppermute | solution.py:383
  65.2 39.0 %collective-permute-start.11 = (bf16[4,24,3072]{2,1,0:T(8,128)(2,1)S(1)}, bf16[4,24,3072]{2,1,0:T(8,128)(2,1)}, u32[]{:S(2)}, u32[]{:S(2)}) collective-permute-start(bf16[4,24,3072]{2,1,0:T(8,128)(2,1)S(1)} %pad_maximum_fusion.3.refs_0_), channel_id=1, source_target_pairs={{0,1},{1,0},{2,3},{3,2},{4,5},{5,4},{6,7},{7,6},{8,9},{9,8},{10,11... | collective-permute-start | bytes 1769480 | tf_op jit(solution)/shard_map/ppermute | solution.py:383
  65.9 38.3 %collective-permute-start.13 = (bf16[4,24,3072]{2,1,0:T(8,128)(2,1)S(1)}, bf16[4,24,3072]{2,1,0:T(8,128)(2,1)}, u32[]{:S(2)}, u32[]{:S(2)}) collective-permute-start(bf16[4,24,3072]{2,1,0:T(8,128)(2,1)S(1)} %pad_maximum_fusion.3.refs_0_), channel_id=1, source_target_pairs={{0,8},{1,9},{2,10},{3,11},{4,12},{5,13},{6,14},{7,15},{8,0},{9,1},... | collective-permute-start | bytes 1769480 | tf_op jit(solution)/shard_map/ppermute | solution.py:383
  66.8 37.9 %collective-permute-start.20 = (bf16[4,96,768]{2,1,0:T(8,128)(2,1)}, bf16[4,96,768]{2,1,0:T(8,128)(2,1)}, u32[]{:S(2)}, u32[]{:S(2)}) collective-permute-start(bf16[4,96,768]{2,1,0:T(8,128)(2,1)} %pad_maximum_fusion.4.refs_0_), channel_id=1, source_target_pairs={{0,1},{1,0},{2,3},{3,2},{4,5},{5,4},{6,7},{7,6},{8,9},{9,8},{10,11... | collective-permute-start | bytes 1769480 | tf_op jit(solution)/shard_map/ppermute | solution.py:383
  104.7 23.5 %collective-permute-start.22 = (bf16[4,96,768]{2,1,0:T(8,128)(2,1)}, bf16[4,96,768]{2,1,0:T(8,128)(2,1)S(1)}, u32[]{:S(2)}, u32[]{:S(2)}) collective-permute-start(bf16[4,96,768]{2,1,0:T(8,128)(2,1)} %collective-permute-done.20.refs_1_), channel_id=1, source_target_pairs={{0,16},{1,17},{2,18},{3,19},{4,20},{5,21},{6,22},{7,23},{8,24},{9,... | collective-permute-start | bytes 1769480 | tf_op jit(solution)/shard_map/ppermute | solution.py:383
  131.2 775.7 %reduce-scatter.2.cloned.1.call-start = ((), (), s32[]{:S(2)}) async-start(), calls=%async_computation.1 | async-start | bytes 14598144 | tf_op jit(solution)/shard_map/reduce_scatter | solution.py:763
  227.4 49.8 %collective-permute-start.27 = (bf16[1,64,768]{2,1,0:T(8,128)(2,1)}, bf16[1,64,768]{2,1,0:T(8,128)(2,1)}, u32[]{:S(2)}, u32[]{:S(2)}) collective-permute-start(bf16[1,64,768]{2,1,0:T(8,128)(2,1)} %fusion.247.refs_0_), channel_id=1, source_target_pairs={{0,1},{1,0},{2,3},{3,2},{4,5},{5,4},{6,7},{7,6},{8,9},{9,8},{10,11... | collective-permute-start | bytes 294920 | tf_op jit(solution)/shard_map/ppermute | solution.py:383
  228.8 50.3 %collective-permute-start.28 = (bf16[1,64,768]{2,1,0:T(8,128)(2,1)}, bf16[1,64,768]{2,1,0:T(8,128)(2,1)}, u32[]{:S(2)}, u32[]{:S(2)}) collective-permute-start(bf16[1,64,768]{2,1,0:T(8,128)(2,1)} %fusion.247.refs_0_), channel_id=1, source_target_pairs={{0,2},{1,3},{2,0},{3,1},{4,6},{5,7},{6,4},{7,5},{8,10},{9,11},{10,... | collective-permute-start | bytes 294920 | tf_op jit(solution)/shard_map/ppermute | solution.py:383
  230.2 62.6 %collective-permute-start.29 = (bf16[1,64,768]{2,1,0:T(8,128)(2,1)}, bf16[1,64,768]{2,1,0:T(8,128)(2,1)}, u32[]{:S(2)}, u32[]{:S(2)}) collective-permute-start(bf16[1,64,768]{2,1,0:T(8,128)(2,1)} %fusion.247.refs_0_), channel_id=1, source_target_pairs={{0,3},{1,2},{2,1},{3,0},{4,7},{5,6},{6,5},{7,4},{8,11},{9,10},{10,... | collective-permute-start | bytes 294920 | tf_op jit(solution)/shard_map/ppermute | solution.py:383
  230.9 61.9 %collective-permute-start.30 = (bf16[1,64,768]{2,1,0:T(8,128)(2,1)}, bf16[1,64,768]{2,1,0:T(8,128)(2,1)}, u32[]{:S(2)}, u32[]{:S(2)}) collective-permute-start(bf16[1,64,768]{2,1,0:T(8,128)(2,1)} %fusion.247.refs_0_), channel_id=1, source_target_pairs={{0,4},{1,5},{2,6},{3,7},{4,0},{5,1},{6,2},{7,3},{8,12},{9,13},{10,... | collective-permute-start | bytes 294920 | tf_op jit(solution)/shard_map/ppermute | solution.py:383
  232.7 60.1 %collective-permute-start.31 = (bf16[1,64,768]{2,1,0:T(8,128)(2,1)}, bf16[1,64,768]{2,1,0:T(8,128)(2,1)}, u32[]{:S(2)}, u32[]{:S(2)}) collective-permute-start(bf16[1,64,768]{2,1,0:T(8,128)(2,1)} %fusion.247.refs_0_), channel_id=1, source_target_pairs={{0,5},{1,4},{2,7},{3,6},{4,1},{5,0},{6,3},{7,2},{8,13},{9,12},{10,... | collective-permute-start | bytes 294920 | tf_op jit(solution)/shard_map/ppermute | solution.py:383
  606.2 53.9 %collective-permute-start.34 = (bf16[64,768]{1,0:T(8,128)(2,1)}, bf16[64,768]{1,0:T(8,128)(2,1)}, u32[]{:S(2)}, u32[]{:S(2)}) collective-permute-start(bf16[64,768]{1,0:T(8,128)(2,1)} %get-tuple-element.235), channel_id=1, source_target_pairs={{0,1},{1,0},{2,3},{3,2},{4,5},{5,4},{6,7},{7,6},{8,9},{9,8},{10,11... | collective-permute-start | bytes 294920 | tf_op jit(solution)/shard_map/ppermute | solution.py:383
  607.7 54.3 %collective-permute-start.35 = (bf16[64,768]{1,0:T(8,128)(2,1)}, bf16[64,768]{1,0:T(8,128)(2,1)}, u32[]{:S(2)}, u32[]{:S(2)}) collective-permute-start(bf16[64,768]{1,0:T(8,128)(2,1)} %get-tuple-element.241), channel_id=1, source_target_pairs={{0,2},{1,3},{2,0},{3,1},{4,6},{5,7},{6,4},{7,5},{8,10},{9,11},{10,... | collective-permute-start | bytes 294920 | tf_op jit(solution)/shard_map/ppermute | solution.py:383
  607.7 63.3 %collective-permute-start.36 = (bf16[64,768]{1,0:T(8,128)(2,1)}, bf16[64,768]{1,0:T(8,128)(2,1)}, u32[]{:S(2)}, u32[]{:S(2)}) collective-permute-start(bf16[64,768]{1,0:T(8,128)(2,1)} %get-tuple-element.240), channel_id=1, source_target_pairs={{0,3},{1,2},{2,1},{3,0},{4,7},{5,6},{6,5},{7,4},{8,11},{9,10},{10,... | collective-permute-start | bytes 294920 | tf_op jit(solution)/shard_map/ppermute | solution.py:383
  609.7 61.3 %collective-permute-start.37 = (bf16[64,768]{1,0:T(8,128)(2,1)}, bf16[64,768]{1,0:T(8,128)(2,1)}, u32[]{:S(2)}, u32[]{:S(2)}) collective-permute-start(bf16[64,768]{1,0:T(8,128)(2,1)} %get-tuple-element.239), channel_id=1, source_target_pairs={{0,4},{1,5},{2,6},{3,7},{4,0},{5,1},{6,2},{7,3},{8,12},{9,13},{10,... | collective-permute-start | bytes 294920 | tf_op jit(solution)/shard_map/ppermute | solution.py:383
  610.1 60.9 %collective-permute-start.38 = (bf16[64,768]{1,0:T(8,128)(2,1)}, bf16[64,768]{1,0:T(8,128)(2,1)}, u32[]{:S(2)}, u32[]{:S(2)}) collective-permute-start(bf16[64,768]{1,0:T(8,128)(2,1)} %get-tuple-element.238), channel_id=1, source_target_pairs={{0,5},{1,4},{2,7},{3,6},{4,1},{5,0},{6,3},{7,2},{8,13},{9,12},{10,... | collective-permute-start | bytes 294920 | tf_op jit(solution)/shard_map/ppermute | solution.py:383
  712.2 39.4 %collective-permute-start.43 = (bf16[1,1,4,2,96,768]{5,4,3,2,1,0:T(8,128)(2,1)}, bf16[1,1,4,2,96,768]{5,4,3,2,1,0:T(8,128)(2,1)}, u32[]{:S(2)}, u32[]{:S(2)}) collective-permute-start(bf16[1,1,4,2,96,768]{5,4,3,2,1,0:T(8,128)(2,1)} %add_convert_fusion.5), channel_id=1, source_target_pairs={{0,16},{1,17},{2,18},{3,19},{4,20},{5,21},{6,22},{7,23},{8,24},{9,... | collective-permute-start | bytes 3538952 | tf_op jit(solution)/shard_map/ppermute | solution.py:383
  718.2 35.8 %collective-permute-start.44 = (bf16[2,1,4,1,24,3072]{5,4,3,2,1,0:T(8,128)(2,1)}, bf16[2,1,4,1,24,3072]{5,4,3,2,1,0:T(8,128)(2,1)}, u32[]{:S(2)}, u32[]{:S(2)}) collective-permute-start(bf16[2,1,4,1,24,3072]{5,4,3,2,1,0:T(8,128)(2,1)} %add_convert_fusion.4), channel_id=1, source_target_pairs={{0,1},{1,0},{2,3},{3,2},{4,5},{5,4},{6,7},{7,6},{8,9},{9,8},{10,11... | collective-permute-start | bytes 3538952 | tf_op jit(solution)/shard_map/ppermute | solution.py:383
  814.1 31.5 %collective-permute-start.66 = (bf16[2,1,4,2,40,768]{5,4,3,2,1,0:T(8,128)(2,1)S(1)}, bf16[2,1,4,2,40,768]{5,4,3,2,1,0:T(8,128)(2,1)S(1)}, u32[]{:S(2)}, u32[]{:S(2)}) collective-permute-start(bf16[2,1,4,2,40,768]{5,4,3,2,1,0:T(8,128)(2,1)S(1)} %constant_dynamic-slice_fusion), channel_id=1, source_target_pairs={{0,8},{1,9},{2,10},{3,11},{4,12},{5,13},{6,14},{7,15},{8,0},{9,1},... | collective-permute-start | bytes 2949128 | tf_op jit(solution)/shard_map/ppermute | solution.py:383
  (353 other events, 3507.2 us)
Sparse Core Ops, SparseCore 0:
  13.7 91.2 all-gather.6
  108.4 84.6 all-gather.8
  196.7 62.8 all-gather.10
  655.4 181.2 reduce-scatter.1

commit v4 on v3

--- a/solution.py
+++ b/solution.py
@@ -613,8 +613,7 @@
         tree,
         (3 * width, width, small_lanes),
     )
-    weights = []
-    for parts in gathered:
+    def unpacked(parts):
         names = ("qkv", "out", "small", "fc", "proj")
         w = {name: part.reshape(-1, part.shape[2]) for name, part in zip(names, parts)}
         share = w.pop("small").reshape(devices, -1)
@@ -623,46 +622,51 @@
             w[name] = share[:, first : first + size].reshape(devices * size).astype(f32)
             first += size
         w["qkv_bias"] = jnp.concatenate([w["q_bias"], jnp.zeros((width,), f32), w["v_bias"]])
-        weights.append(w)
+        return w
 
     def project(w, normed):
         return (nn(normed, w["qkv"]) + w["qkv_bias"]).astype(bf16)
 
-    prompt_rows = x_prompt.astype(f32)
-    prompt_states = []
+    def cont_forward(layer, current):
+        w = weights[layer]
+        normed = norm(current, w["ln1_gain"], w["ln1_bias"])
+        qkv = project(w, normed)
+        mixed, lse = attend(offsets, qkv, prompt_states[layer][2])
+        result, kept = block_output(w, current, mixed)
+        return result, (current, normed, qkv, mixed, lse, kept)
+
+    inputs = x_cont.astype(f32)
+    latent = inputs.reshape(rows, width)
+    prompt_rows, all_rows = x_prompt.astype(f32), x_all
+    weights, prompt_states, latent_states = [], [], []
     for layer in range(LAYERS):
-        w = weights[layer]
-        if layer == 0:
-            all_normed = norm(x_all.astype(f32), w["ln1_gain"], w["ln1_bias"])
-        else:
-            all_normed = gather_rows(norm(prompt_rows, w["ln1_gain"], w["ln1_bias"]), place_ref, tree)
+        parts = gathered[layer]
+        if layer > 0:
+            early, latent = lax.optimization_barrier((parts[:-1], latent))
+            parts = list(early) + parts[-1:]
+        w = unpacked(parts)
+        weights.append(w)
+        all_normed = norm(all_rows.astype(f32), w["ln1_gain"], w["ln1_bias"])
         pqkv = project(w, all_normed)
         mixed, lse = prompt_attend(place_ref, pqkv, prompt_dev)
         result, kept = block_output(w, prompt_rows, mixed)
         prompt_states.append((prompt_rows, all_normed, pqkv, mixed, lse, kept))
         prompt_rows = result
+        if layer + 1 < LAYERS:
+            all_rows = gather_rows(prompt_rows, place_ref, tree)
+        latent, state = cont_forward(layer, latent)
+        latent_states.append(state)
     prompt_out = prompt_rows
-
-    def pass_forward(current):
-        states = []
-        for layer in range(LAYERS):
-            w = weights[layer]
-            normed = norm(current, w["ln1_gain"], w["ln1_bias"])
-            qkv = project(w, normed)
-            mixed, lse = attend(offsets, qkv, prompt_states[layer][2])
-            result, kept = block_output(w, current, mixed)
-            states.append((current, normed, qkv, mixed, lse, kept))
-            current = result
-        return current, states
-
-    inputs = x_cont.astype(f32)
-    latent, latent_states = pass_forward(inputs.reshape(rows, width))
     latent = latent.reshape(count, length, width)
     shifted = jnp.concatenate([jnp.zeros((count, 1, width), f32), latent[:, :-1]], 1)
     marked = jnp.any(
         thought_pos[:, :, None] + 1 == lax.broadcasted_iota(jnp.int32, (1, 1, length), 2), 1
     )[:, :, None]
-    current, language_states = pass_forward(jnp.where(marked, shifted, inputs).reshape(rows, width))
+    current = jnp.where(marked, shifted, inputs).reshape(rows, width)
+    language_states = []
+    for layer in range(LAYERS):
+        current, state = cont_forward(layer, current)
+        language_states.append(state)
     cont_out = current.reshape(count, length, width).astype(bf16)
 
     carries = [jnp.zeros((plen, 2 * width), f32) for layer in range(LAYERS)]

time: 927 us -> 895 us (0.965)
  waiting for transfers between devices: 150 us -> 132 us
  local copies, waits for them, and re-layouts: 98 us -> 81.7 us
    all_gather x1, waiting for transfers between devices: 34.1 us -> 0.01 us  [gather_plain(): joined = lax.all_gather(jnp.concatenate([head, fc], 1), ALL, axis=0)]
    ppermute x78, waiting for transfers between devices: 116 us -> 132 us  [swap(): return lax.ppermute(value, axes, [(i, i ^ code) for i in range(total)])]
    convert_element_type x18, local copies, waits for them, and re-layouts: 16 us -> 1.44 us  [unpacked(): w[name] = share[:, first:first + size].reshape(devices * size).astype(f32)]
    unnamed x604 -> x576, local copies, waits for them, and re-layouts: 39.6 us -> 36.3 us
  transfers between devices with their start and end apart: 82 -> 82, of which waited for: 27 -> 30; matrix products, arithmetic and copies ran while one was open for 27% -> 27% of each run, Pallas kernels for 10% -> 10%
where the time goes in v4:
time: 895 us; the launch traced here: 889 us
  matrix products  245 us (27%)
  Pallas kernels  204 us (23%)
  waiting for transfers between devices  132 us (15%)
  starting transfers between devices  119 us (13%)
  other arithmetic  90.5 us (10%)
  local copies, waits for them, and re-layouts  81.7 us (9%)
  between operations  18.2 us (2%)
    ppermute x78, waiting for transfers between devices, swap(): return lax.ppermute(value, axes, [(i, i ^ code) for i in range(total)])  132 us
    ppermute x78, starting transfers between devices, swap(): return lax.ppermute(value, axes, [(i, i ^ code) for i in range(total)])  118 us
    dot_general x24, matrix products, nt(): lax.dot_general(left, right, (((1,), (1,)), ((), ())), preferred_element_...  104 us
    pallas_call x4, Pallas kernels, attend_back(): pl.pallas_call(functools.partial(attend_back_kernel, width=head_width, pa...  95.9 us
    dot_general x24, matrix products, nn(): lax.dot_general(left, right, (((1,), (0,)), ((), ())), preferred_element_...  91.1 us
    pallas_call x4, Pallas kernels, attend(): pl.pallas_call(functools.partial(attend_kernel, width=head_width), grid_s...  65.6 us
    dot_general x8, matrix products, tn(): lax.dot_general(left, right, (((0,), (0,)), ((), ())), preferred_element_...  49.4 us
    unnamed x576, local copies, waits for them, and re-layouts  36.3 us
  transfers between devices with their start and end apart: 82, of which 30 were waited for; matrix products, arithmetic and copies ran while one was open for 27% of the time, Pallas kernels for 10%

profile of v4, /device:TPU:0, one launch (start us, length us, event | category | flops | bytes accessed | tf_op | source)
XLA Modules:
  0.0 889.0 jit_solution(7557688440718897158)
XLA Ops:
  51.7 11.0 %collective-permute-done.17 = bf16[1,96,768]{2,1,0:T(8,128)(2,1)S(1)} collective-permute-done((bf16[1,96,768]{2,1,0:T(8,128)(2,1)S(1)}, bf16[1,96,768]{2,1,0:T(8,128)(2,1)S(1)}, u32[]{:S(2)}, u32[]{:S(2)}) %collective-permute-start.17) | collective-permute-done | bytes 147488 | tf_op jit(solution)/shard_map/ppermute | solution.py:383
  78.6 7.6 collective-permute-done.3.refs_4_
  96.0 7.3 collective-permute-done.6.refs_7_
  111.2 8.9 %collective-permute-done.21.refs_2_ = bf16[4,96,768]{2,1,0:T(8,128)(2,1)S(1)} collective-permute-done((bf16[4,96,768]{2,1,0:T(8,128)(2,1)}, bf16[4,96,768]{2,1,0:T(8,128)(2,1)S(1)}, u32[]{:S(2)}, u32[]{:S(2)}) %collective-permute-start.21) | collective-permute-done | bytes 589856 | tf_op jit(solution)/shard_map/ppermute | solution.py:383
  121.2 10.5 %collective-permute-done.22.refs_3_ = bf16[4,96,768]{2,1,0:T(8,128)(2,1)S(1)} collective-permute-done((bf16[4,96,768]{2,1,0:T(8,128)(2,1)}, bf16[4,96,768]{2,1,0:T(8,128)(2,1)S(1)}, u32[]{:S(2)}, u32[]{:S(2)}) %collective-permute-start.22) | collective-permute-done | bytes 589856 | tf_op jit(solution)/shard_map/ppermute | solution.py:383
  185.2 16.5 %attend.4 = (bf16[512,768]{1,0:T(8,128)(2,1)}, f32[12,2,256]{2,1,0:T(2,128)}) custom-call(s32[2]{0:T(128)} %seen_ref.15, bf16[512,2304]{1,0:T(8,128)(2,1)} %fusion.123.q_ref.k_ref.v_ref, bf16[512,2304]{1,0:T(8,128)(2,1)} %fusion.123.q_ref.k_ref.v_ref, bf16[512,2304]{1,0:T(8,128)(2,1)} %fusion.123.q_ref.k_ref.v_ref, ...), custom_call_target="tpu_custom_call" | custom-call | flops 1207959552 | bytes 4718592 | tf_op jit(solution)/shard_map/attend/pallas_call | solution.py:80
  268.6 16.3 %attend.5 = (bf16[512,768]{1,0:T(8,128)(2,1)}, f32[12,2,256]{2,1,0:T(2,128)}) custom-call(s32[2]{0:T(128)} %seen_ref.15, bf16[512,2304]{1,0:T(8,128)(2,1)} %fusion.125.q_ref.k_ref.v_ref, bf16[512,2304]{1,0:T(8,128)(2,1)} %fusion.125.q_ref.k_ref.v_ref, bf16[512,2304]{1,0:T(8,128)(2,1)} %fusion.125.q_ref.k_ref.v_ref, ...), custom_call_target="tpu_custom_call" | custom-call | flops 1207959552 | bytes 4718592 | tf_op jit(solution)/shard_map/attend/pallas_call | solution.py:80
  308.4 16.4 %attend.6 = (bf16[512,768]{1,0:T(8,128)(2,1)}, f32[12,2,256]{2,1,0:T(2,128)}) custom-call(s32[2]{0:T(128)} %seen_ref.15, bf16[512,2304]{1,0:T(8,128)(2,1)} %fusion.126.q_ref.k_ref.v_ref, bf16[512,2304]{1,0:T(8,128)(2,1)} %fusion.126.q_ref.k_ref.v_ref, bf16[512,2304]{1,0:T(8,128)(2,1)} %fusion.126.q_ref.k_ref.v_ref, ...), custom_call_target="tpu_custom_call" | custom-call | flops 1207959552 | bytes 4718592 | tf_op jit(solution)/shard_map/attend/pallas_call | solution.py:80
  343.7 16.5 %attend.7 = (bf16[512,768]{1,0:T(8,128)(2,1)}, f32[12,2,256]{2,1,0:T(2,128)}) custom-call(s32[2]{0:T(128)} %seen_ref.15, bf16[512,2304]{1,0:T(8,128)(2,1)} %fusion.127.q_ref.k_ref.v_ref, bf16[512,2304]{1,0:T(8,128)(2,1)} %fusion.127.q_ref.k_ref.v_ref, bf16[512,2304]{1,0:T(8,128)(2,1)} %fusion.127.q_ref.k_ref.v_ref, ...), custom_call_target="tpu_custom_call" | custom-call | flops 1207959552 | bytes 4718592 | tf_op jit(solution)/shard_map/attend/pallas_call | solution.py:80
  385.7 23.9 %attend_back.4 = (bf16[512,2304]{1,0:T(8,128)(2,1)}, f32[512,1536]{1,0:T(8,128)}) custom-call(s32[2]{0:T(128)} %seen_ref.15, bf16[512,2304]{1,0:T(8,128)(2,1)} %fusion.127.q_ref.k_ref.v_ref, bf16[512,2304]{1,0:T(8,128)(2,1)} %fusion.127.q_ref.k_ref.v_ref, bf16[512,2304]{1,0:T(8,128)(2,1)} %fusion.127.q_ref.k_ref.v_ref, ...), custom_call_target="tpu_custom_call" | custom-call | flops 3019898880 | bytes 14155776 | tf_op jit(solution)/shard_map/attend_back/pallas_call | solution.py:187
  416.7 9.7 %fusion.294 = (bf16[3072]{0:T(1024)(128)(2,1)}, bf16[512,3072]{1,0:T(8,128)(2,1)S(1)}) fusion(f32[512,3072]{1,0:T(8,128)} %get-tuple-element.350, f32[3072]{0:T(1024)S(1)} %copy-done.147, bf16[512,768]{1,0:T(8,128)(2,1)S(1)} %get-tuple-element.191, bf16[3072,768]{1,0:T(8,128)(2,1)} %bitcast.415), kind=kOutput, calls=%fused_computation.650 | convolution fusion | flops 2450519040 | bytes 14960640 | tf_op jit(solution)/shard_map/dot_general | solution.py:27
  434.2 23.9 %attend_back.5 = (bf16[512,2304]{1,0:T(8,128)(2,1)}, f32[512,1536]{1,0:T(8,128)}) custom-call(s32[2]{0:T(128)} %seen_ref.15, bf16[512,2304]{1,0:T(8,128)(2,1)} %fusion.126.q_ref.k_ref.v_ref, bf16[512,2304]{1,0:T(8,128)(2,1)} %fusion.126.q_ref.k_ref.v_ref, bf16[512,2304]{1,0:T(8,128)(2,1)} %fusion.126.q_ref.k_ref.v_ref, ...), custom_call_target="tpu_custom_call" | custom-call | flops 3019898880 | bytes 14155776 | tf_op jit(solution)/shard_map/attend_back/pallas_call | solution.py:187
  486.8 23.9 %attend_back.6 = (bf16[512,2304]{1,0:T(8,128)(2,1)}, f32[512,1536]{1,0:T(8,128)}) custom-call(s32[2]{0:T(128)} %seen_ref.15, bf16[512,2304]{1,0:T(8,128)(2,1)} %fusion.125.q_ref.k_ref.v_ref, bf16[512,2304]{1,0:T(8,128)(2,1)} %fusion.125.q_ref.k_ref.v_ref, bf16[512,2304]{1,0:T(8,128)(2,1)} %fusion.125.q_ref.k_ref.v_ref, ...), custom_call_target="tpu_custom_call" | custom-call | flops 3019898880 | bytes 14155776 | tf_op jit(solution)/shard_map/attend_back/pallas_call | solution.py:187
  534.1 7.4 prompt_back.2
  551.1 8.8 fusion.113
  562.6 9.8 %collective-permute-start.35 = (bf16[64,768]{1,0:T(8,128)(2,1)}, bf16[64,768]{1,0:T(8,128)(2,1)}, u32[]{:S(2)}, u32[]{:S(2)}) collective-permute-start(bf16[64,768]{1,0:T(8,128)(2,1)} %get-tuple-element.251), channel_id=1, source_target_pairs={{0,2},{1,3},{2,0},{3,1},{4,6},{5,7},{6,4},{7,5},{8,10},{9,11},{10,... | collective-permute-start | bytes 294920 | tf_op jit(solution)/shard_map/ppermute | solution.py:383
  605.7 9.5 %fusion.295 = (bf16[3072]{0:T(1024)(128)(2,1)}, bf16[512,3072]{1,0:T(8,128)(2,1)S(1)}) fusion(f32[512,3072]{1,0:T(8,128)} %get-tuple-element.338, f32[3072]{0:T(1024)S(1)} %copy-done.148, bf16[512,768]{1,0:T(8,128)(2,1)S(1)} %get-tuple-element.189, bf16[3072,768]{1,0:T(8,128)(2,1)} %bitcast.416), kind=kOutput, calls=%fused_computation.651 | convolution fusion | flops 2450519040 | bytes 14960640 | tf_op jit(solution)/shard_map/dot_general | solution.py:27
  646.4 9.0 %fusion.110 = bf16[768,3072]{1,0:T(8,128)(2,1)S(1)} fusion(bf16[64,3072]{1,0:T(8,128)(2,1)S(1)} %get-tuple-element.370, bf16[512,3072]{1,0:T(8,128)(2,1)} %copy-done.240, bf16[512,3072]{1,0:T(8,128)(2,1)S(1)} %copy-done.238, bf16[64,768]{1,0:T(8,128)(2,1)S(1)} %copy-done.113, bf16[512,768]{1,0:T(8,128)(2,1)S(1)} %copy-done.76, ...), kind=kOutput, calls=%fused_computation.126 | convolution fusion | flops 5161254912 | bytes 13074432 | tf_op jit(solution)/shard_map/dot_general | solution.py:31
  688.1 24.3 %attend_back.7 = (bf16[512,2304]{1,0:T(8,128)(2,1)}, f32[512,1536]{1,0:T(8,128)}) custom-call(s32[2]{0:T(128)} %seen_ref.15, bf16[512,2304]{1,0:T(8,128)(2,1)} %fusion.123.q_ref.k_ref.v_ref, bf16[512,2304]{1,0:T(8,128)(2,1)} %fusion.123.q_ref.k_ref.v_ref, bf16[512,2304]{1,0:T(8,128)(2,1)} %fusion.123.q_ref.k_ref.v_ref, ...), custom_call_target="tpu_custom_call" | custom-call | flops 3019898880 | bytes 14155776 | tf_op jit(solution)/shard_map/attend_back/pallas_call | solution.py:187
  722.3 7.9 prompt_back.3
  788.3 7.2 fusion.116
  797.7 8.4 collective-permute-done.73
  828.5 9.2 %collective-permute-done.67 = bf16[1,1,4,2,40,768]{5,4,3,2,1,0:T(8,128)(2,1)S(1)} collective-permute-done((bf16[1,1,4,2,40,768]{5,4,3,2,1,0:T(8,128)(2,1)S(1)}, bf16[1,1,4,2,40,768]{5,4,3,2,1,0:T(8,128)(2,1)S(1)}, u32[]{:S(2)}, u32[]{:S(2)}) %collective-permute-start.67) | collective-permute-done | bytes 491552 | tf_op jit(solution)/shard_map/ppermute | solution.py:383
  841.7 8.2 collective-permute-start.57
  (1075 shorter events, 568.9 us)
Async XLA Ops:
  7.2 138.9 %all-gather.7.cloned.1.call-start = ((), (), s32[]{:S(2)}) async-start(), calls=%async_computation.2 | async-start | bytes 5068800 | tf_op jit(solution)/shard_map/all_gather | solution.py:465
  13.6 222.3 %all-gather.9.cloned.1.call-start = ((), (), s32[]{:S(2)}) async-start(), calls=%async_computation.3 | async-start | bytes 9934848 | tf_op jit(solution)/shard_map/all_gather | solution.py:453
  41.4 255.1 %all-gather.11.cloned.1.call-start = ((), (), s32[]{:S(2)}) async-start(), calls=%async_computation.4 | async-start | bytes 4866048 | tf_op jit(solution)/shard_map/all_gather | solution.py:458
  41.4 26.1 %collective-permute-start = (bf16[1,64,768]{2,1,0:T(8,128)(2,1)S(1)}, bf16[1,64,768]{2,1,0:T(8,128)(2,1)S(1)}, u32[]{:S(2)}, u32[]{:S(2)}) collective-permute-start(bf16[1,64,768]{2,1,0:T(8,128)(2,1)S(1)} %bitcast.501), channel_id=1, source_target_pairs={{0,1},{1,0},{2,3},{3,2},{4,5},{5,4},{6,7},{7,6},{8,9},{9,8},{10,11... | collective-permute-start | bytes 294920 | tf_op jit(solution)/shard_map/ppermute | solution.py:383
  43.0 25.5 %collective-permute-start.1 = (bf16[1,64,768]{2,1,0:T(8,128)(2,1)S(1)}, bf16[1,64,768]{2,1,0:T(8,128)(2,1)S(1)}, u32[]{:S(2)}, u32[]{:S(2)}) collective-permute-start(bf16[1,64,768]{2,1,0:T(8,128)(2,1)S(1)} %bitcast.502), channel_id=1, source_target_pairs={{0,2},{1,3},{2,0},{3,1},{4,6},{5,7},{6,4},{7,5},{8,10},{9,11},{10,... | collective-permute-start | bytes 294920 | tf_op jit(solution)/shard_map/ppermute | solution.py:383
  62.6 42.1 %collective-permute-start.10 = (bf16[4,24,3072]{2,1,0:T(8,128)(2,1)S(1)}, bf16[4,24,3072]{2,1,0:T(8,128)(2,1)}, u32[]{:S(2)}, u32[]{:S(2)}) collective-permute-start(bf16[4,24,3072]{2,1,0:T(8,128)(2,1)S(1)} %pad_maximum_fusion.3.refs_0_), channel_id=1, source_target_pairs={{0,16},{1,17},{2,18},{3,19},{4,20},{5,21},{6,22},{7,23},{8,24},{9,... | collective-permute-start | bytes 1769480 | tf_op jit(solution)/shard_map/ppermute | solution.py:383
  65.5 39.2 %collective-permute-start.11 = (bf16[4,24,3072]{2,1,0:T(8,128)(2,1)S(1)}, bf16[4,24,3072]{2,1,0:T(8,128)(2,1)}, u32[]{:S(2)}, u32[]{:S(2)}) collective-permute-start(bf16[4,24,3072]{2,1,0:T(8,128)(2,1)S(1)} %pad_maximum_fusion.3.refs_0_), channel_id=1, source_target_pairs={{0,1},{1,0},{2,3},{3,2},{4,5},{5,4},{6,7},{7,6},{8,9},{9,8},{10,11... | collective-permute-start | bytes 1769480 | tf_op jit(solution)/shard_map/ppermute | solution.py:383
  66.7 38.1 %collective-permute-start.13 = (bf16[4,24,3072]{2,1,0:T(8,128)(2,1)S(1)}, bf16[4,24,3072]{2,1,0:T(8,128)(2,1)}, u32[]{:S(2)}, u32[]{:S(2)}) collective-permute-start(bf16[4,24,3072]{2,1,0:T(8,128)(2,1)S(1)} %pad_maximum_fusion.3.refs_0_), channel_id=1, source_target_pairs={{0,8},{1,9},{2,10},{3,11},{4,12},{5,13},{6,14},{7,15},{8,0},{9,1},... | collective-permute-start | bytes 1769480 | tf_op jit(solution)/shard_map/ppermute | solution.py:383
  67.6 37.9 %collective-permute-start.20 = (bf16[4,96,768]{2,1,0:T(8,128)(2,1)}, bf16[4,96,768]{2,1,0:T(8,128)(2,1)}, u32[]{:S(2)}, u32[]{:S(2)}) collective-permute-start(bf16[4,96,768]{2,1,0:T(8,128)(2,1)} %pad_maximum_fusion.4.refs_0_), channel_id=1, source_target_pairs={{0,1},{1,0},{2,3},{3,2},{4,5},{5,4},{6,7},{7,6},{8,9},{9,8},{10,11... | collective-permute-start | bytes 1769480 | tf_op jit(solution)/shard_map/ppermute | solution.py:383
  105.5 26.2 %collective-permute-start.22 = (bf16[4,96,768]{2,1,0:T(8,128)(2,1)}, bf16[4,96,768]{2,1,0:T(8,128)(2,1)S(1)}, u32[]{:S(2)}, u32[]{:S(2)}) collective-permute-start(bf16[4,96,768]{2,1,0:T(8,128)(2,1)} %collective-permute-done.20.refs_1_), channel_id=1, source_target_pairs={{0,16},{1,17},{2,18},{3,19},{4,20},{5,21},{6,22},{7,23},{8,24},{9,... | collective-permute-start | bytes 1769480 | tf_op jit(solution)/shard_map/ppermute | solution.py:383
  134.6 743.3 %reduce-scatter.2.cloned.1.call-start = ((), (), s32[]{:S(2)}) async-start(), calls=%async_computation.1 | async-start | bytes 14598144 | tf_op jit(solution)/shard_map/reduce_scatter | solution.py:767
  175.5 38.8 %collective-permute-start.27 = (f32[1,64,768]{2,1,0:T(8,128)S(1)}, f32[1,64,768]{2,1,0:T(8,128)S(1)}, u32[]{:S(2)}, u32[]{:S(2)}) collective-permute-start(f32[1,64,768]{2,1,0:T(8,128)S(1)} %bitcast.452), channel_id=1, source_target_pairs={{0,1},{1,0},{2,3},{3,2},{4,5},{5,4},{6,7},{7,6},{8,9},{9,8},{10,11... | collective-permute-start | bytes 589832 | tf_op jit(solution)/shard_map/ppermute | solution.py:383
  175.5 42.1 %collective-permute-start.28 = (f32[1,64,768]{2,1,0:T(8,128)S(1)}, f32[1,64,768]{2,1,0:T(8,128)S(1)}, u32[]{:S(2)}, u32[]{:S(2)}) collective-permute-start(f32[1,64,768]{2,1,0:T(8,128)S(1)} %bitcast.453), channel_id=1, source_target_pairs={{0,2},{1,3},{2,0},{3,1},{4,6},{5,7},{6,4},{7,5},{8,10},{9,11},{10,... | collective-permute-start | bytes 589832 | tf_op jit(solution)/shard_map/ppermute | solution.py:383
  175.5 44.7 %collective-permute-start.29 = (f32[1,64,768]{2,1,0:T(8,128)S(1)}, f32[1,64,768]{2,1,0:T(8,128)S(1)}, u32[]{:S(2)}, u32[]{:S(2)}) collective-permute-start(f32[1,64,768]{2,1,0:T(8,128)S(1)} %bitcast.454), channel_id=1, source_target_pairs={{0,3},{1,2},{2,1},{3,0},{4,7},{5,6},{6,5},{7,4},{8,11},{9,10},{10,... | collective-permute-start | bytes 589832 | tf_op jit(solution)/shard_map/ppermute | solution.py:383
  179.0 41.3 %collective-permute-start.30 = (f32[1,64,768]{2,1,0:T(8,128)S(1)}, f32[1,64,768]{2,1,0:T(8,128)}, u32[]{:S(2)}, u32[]{:S(2)}) collective-permute-start(f32[1,64,768]{2,1,0:T(8,128)S(1)} %bitcast.455), channel_id=1, source_target_pairs={{0,4},{1,5},{2,6},{3,7},{4,0},{5,1},{6,2},{7,3},{8,12},{9,13},{10,... | collective-permute-start | bytes 589832 | tf_op jit(solution)/shard_map/ppermute | solution.py:383
  179.3 41.0 %collective-permute-start.31 = (f32[1,64,768]{2,1,0:T(8,128)S(1)}, f32[1,64,768]{2,1,0:T(8,128)}, u32[]{:S(2)}, u32[]{:S(2)}) collective-permute-start(f32[1,64,768]{2,1,0:T(8,128)S(1)} %bitcast.456), channel_id=1, source_target_pairs={{0,5},{1,4},{2,7},{3,6},{4,1},{5,0},{6,3},{7,2},{8,13},{9,12},{10,... | collective-permute-start | bytes 589832 | tf_op jit(solution)/shard_map/ppermute | solution.py:383
  562.2 65.9 %collective-permute-start.34 = (bf16[64,768]{1,0:T(8,128)(2,1)}, bf16[64,768]{1,0:T(8,128)(2,1)}, u32[]{:S(2)}, u32[]{:S(2)}) collective-permute-start(bf16[64,768]{1,0:T(8,128)(2,1)} %get-tuple-element.245), channel_id=1, source_target_pairs={{0,1},{1,0},{2,3},{3,2},{4,5},{5,4},{6,7},{7,6},{8,9},{9,8},{10,11... | collective-permute-start | bytes 294920 | tf_op jit(solution)/shard_map/ppermute | solution.py:383
  562.6 67.6 %collective-permute-start.35 = (bf16[64,768]{1,0:T(8,128)(2,1)}, bf16[64,768]{1,0:T(8,128)(2,1)}, u32[]{:S(2)}, u32[]{:S(2)}) collective-permute-start(bf16[64,768]{1,0:T(8,128)(2,1)} %get-tuple-element.251), channel_id=1, source_target_pairs={{0,2},{1,3},{2,0},{3,1},{4,6},{5,7},{6,4},{7,5},{8,10},{9,11},{10,... | collective-permute-start | bytes 294920 | tf_op jit(solution)/shard_map/ppermute | solution.py:383
  572.4 63.7 %collective-permute-start.36 = (bf16[64,768]{1,0:T(8,128)(2,1)}, bf16[64,768]{1,0:T(8,128)(2,1)}, u32[]{:S(2)}, u32[]{:S(2)}) collective-permute-start(bf16[64,768]{1,0:T(8,128)(2,1)} %get-tuple-element.250), channel_id=1, source_target_pairs={{0,3},{1,2},{2,1},{3,0},{4,7},{5,6},{6,5},{7,4},{8,11},{9,10},{10,... | collective-permute-start | bytes 294920 | tf_op jit(solution)/shard_map/ppermute | solution.py:383
  572.8 63.2 %collective-permute-start.37 = (bf16[64,768]{1,0:T(8,128)(2,1)}, bf16[64,768]{1,0:T(8,128)(2,1)}, u32[]{:S(2)}, u32[]{:S(2)}) collective-permute-start(bf16[64,768]{1,0:T(8,128)(2,1)} %get-tuple-element.249), channel_id=1, source_target_pairs={{0,4},{1,5},{2,6},{3,7},{4,0},{5,1},{6,2},{7,3},{8,12},{9,13},{10,... | collective-permute-start | bytes 294920 | tf_op jit(solution)/shard_map/ppermute | solution.py:383
  574.9 61.1 %collective-permute-start.38 = (bf16[64,768]{1,0:T(8,128)(2,1)}, bf16[64,768]{1,0:T(8,128)(2,1)}, u32[]{:S(2)}, u32[]{:S(2)}) collective-permute-start(bf16[64,768]{1,0:T(8,128)(2,1)} %get-tuple-element.248), channel_id=1, source_target_pairs={{0,5},{1,4},{2,7},{3,6},{4,1},{5,0},{6,3},{7,2},{8,13},{9,12},{10,... | collective-permute-start | bytes 294920 | tf_op jit(solution)/shard_map/ppermute | solution.py:383
  679.1 38.1 %collective-permute-start.43 = (bf16[1,1,4,2,96,768]{5,4,3,2,1,0:T(8,128)(2,1)}, bf16[1,1,4,2,96,768]{5,4,3,2,1,0:T(8,128)(2,1)}, u32[]{:S(2)}, u32[]{:S(2)}) collective-permute-start(bf16[1,1,4,2,96,768]{5,4,3,2,1,0:T(8,128)(2,1)} %add_convert_fusion.5), channel_id=1, source_target_pairs={{0,16},{1,17},{2,18},{3,19},{4,20},{5,21},{6,22},{7,23},{8,24},{9,... | collective-permute-start | bytes 3538952 | tf_op jit(solution)/shard_map/ppermute | solution.py:383
  686.4 33.3 %collective-permute-start.44 = (bf16[2,1,4,1,24,3072]{5,4,3,2,1,0:T(8,128)(2,1)}, bf16[2,1,4,1,24,3072]{5,4,3,2,1,0:T(8,128)(2,1)}, u32[]{:S(2)}, u32[]{:S(2)}) collective-permute-start(bf16[2,1,4,1,24,3072]{5,4,3,2,1,0:T(8,128)(2,1)} %add_convert_fusion.4), channel_id=1, source_target_pairs={{0,1},{1,0},{2,3},{3,2},{4,5},{5,4},{6,7},{7,6},{8,9},{9,8},{10,11... | collective-permute-start | bytes 3538952 | tf_op jit(solution)/shard_map/ppermute | solution.py:383
  781.7 31.4 %collective-permute-start.66 = (bf16[2,1,4,2,40,768]{5,4,3,2,1,0:T(8,128)(2,1)S(1)}, bf16[2,1,4,2,40,768]{5,4,3,2,1,0:T(8,128)(2,1)S(1)}, u32[]{:S(2)}, u32[]{:S(2)}) collective-permute-start(bf16[2,1,4,2,40,768]{5,4,3,2,1,0:T(8,128)(2,1)S(1)} %constant_dynamic-slice_fusion), channel_id=1, source_target_pairs={{0,8},{1,9},{2,10},{3,11},{4,12},{5,13},{6,14},{7,15},{8,0},{9,1},... | collective-permute-start | bytes 2949128 | tf_op jit(solution)/shard_map/ppermute | solution.py:383
  (339 other events, 3752.6 us)
Sparse Core Ops, SparseCore 0:
  13.7 92.1 all-gather.6
  108.8 100.3 all-gather.8
  212.2 66.5 all-gather.10
  623.4 186.7 reduce-scatter.1
